TPU v7x, 32 devices: a whole 2x2x4 slice. The times are simulated.
32 devices in a mesh: dp: 2 (over core), blk: 4 (over z), uly: 4 (over y, x).
Axes of the slice: x: 2, y: 2, z: 4, core: 2. Of those that a mesh axis runs over, the one named last changes fastest.
Arguments:
- tokens: bfloat16 [4, 1024, 1536], P('dp', ('blk', 'uly')), may hold values from -6 to 6
- cotangent: bfloat16 [4, 1024, 1536], P('dp', ('blk', 'uly')), may hold values from -6 to 6
- lengths: int32 [4], P('dp'), may hold values from 256 to 1024, as said below
- owner_slot: int32 [2856], replicated, may hold values from 0 to 2879, as said below
- master: float32 [2880, 128, 128], P(('dp', 'blk', 'uly'))
- moment_first: float32 [2880, 128, 128], P(('dp', 'blk', 'uly'))
- moment_second: float32 [2880, 128, 128], P(('dp', 'blk', 'uly')), as said below
- basis_left: float32 [2880, 128, 128], P(('dp', 'blk', 'uly')), as said below
- basis_right: float32 [2880, 128, 128], P(('dp', 'blk', 'uly')), as said below
- small_master: float32 [5120], P(('dp', 'blk', 'uly'))
- small_first: float32 [5120], P(('dp', 'blk', 'uly')), may hold values from -181.01933 to 181.01933
- small_second: float32 [5120], P(('dp', 'blk', 'uly')), may hold values from 2048 to 8192
Outputs:
- mixed: bfloat16 [4, 1024, 1536], P('dp', ('blk', 'uly'))
- grad_tokens: float32 [4, 1024, 1536], P('dp', ('blk', 'uly'))
- moment_first_new: float32 [2880, 128, 128], P(('dp', 'blk', 'uly'))
- moment_second_new: float32 [2880, 128, 128], P(('dp', 'blk', 'uly'))
- master_new: float32 [2880, 128, 128], P(('dp', 'blk', 'uly'))
- small_first_new: float32 [5120], P(('dp', 'blk', 'uly'))
- small_second_new: float32 [5120], P(('dp', 'blk', 'uly'))
- small_new: float32 [5120], P(('dp', 'blk', 'uly'))
Inputs may be any that keep to these rules, and one draw needn't show every extreme that they name: `lengths`: at least 256 real tokens each, the rest padding; in every draw some sequence has all 1024. `owner_slot`: distinct slots; slot s is slot s % 90 of the device at position s // 90 in the order dp, blk, uly; the last slot is always used. `basis_left`: each slot's matrix is orthogonal. `basis_right`: each slot's matrix is orthogonal. `moment_second`: positive.
All inputs are finite; a program needn't handle non-finite values.
Results may differ from a plain program's by a relative error of at most 0.017.
Values may be sent and summed in bfloat16 or wider, within the bound.
No kernel may reach another device: no remote copies, remote signals or barrier semaphores. Data moves between devices by JAX's collectives and lax.ppermute only.
A program may use at most 704 MiB of HBM per device.

v0:
```python
import math

import jax
import jax.numpy as jnp
import numpy as np
from jax import lax
from jax.sharding import PartitionSpec as P

D = 1536
QH = 12
KVH = 2
HD = 128
FF = 8960
BLOCK = 128
QW = 1536
KVW = 256
N_TILES = 2856


NORM_EPS = 1e-06
ROPE_BASE = 1000000.0
BETA_FIRST = 0.5
BETA_SECOND = 0.5
ADAM_EPS = 1e-08
SCALE_EPS = 1e-06
RELATIVE_RATE = 0.5
SMALL_RATE = 0.25
WEIGHT_DECAY = 0.01
MASK_FILL = -1e30
TOP_PRECISION = lax.Precision.HIGHEST


def matrix_shapes():
    return [(D, QW), (D, KVW), (D, KVW), (QW, D), (D, FF), (D, FF), (FF, D)]


def split_small(vector):
    edges = [0, D, 2 * D, 2 * D + QW, 2 * D + QW + KVW, 2 * D + QW + 2 * KVW]
    return [vector[edges[number] : edges[number + 1]] for number in range(5)]


def arrange(slot_copies, small_copies, owner_slot):
    matrices = []
    offset = 0
    for row_count, col_count in matrix_shapes():
        tile_count = row_count // BLOCK * (col_count // BLOCK)
        picked = jnp.take(slot_copies, owner_slot[offset : offset + tile_count], axis=0)
        blocked = picked.reshape(row_count // BLOCK, col_count // BLOCK, BLOCK, BLOCK)
        matrices.append(blocked.transpose(0, 2, 1, 3).reshape(row_count, col_count))
        offset = offset + tile_count
    smalls = [member.astype(jnp.float32) for member in split_small(small_copies)]
    return (matrices, smalls)


def tile_tables():
    left_bases = [0, 0, 0, D // BLOCK, (D + QW) // BLOCK, (D + QW) // BLOCK, (2 * D + QW) // BLOCK]
    right_bases = [
        0,
        QW // BLOCK,
        (QW + KVW) // BLOCK,
        (QW + 2 * KVW) // BLOCK,
        (QW + 2 * KVW + D) // BLOCK,
        (QW + 2 * KVW + D + FF) // BLOCK,
        (QW + 2 * KVW + D + 2 * FF) // BLOCK,
    ]
    left_list = []
    right_list = []
    for number, shape_pair in enumerate(matrix_shapes()):
        grid_rows, grid_cols = np.meshgrid(
            np.arange(shape_pair[0] // BLOCK), np.arange(shape_pair[1] // BLOCK), indexing="ij"
        )
        left_list.append(left_bases[number] + grid_rows.reshape(-1))
        right_list.append(right_bases[number] + grid_cols.reshape(-1))
    return (np.concatenate(left_list).astype(np.int32), np.concatenate(right_list).astype(np.int32))


def rotate(values, positions, direction):
    half_size = HD // 2
    frequency = ROPE_BASE ** (-2.0 * jnp.arange(half_size, dtype=jnp.float32) / HD)
    angles = positions.astype(jnp.float32)[:, None] * frequency[None, :]
    cosine = jnp.cos(angles)[:, None, :]
    sine = direction * jnp.sin(angles)[:, None, :]
    first_half = values[..., :half_size]
    second_half = values[..., half_size:]
    return jnp.concatenate(
        [first_half * cosine - second_half * sine, second_half * cosine + first_half * sine],
        axis=-1,
    )


def forward_product(left_side, weight):
    return jnp.dot(left_side, weight, preferred_element_type=jnp.float32)


def back_product(grads, weight):
    return jnp.einsum("nf,df->nd", grads, weight, preferred_element_type=jnp.float32)


def outer_blocks(values):
    return values.reshape(values.shape[0], -1, BLOCK).transpose(1, 0, 2)


def norm_backward(values, inverse, gain, grad_normed):
    scaled = values * inverse
    gained = grad_normed * gain
    grad_values = inverse * (gained - scaled * jnp.mean(gained * scaled, axis=-1, keepdims=True))
    return (grad_values, jnp.sum(grad_normed * scaled, axis=0))


def local(
    tokens,
    cotangent,
    lengths,
    owner_slot,
    master,
    moment_first,
    moment_second,
    basis_left,
    basis_right,
    small_master,
    small_first,
    small_second,
):
    uly_count = lax.axis_size("uly")
    blk_count = lax.axis_size("blk")
    all_count = lax.axis_size("dp") * blk_count * uly_count
    uly_index = lax.axis_index("uly")
    blk_index = lax.axis_index("blk")
    seq_count = tokens.shape[0]
    rows_local = tokens.shape[1]
    token_count = seq_count * rows_local
    span_rows = rows_local * uly_count
    heads_local = QH // uly_count
    slot_local = master.shape[0]
    slot_total = slot_local * all_count
    score_root = math.sqrt(HD)
    positions = (blk_index * uly_count + uly_index) * rows_local + jnp.arange(
        rows_local, dtype=jnp.int32
    )
    query_pos = blk_index * span_rows + jnp.arange(span_rows, dtype=jnp.int32)
    key_head = uly_index * heads_local // (QH // KVH)
    head_pick = (jnp.arange(KVH, dtype=jnp.int32) == key_head).astype(jnp.float32)
    slot_copies, small_copies = (
        lax.all_gather(master.astype(jnp.bfloat16), ("dp", "blk", "uly"), axis=0, tiled=True),
        lax.all_gather(small_master.astype(jnp.bfloat16), ("dp", "blk", "uly"), axis=0, tiled=True),
    )
    matrices, smalls = arrange(slot_copies, small_copies, owner_slot)
    w_query, w_key, w_value, w_out, w_gate, w_up, w_down = matrices
    gain_first, gain_second, bias_query, bias_key, bias_value = smalls
    token_rows = tokens.reshape(token_count, D).astype(jnp.float32)
    inverse_first = lax.rsqrt(jnp.mean(token_rows * token_rows, axis=-1, keepdims=True) + NORM_EPS)
    normed = (token_rows * inverse_first * gain_first).astype(jnp.bfloat16)
    query_lin = forward_product(normed, w_query) + bias_query
    key_lin = forward_product(normed, w_key) + bias_key
    value_rows = (
        (forward_product(normed, w_value) + bias_value)
        .astype(jnp.bfloat16)
        .reshape(seq_count, rows_local, KVH, HD)
    )
    query_rot = rotate(query_lin.reshape(seq_count, rows_local, QH, HD), positions, 1.0).astype(
        jnp.bfloat16
    )
    key_rot = rotate(key_lin.reshape(seq_count, rows_local, KVH, HD), positions, 1.0).astype(
        jnp.bfloat16
    )
    query_heads = lax.all_to_all(query_rot, "uly", split_axis=2, concat_axis=1, tiled=True)
    key_span, value_span = (
        lax.all_gather(key_rot, "uly", axis=1, tiled=True),
        lax.all_gather(value_rows, "uly", axis=1, tiled=True),
    )

    def score_block(key_piece, first_row):
        key_sel = lax.dynamic_index_in_dim(key_piece, key_head, 2, keepdims=False)
        scores = (
            jnp.einsum("sqhd,skd->sqhk", query_heads, key_sel, preferred_element_type=jnp.float32)
            / score_root
        )
        key_pos = first_row + jnp.arange(key_piece.shape[1], dtype=jnp.int32)
        causal = key_pos[None, :] <= query_pos[:, None]
        inside = key_pos[None, :] < lengths[:, None]
        allowed = causal[None, :, None, :] & inside[:, None, None, :]
        return (scores, allowed)

    def forward_fold(carried, arrived, first_row):
        running_max, running_sum, accumulated = carried
        key_piece, value_piece = arrived
        scores, allowed = score_block(key_piece, first_row)
        new_max = jnp.maximum(running_max, jnp.max(jnp.where(allowed, scores, MASK_FILL), axis=-1))
        probs = jnp.where(allowed, jnp.exp(scores - new_max[..., None]), 0.0)
        factor = jnp.exp(running_max - new_max)
        value_sel = lax.dynamic_index_in_dim(value_piece, key_head, 2, keepdims=False).astype(
            jnp.float32
        )
        accumulated = accumulated * factor[..., None] + jnp.einsum(
            "sqhk,skd->sqhd", probs, value_sel, precision=TOP_PRECISION
        )
        return (new_max, running_sum * factor + jnp.sum(probs, axis=-1), accumulated)

    def fold_whole(step_fn, initial, whole_set):

        def one_step(step_index, carried):
            first_row = step_index * span_rows
            arrived = tuple(
                (lax.dynamic_slice_in_dim(member, first_row, span_rows, 1) for member in whole_set)
            )
            return step_fn(carried, arrived, first_row)

        return lax.fori_loop(0, blk_count, one_step, initial)

    stat_shape = (seq_count, span_rows, heads_local)
    forward_start = (
        jnp.full(stat_shape, MASK_FILL, jnp.float32),
        jnp.zeros(stat_shape, jnp.float32),
        jnp.zeros(stat_shape + (HD,), jnp.float32),
    )
    key_whole, value_whole = (
        lax.all_gather(key_span, "blk", axis=1, tiled=True),
        lax.all_gather(value_span, "blk", axis=1, tiled=True),
    )
    running_max, running_sum, accumulated = fold_whole(
        forward_fold, forward_start, (key_whole, value_whole)
    )
    attended = accumulated / running_sum[..., None]
    log_sum = running_max + jnp.log(running_sum)
    out_rows = lax.all_to_all(
        attended.astype(jnp.bfloat16), "uly", split_axis=1, concat_axis=2, tiled=True
    ).reshape(token_count, QW)
    middle = token_rows + forward_product(out_rows, w_out)
    inverse_second = lax.rsqrt(jnp.mean(middle * middle, axis=-1, keepdims=True) + NORM_EPS)
    normed_two = (middle * inverse_second * gain_second).astype(jnp.bfloat16)
    gate_lin = forward_product(normed_two, w_gate)
    upward = forward_product(normed_two, w_up)
    hidden = (jax.nn.silu(gate_lin) * upward).astype(jnp.bfloat16)
    mixed_out = (
        (middle + forward_product(hidden, w_down))
        .astype(jnp.bfloat16)
        .reshape(seq_count, rows_local, D)
    )
    valid_rows = (positions[None, :] < lengths[:, None]).astype(jnp.float32)
    seed_grad = (cotangent.astype(jnp.float32) * valid_rows[:, :, None]).reshape(token_count, D)
    seed_low = seed_grad.astype(jnp.bfloat16)
    grad_hidden = back_product(seed_low, w_down)
    gate_sigmoid = jax.nn.sigmoid(gate_lin)
    grad_gate = (
        grad_hidden * upward * gate_sigmoid * (1.0 + gate_lin * (1.0 - gate_sigmoid))
    ).astype(jnp.bfloat16)
    grad_up = (grad_hidden * gate_lin * gate_sigmoid).astype(jnp.bfloat16)
    grad_normed_two = back_product(grad_gate, w_gate) + back_product(grad_up, w_up)
    norm_part_two, gain_second_grad = norm_backward(
        middle, inverse_second, gain_second, grad_normed_two
    )
    grad_middle = seed_grad + norm_part_two
    grad_middle_low = grad_middle.astype(jnp.bfloat16)
    grad_out_rows = (
        back_product(grad_middle_low, w_out)
        .astype(jnp.bfloat16)
        .reshape(seq_count, rows_local, QH, HD)
    )
    grad_heads = lax.all_to_all(grad_out_rows, "uly", split_axis=2, concat_axis=1, tiled=True)
    grad_heads_wide = grad_heads.astype(jnp.float32)
    row_delta = jnp.sum(grad_heads_wide * attended, axis=-1)

    def backward_fold(carried, arrived, first_row):
        grad_query, grad_keys, grad_values = carried
        key_piece, value_piece = arrived
        scores, allowed = score_block(key_piece, first_row)
        probs = jnp.where(allowed, jnp.exp(scores - log_sum[..., None]), 0.0)
        value_sel = lax.dynamic_index_in_dim(value_piece, key_head, 2, keepdims=False)
        key_sel = lax.dynamic_index_in_dim(key_piece, key_head, 2, keepdims=False)
        grad_prob = jnp.einsum(
            "sqhd,skd->sqhk", grad_heads, value_sel, preferred_element_type=jnp.float32
        )
        grad_score = (probs * (grad_prob - row_delta[..., None])).astype(jnp.bfloat16)
        grad_query = grad_query + jnp.einsum(
            "sqhk,skd->sqhd", grad_score, key_sel, preferred_element_type=jnp.float32
        )
        key_part = jnp.einsum(
            "sqhk,sqhd->skd", grad_score, query_heads, preferred_element_type=jnp.float32
        )
        value_part = jnp.einsum("sqhk,sqhd->skd", probs, grad_heads_wide, precision=TOP_PRECISION)
        key_part = key_part[:, :, None, :] * head_pick[None, None, :, None]
        value_part = value_part[:, :, None, :] * head_pick[None, None, :, None]
        grad_keys = lax.dynamic_update_slice_in_dim(grad_keys, key_part, first_row, 1)
        grad_values = lax.dynamic_update_slice_in_dim(grad_values, value_part, first_row, 1)
        return (grad_query, grad_keys, grad_values)

    kv_shape = (seq_count, span_rows * blk_count, KVH, HD)
    backward_start = (
        jnp.zeros(stat_shape + (HD,), jnp.float32),
        jnp.zeros(kv_shape, jnp.float32),
        jnp.zeros(kv_shape, jnp.float32),
    )
    grad_query, grad_keys, grad_values = fold_whole(
        backward_fold, backward_start, (key_whole, value_whole)
    )
    grad_query_low = (grad_query / score_root).astype(jnp.bfloat16)
    grad_query_rows = lax.all_to_all(grad_query_low, "uly", split_axis=1, concat_axis=2, tiled=True)
    grad_keys_span, grad_values_span = (
        lax.psum_scatter(
            (grad_keys / score_root).astype(jnp.bfloat16), "blk", scatter_dimension=1, tiled=True
        ).astype(jnp.float32),
        lax.psum_scatter(
            grad_values.astype(jnp.bfloat16), "blk", scatter_dimension=1, tiled=True
        ).astype(jnp.float32),
    )
    grad_keys_rows, grad_values_rows = (
        lax.psum_scatter(grad_keys_span, "uly", scatter_dimension=1, tiled=True),
        lax.psum_scatter(grad_values_span, "uly", scatter_dimension=1, tiled=True),
    )
    grad_query_lin = (
        rotate(grad_query_rows.astype(jnp.float32), positions, -1.0)
        .astype(jnp.bfloat16)
        .reshape(token_count, QW)
    )
    key_rounded = lax.optimization_barrier(grad_keys_rows.astype(jnp.bfloat16)).astype(jnp.float32)
    grad_key_lin = (
        rotate(key_rounded, positions, -1.0).astype(jnp.bfloat16).reshape(token_count, KVW)
    )
    grad_value_lin = grad_values_rows.astype(jnp.bfloat16).reshape(token_count, KVW)
    grad_normed = (
        back_product(grad_query_lin, w_query)
        + back_product(grad_key_lin, w_key)
        + back_product(grad_value_lin, w_value)
    )
    norm_part_first, gain_first_grad = norm_backward(
        token_rows, inverse_first, gain_first, grad_normed
    )
    grad_tokens = (grad_middle + norm_part_first).reshape(seq_count, rows_local, D)
    small_partial = jnp.concatenate(
        [
            gain_first_grad,
            gain_second_grad,
            jnp.sum(grad_query_lin, axis=0, dtype=jnp.float32),
            jnp.sum(grad_key_lin, axis=0, dtype=jnp.float32),
            jnp.sum(grad_value_lin, axis=0, dtype=jnp.float32),
        ]
    )
    grad_small = lax.psum_scatter(
        small_partial, ("dp", "blk", "uly"), scatter_dimension=0, tiled=True
    )
    left_table = jnp.concatenate(
        [
            outer_blocks(normed),
            outer_blocks(out_rows),
            outer_blocks(normed_two),
            outer_blocks(hidden),
        ],
        axis=0,
    )
    right_table = jnp.concatenate(
        [
            outer_blocks(grad_query_lin),
            outer_blocks(grad_key_lin),
            outer_blocks(grad_value_lin),
            outer_blocks(grad_middle_low),
            outer_blocks(grad_gate),
            outer_blocks(grad_up),
            outer_blocks(seed_low),
        ],
        axis=0,
    )
    left_ids, right_ids = tile_tables()
    tile_of_slot = (
        jnp.zeros((slot_total,), jnp.int32).at[owner_slot].set(jnp.arange(N_TILES, dtype=jnp.int32))
    )
    slot_used = jnp.zeros((slot_total,), jnp.float32).at[owner_slot].set(1.0)
    slot_left = jnp.take(jnp.asarray(left_ids), tile_of_slot)
    slot_right = jnp.take(jnp.asarray(right_ids), tile_of_slot)
    row_ids = jnp.arange(lax.axis_size(("dp", "blk", "uly")) * slot_local, dtype=jnp.int32)
    global_ids = row_ids // slot_local * slot_local + row_ids % slot_local
    left_part = jnp.take(left_table, jnp.take(slot_left, global_ids), axis=0)
    right_part = jnp.take(right_table, jnp.take(slot_right, global_ids), axis=0)
    used_mask = jnp.take(slot_used, global_ids)
    grad_slots = lax.psum_scatter(
        jnp.einsum("snb,snc->sbc", left_part, right_part, preferred_element_type=jnp.float32)
        * used_mask[:, None, None],
        ("dp", "blk", "uly"),
        scatter_dimension=0,
        tiled=True,
    )
    rotated = jnp.einsum("sji,sjk->sik", basis_left, grad_slots, precision=TOP_PRECISION)
    rotated = jnp.einsum("sik,skl->sil", rotated, basis_right, precision=TOP_PRECISION)
    first_new = BETA_FIRST * moment_first + (1.0 - BETA_FIRST) * rotated
    second_new = BETA_SECOND * moment_second + (1.0 - BETA_SECOND) * rotated * rotated
    normalized = first_new / (jnp.sqrt(second_new) + ADAM_EPS)
    update = jnp.einsum("sik,skl->sil", basis_left, normalized, precision=TOP_PRECISION)
    update = jnp.einsum("sik,slk->sil", update, basis_right, precision=TOP_PRECISION)
    tile_scale = jnp.sqrt(jnp.mean(master * master, axis=(1, 2), keepdims=True) + SCALE_EPS)
    master_new = master - RELATIVE_RATE * tile_scale * (update + WEIGHT_DECAY * master)
    small_first_new = BETA_FIRST * small_first + (1.0 - BETA_FIRST) * grad_small
    small_second_new = BETA_SECOND * small_second + (1.0 - BETA_SECOND) * grad_small * grad_small
    small_new = small_master - SMALL_RATE * (
        small_first_new / (jnp.sqrt(small_second_new) + ADAM_EPS) + WEIGHT_DECAY * small_master
    )
    return (
        mixed_out,
        grad_tokens,
        first_new,
        second_new,
        master_new,
        small_first_new,
        small_second_new,
        small_new,
    )


def solution(mesh):
    in_specs = (
        P("dp", ("blk", "uly"), None),
        P("dp", ("blk", "uly"), None),
        P("dp"),
        P(),
        P(("dp", "blk", "uly"), None, None),
        P(("dp", "blk", "uly"), None, None),
        P(("dp", "blk", "uly"), None, None),
        P(("dp", "blk", "uly"), None, None),
        P(("dp", "blk", "uly"), None, None),
        P(("dp", "blk", "uly")),
        P(("dp", "blk", "uly")),
        P(("dp", "blk", "uly")),
    )
    out_specs = (
        P("dp", ("blk", "uly"), None),
        P("dp", ("blk", "uly"), None),
        P(("dp", "blk", "uly"), None, None),
        P(("dp", "blk", "uly"), None, None),
        P(("dp", "blk", "uly"), None, None),
        P(("dp", "blk", "uly")),
        P(("dp", "blk", "uly")),
        P(("dp", "blk", "uly")),
    )
    return jax.shard_map(local, mesh=mesh, in_specs=in_specs, out_specs=out_specs, check_vma=False)
```

profile of v0, /device:TPU:10, one launch (start us, length us, event | category | flops | bytes accessed | tf_op | source)
XLA Modules:
  0.0 2987.7 jit_solution(958736964098146163)
XLA Ops:
  16.5 47.2 %all-reduce = bf16[5120]{0:T(1024)(128)(2,1)S(1)} all-reduce(bf16[5120]{0:T(1024)(128)(2,1)S(1)} %dynamic-update-slice), channel_id=1, replica_groups=mesh['dp'=2,'blk'=4,'uly'=4] {'dp','blk','uly'}, use_global_device_ids=true, to_apply=%add | all-reduce | flops 5120 | bytes 20480
  67.5 434.3 %all-gather.4.cloned.1.call-done = bf16[2880,128,128]{2,1,0:T(8,128)(2,1)} async-done(((bf16[90,128,128]{2,1,0:T(8,128)(2,1)}), bf16[2880,128,128]{2,1,0:T(8,128)(2,1)}) %all-gather.4.cloned.1.call-update) | async-done | bytes 94371856 | tf_op jit(solution)/shard_map/all_gather | solution.py:144
  547.4 23.3 gather_fusion.9
  570.7 18.3 broadcast_select_fusion
  589.1 36.1 %copy.222 = bf16[70,12,128,128]{2,0,3,1:T(8,128)(2,1)} copy(bf16[70,12,128,128]{3,2,1,0:T(8,128)(2,1)} %bitcast.329) | data formatting | bytes 55050240 | tf_op jit(solution)/shard_map/reshape | solution.py:48
  635.2 23.3 gather_fusion.7
  658.4 18.3 broadcast_select_fusion.2
  676.8 23.3 gather_fusion.8
  700.0 18.3 broadcast_select_fusion.1
  718.4 15.9 fusion.42
  777.6 19.5 copy.220
  797.0 19.2 copy.221
  837.9 23.9 multiply_convert_fusion.1
  861.8 15.9 fusion.46
  877.7 17.1 multiply_reduce_fusion.1
  919.3 27.7 while.43
  1046.4 15.5 gather_fusion.2
  1105.5 63.4 %gather_fusion = bf16[2880,128,128]{2,1,0:T(8,128)(2,1)} fusion(bf16[106,128,128]{2,1,0:T(8,128)(2,1)S(1)} %pad_maximum_fusion, s32[3072]{0:T(1024)S(1)} %pad_clamp_fusion.2), kind=kCustom, calls=%fused_computation.11 | custom fusion | bytes 188755200 | tf_op jit(solution)/shard_map/jit(_take)/gather | solution.py:371
  1177.8 21.0 reduce-scatter.22.cloned.1.call-done
  1206.3 66.6 %gather_fusion.1 = bf16[2880,128,128]{2,1,0:T(8,128)(2,1)} fusion(bf16[180,128,128]{2,1,0:T(8,128)(2,1)} %bitcast_dynamic-update-slice_fusion.2, s32[3072]{0:T(1024)S(1)} %copy-done.47), kind=kCustom, calls=%fused_computation.12 | custom fusion | bytes 188755200 | tf_op jit(solution)/shard_map/jit(_take)/gather | solution.py:372
  1272.9 136.2 %broadcast_multiply_fusion = f32[2880,128,128]{2,1,0:T(8,128)} fusion(f32[2880]{0:T(1024)S(1)} %broadcast_select_fusion.9, bf16[2880,128,128]{2,1,0:T(8,128)(2,1)} %gather_fusion.1, pred[2880]{0:T(1024)(128)(4,1)S(1)} %get-tuple-element.1094, bf16[2880,128,128]{2,1,0:T(8,128)(2,1)} %gather_fusion, pred[2880]{0:T(1024)(128)(4,1)S(1)} %copy-done.40), kind=kOutput, calls=%fused_computation.70 | convolution fusion | flops 12221153280 | bytes 377504640 | tf_op jit(solution)/shard_map/snb,snc->sbc/dot_general | solution.py:375
  1410.2 18.4 fusion.90
  1436.8 40.3 %all-reduce.2 = f32[5120]{0:T(1024)S(1)} all-reduce(f32[5120]{0:T(1024)S(1)} %constant_dynamic-update-slice_fusion.2), channel_id=7, replica_groups=mesh['dp'=2,'blk'=4,'uly'=4] {'dp','blk','uly'}, use_global_device_ids=true, to_apply=%region_24.30.clone | all-reduce | flops 5120 | bytes 40960
  1479.0 1447.1 %reduce-scatter.28.cloned.1.call-done = f32[90,128,128]{2,1,0:T(8,128)} async-done(((f32[2880,128,128]{2,1,0:T(8,128)}), f32[90,128,128]{2,1,0:T(8,128)}) %reduce-scatter.28.cloned.1.call-update) | async-done | bytes 5898256
  (426 shorter events, 423.9 us)
Async XLA Ops:
  7.2 56.5 %copy-start.41 = (s32[2856]{0:T(1024)S(1)}, s32[2856]{0:T(1024)}, u32[]{:S(2)}) copy-start(s32[2856]{0:T(1024)} %param.31) | copy-start | bytes 34276
  7.2 56.9 %copy-start.46 = (s32[2]{0:T(128)S(1)}, s32[2]{0:T(128)}, u32[]{:S(2)}) copy-start(s32[2]{0:T(128)} %param.30) | copy-start | bytes 28
  7.2 59.3 %copy-start.38 = (bf16[2,64,1536]{2,1,0:T(8,128)(2,1)S(1)}, bf16[2,64,1536]{2,1,0:T(8,128)(2,1)}, u32[]{:S(2)}) copy-start(bf16[2,64,1536]{2,1,0:T(8,128)(2,1)} %param.29) | copy-start | bytes 1179652
  7.2 494.6 %all-gather.4.cloned.1.call-start = ((), (), s32[]{:S(2)}) async-start(), calls=%async_computation.9 | async-start | bytes 97320960 | tf_op jit(solution)/shard_map/all_gather | solution.py:144
  15.1 730.5 %all-gather.6.cloned.1.call-start = ((), (), s32[]{:S(2)}) async-start(), calls=%async_computation.10 | async-start | bytes 1310720 | tf_op jit(solution)/shard_map/all_gather | solution.py:217
  64.1 443.1 %copy-start.52 = (f32[2,64]{1,0:T(2,128)}, f32[2,64]{1,0:T(2,128)S(1)}, u32[]{:S(2)}) copy-start(f32[2,64]{1,0:T(2,128)S(1)} %add_rsqrt_fusion) | copy-start | bytes 1540
  65.5 441.7 %copy-start.43 = (f32[1536]{0:T(1024)}, f32[1536]{0:T(1024)S(1)}, u32[]{:S(2)}) copy-start(f32[1536]{0:T(1024)S(1)} %get-tuple-element.1073) | copy-start | bytes 18436
  66.3 474.6 %copy-start.30 = (f32[64,64]{1,0:T(8,128)}, f32[64,64]{1,0:T(8,128)S(1)}, u32[]{:S(2)}) copy-start(f32[64,64]{1,0:T(8,128)S(1)} %get-tuple-element.1079) | copy-start | bytes 49156
  67.5 650.9 %copy-start.25 = (bf16[2,64,1536]{2,1,0:T(8,128)(2,1)}, bf16[2,64,1536]{2,1,0:T(8,128)(2,1)S(1)}, u32[]{:S(2)}) copy-start(bf16[2,64,1536]{2,1,0:T(8,128)(2,1)S(1)} %get-tuple-element.1054) | copy-start | bytes 1179652
  542.6 203.0 %all-to-all-start = ((bf16[2,64,12,128]{3,1,0,2:T(8,128)(2,1)}), bf16[2,64,12,128]{3,1,0,2:T(8,128)(2,1)S(1)}, u32[]{:S(2)}, u32[]{:S(2)}) async-start(bf16[2,64,12,128]{3,1,0,2:T(8,128)(2,1)} %copy.210), calls=%async_computation | async-start | bytes 786432 | tf_op jit(solution)/shard_map/all_to_all | solution.py:166
  547.4 199.6 %all-gather.8.cloned.1.call-start = ((), (), s32[]{:S(2)}) async-start(), calls=%async_computation.11 | async-start | bytes 1310720 | tf_op jit(solution)/shard_map/all_gather | solution.py:218
  763.9 52.2 %all-to-all-start.1 = ((bf16[2,256,3,128]{3,0,2,1:T(2,128)(2,1)}), bf16[2,256,3,128]{3,0,2,1:T(2,128)(2,1)S(1)}, u32[]{:S(2)}, u32[]{:S(2)}) async-start(bf16[2,256,3,128]{3,0,2,1:T(2,128)(2,1)} %copy.216), calls=%async_computation.1 | async-start | bytes 786432 | tf_op jit(solution)/shard_map/all_to_all | solution.py:225
  821.8 73.0 %copy-start.22 = (f32[128,1536]{1,0:T(8,128)}, f32[128,1536]{1,0:T(8,128)S(1)}, u32[]{:S(2)}) copy-start(f32[128,1536]{1,0:T(8,128)S(1)} %get-tuple-element.1081) | copy-start | bytes 2359300
  905.6 9.5 all-to-all-start.2
  909.8 153.3 %reduce-scatter.24.cloned.1.call-start = ((), (), s32[]{:S(2)}) async-start(), calls=%async_computation.14 | async-start | bytes 1310720
  950.3 219.7 %reduce-scatter.20.cloned.1.call-start = ((), (), s32[]{:S(2)}) async-start(), calls=%async_computation.12 | async-start | bytes 1310720
  969.1 207.0 %reduce-scatter.26.cloned.1.call-start = ((), (), s32[]{:S(2)}) async-start(), calls=%async_computation.15 | async-start | bytes 655360
  969.2 92.8 %copy-start.50 = (f32[128]{0:T(128)}, f32[128]{0:T(128)S(1)}, u32[]{:S(2)}) copy-start(f32[128]{0:T(128)S(1)} %rsqrt.22) | copy-start | bytes 1540
  1098.7 70.2 %all-to-all-start.3 = ((bf16[2,256,3,128]{3,0,2,1:T(2,128)(2,1)}), bf16[2,256,3,128]{3,0,2,1:T(2,128)(2,1)}, u32[]{:S(2)}, u32[]{:S(2)}) async-start(bf16[2,256,3,128]{3,0,2,1:T(2,128)(2,1)} %copy.227), calls=%async_computation.3 | async-start | bytes 786432 | tf_op jit(solution)/shard_map/all_to_all | solution.py:297
  1103.4 95.4 %reduce-scatter.22.cloned.1.call-start = ((), (), s32[]{:S(2)}) async-start(), calls=%async_computation.13 | async-start | bytes 655360
  1172.5 1753.6 %reduce-scatter.28.cloned.1.call-start = ((), (), s32[]{:S(2)}) async-start(), calls=%async_computation.16 | async-start | bytes 194641920
  1200.1 72.8 %copy-start.32 = (bf16[2,64,2,64]{3,2,1,0:T(2,128)(2,1)}, bf16[2,64,2,64]{3,2,1,0:T(2,128)(2,1)S(1)}, u32[]{:S(2)}) copy-start(bf16[2,64,2,64]{3,2,1,0:T(2,128)(2,1)S(1)} %get-tuple-element.1055) | copy-start | bytes 98308
  1200.1 72.8 %copy-start.34 = (bf16[2,64,2,64]{3,2,1,0:T(2,128)(2,1)}, bf16[2,64,2,64]{3,2,1,0:T(2,128)(2,1)S(1)}, u32[]{:S(2)}) copy-start(bf16[2,64,2,64]{3,2,1,0:T(2,128)(2,1)S(1)} %get-tuple-element.1056) | copy-start | bytes 98308
  1206.3 66.6 %copy-start.40 = (pred[2880]{0:T(1024)(128)(4,1)S(1)}, pred[2880]{0:T(1024)(128)(4,1)}, u32[]{:S(2)}) copy-start(pred[2880]{0:T(1024)(128)(4,1)} %get-tuple-element.1095) | copy-start | bytes 8644
  (59 other events, 878.5 us)
Sparse Core Ops, SparseCore 0:
  15.3 486.5 all-gather.3
  517.5 28.8 all-gather.5
  635.3 28.3 all-gather.7
  950.5 25.3 reduce-scatter.23
  978.0 25.7 reduce-scatter.19
  1065.6 25.2 reduce-scatter.25
  1172.6 26.1 reduce-scatter.21
  1409.2 1516.8 reduce-scatter.27
where the time goes:
time: 3000 us; the launch traced here: 2990 us
  waiting for transfers between devices  1910 us (64%)
  local copies, waits for them, and re-layouts  492 us (16%)
  matrix products  344 us (11%)
  blocking collectives  106 us (4%)
  other arithmetic  104 us (3%)
    unnamed x13, waiting for transfers between devices  1470 us
    all_gather x1, waiting for transfers between devices, local(): lax.all_gather(master.astype(jnp.bfloat16), ('dp', 'blk', 'uly'), axis=0,...  434 us
    dot_general x1, matrix products, local(): jnp.einsum('snb,snc->sbc', left_part, right_part, preferred_element_type=...  136 us
    gather x7, local copies, waits for them, and re-layouts, arrange(): jnp.take(slot_copies, owner_slot[offset:offset + tile_count], axis=0)  96 us
    unnamed x2, blocking collectives  87.5 us
    reshape x7, local copies, waits for them, and re-layouts, arrange(): picked.reshape(row_count // BLOCK, col_count // BLOCK, BLOCK, BLOCK)  86.4 us
    gather x2, local copies, waits for them, and re-layouts, local(): right_part = jnp.take(right_table, jnp.take(slot_right, global_ids), axis=0)  82 us
    gather x2, local copies, waits for them, and re-layouts, local(): left_part = jnp.take(left_table, jnp.take(slot_left, global_ids), axis=0)  78.8 us
  transfers between devices with their start and end apart: 12, of which 4 were waited for; matrix products, arithmetic and copies ran while one was open for 17% of the time, Pallas kernels for 0%

commit v1 on v0

--- a/solution.py
+++ b/solution.py
@@ -27,7 +27,7 @@
 SMALL_RATE = 0.25
 WEIGHT_DECAY = 0.01
 MASK_FILL = -1e30
-TOP_PRECISION = lax.Precision.HIGHEST
+TOP_PRECISION = lax.Precision.DEFAULT
 
 
 def matrix_shapes():
@@ -372,12 +372,14 @@
     right_part = jnp.take(right_table, jnp.take(slot_right, global_ids), axis=0)
     used_mask = jnp.take(slot_used, global_ids)
     grad_slots = lax.psum_scatter(
-        jnp.einsum("snb,snc->sbc", left_part, right_part, preferred_element_type=jnp.float32)
-        * used_mask[:, None, None],
+        (
+            jnp.einsum("snb,snc->sbc", left_part, right_part, preferred_element_type=jnp.float32)
+            * used_mask[:, None, None]
+        ).astype(jnp.bfloat16),
         ("dp", "blk", "uly"),
         scatter_dimension=0,
         tiled=True,
-    )
+    ).astype(jnp.float32)
     rotated = jnp.einsum("sji,sjk->sik", basis_left, grad_slots, precision=TOP_PRECISION)
     rotated = jnp.einsum("sik,skl->sil", rotated, basis_right, precision=TOP_PRECISION)
     first_new = BETA_FIRST * moment_first + (1.0 - BETA_FIRST) * rotated

time: 3000 us -> 2200 us (0.73)
  waiting for transfers between devices: 1910 us -> 1170 us
  matrix products: 344 us -> 286 us
    unnamed x13, waiting for transfers between devices: 1470 us -> 728 us
  transfers between devices with their start and end apart: 12 -> 12, of which waited for: 4 -> 4; matrix products, arithmetic and copies ran while one was open for 17% -> 23% of each run, Pallas kernels for 0% -> 0%
where the time goes in v1:
time: 2200 us; the launch traced here: 2190 us
  waiting for transfers between devices  1170 us (53%)
  local copies, waits for them, and re-layouts  492 us (22%)
  matrix products  286 us (13%)
  blocking collectives  106 us (5%)
  other arithmetic  104 us (5%)
    unnamed x13, waiting for transfers between devices  728 us
    all_gather x1, waiting for transfers between devices, local(): lax.all_gather(master.astype(jnp.bfloat16), ('dp', 'blk', 'uly'), axis=0,...  434 us
    dot_general x1, matrix products, local(): jnp.einsum('snb,snc->sbc', left_part, right_part, preferred_element_type=...  107 us
    gather x7, local copies, waits for them, and re-layouts, arrange(): jnp.take(slot_copies, owner_slot[offset:offset + tile_count], axis=0)  95.8 us
    unnamed x2, blocking collectives  87.5 us
    reshape x7, local copies, waits for them, and re-layouts, arrange(): picked.reshape(row_count // BLOCK, col_count // BLOCK, BLOCK, BLOCK)  85.4 us
    gather x2, local copies, waits for them, and re-layouts, local(): right_part = jnp.take(right_table, jnp.take(slot_right, global_ids), axis=0)  82 us
    gather x2, local copies, waits for them, and re-layouts, local(): left_part = jnp.take(left_table, jnp.take(slot_left, global_ids), axis=0)  78.7 us
  transfers between devices with their start and end apart: 12, of which 4 were waited for; matrix products, arithmetic and copies ran while one was open for 23% of the time, Pallas kernels for 0%

profile of v1, /device:TPU:10, one launch (start us, length us, event | category | flops | bytes accessed | tf_op | source)
XLA Modules:
  0.0 2188.1 jit_solution(16429187559119946070)
XLA Ops:
  16.5 47.2 %all-reduce = bf16[5120]{0:T(1024)(128)(2,1)S(1)} all-reduce(bf16[5120]{0:T(1024)(128)(2,1)S(1)} %dynamic-update-slice), channel_id=1, replica_groups=mesh['dp'=2,'blk'=4,'uly'=4] {'dp','blk','uly'}, use_global_device_ids=true, to_apply=%add | all-reduce | flops 5120 | bytes 20480
  68.2 433.6 %all-gather.4.cloned.1.call-done = bf16[2880,128,128]{2,1,0:T(8,128)(2,1)} async-done(((bf16[90,128,128]{2,1,0:T(8,128)(2,1)}), bf16[2880,128,128]{2,1,0:T(8,128)(2,1)}) %all-gather.4.cloned.1.call-update) | async-done | bytes 94371856 | tf_op jit(solution)/shard_map/all_gather | solution.py:144
  546.3 23.3 %gather_fusion.9 = bf16[840,128,128]{2,1,0:T(8,128)(2,1)} fusion(bf16[2880,128,128]{2,1,0:T(8,128)(2,1)} %all-gather.4.cloned.1.call-done, s32[1024]{0:T(1024)S(1)} %get-tuple-element.1088), kind=kCustom, calls=%fused_computation.8.clone | custom fusion | bytes 55053600 | tf_op jit(solution)/shard_map/jit(_take)/gather | solution.py:47
  569.6 18.3 broadcast_select_fusion
  588.0 35.1 %copy.222 = bf16[70,12,128,128]{2,0,3,1:T(8,128)(2,1)} copy(bf16[70,12,128,128]{3,2,1,0:T(8,128)(2,1)} %bitcast.328) | data formatting | bytes 55050240 | tf_op jit(solution)/shard_map/reshape | solution.py:48
  633.0 23.2 %gather_fusion.7 = bf16[840,128,128]{2,1,0:T(8,128)(2,1)} fusion(bf16[2880,128,128]{2,1,0:T(8,128)(2,1)} %all-gather.4.cloned.1.call-done, s32[1024]{0:T(1024)S(1)} %get-tuple-element.1090), kind=kCustom, calls=%fused_computation.2.clone | custom fusion | bytes 55053600 | tf_op jit(solution)/shard_map/jit(_take)/gather | solution.py:47
  656.3 18.3 broadcast_select_fusion.2
  674.6 23.2 %gather_fusion.8 = bf16[840,128,128]{2,1,0:T(8,128)(2,1)} fusion(bf16[2880,128,128]{2,1,0:T(8,128)(2,1)} %all-gather.4.cloned.1.call-done, s32[1024]{0:T(1024)S(1)} %get-tuple-element.1089), kind=kCustom, calls=%fused_computation.7.clone | custom fusion | bytes 55053600 | tf_op jit(solution)/shard_map/jit(_take)/gather | solution.py:47
  697.8 18.3 broadcast_select_fusion.1
  771.5 19.4 copy.220
  790.9 19.2 copy.221
  817.8 16.0 fusion.48
  833.8 23.9 %multiply_convert_fusion.2 = (bf16[128,8960]{1,0:T(8,128)(2,1)}, bf16[128,8960]{1,0:T(8,128)(2,1)}, bf16[128,8960]{1,0:T(8,128)(2,1)}) fusion(f32[128,8960]{1,0:T(8,128)} %fusion.42, f32[128,8960]{1,0:T(8,128)} %fusion.48, bf16[128,1536]{1,0:T(8,128)(2,1)S(1)} %multiply_convert_fusion.6, bf16[192,8,70,128]{3,2,1,0:T(8,128)(2,1)} %bitcast.334), kind=kOutput, calls=%fused_computation.118 | convolution fusion | flops 3541565440 | bytes 43974656 | tf_op jit(solution)/shard_map/dot_general | solution.py:92
  873.7 17.1 multiply_reduce_fusion.1
  915.2 22.8 %while.43 = (s32[]{:T(128)}, f32[2,256,3,128]{3,1,2,0:T(8,128)S(1)}, f32[2,1024,2,128]{3,2,1,0:T(2,128)}, bf16[2,1024,2,128]{3,2,1,0:T(2,128)(2,1)}, s32[2]{0:T(...) while((s32[]{:T(128)}, ...), condition=%wide.region_9.13_spmd.clone, body=%wide.region_8.12_spmd.clone.sunk | while | flops 506528768 | bytes 21517680 | solution.py:208
  1096.3 63.4 %gather_fusion = bf16[2880,128,128]{2,1,0:T(8,128)(2,1)} fusion(bf16[106,128,128]{2,1,0:T(8,128)(2,1)S(1)} %pad_maximum_fusion, s32[3072]{0:T(1024)S(1)} %pad_clamp_fusion.2), kind=kCustom, calls=%fused_computation.11 | custom fusion | bytes 188755200 | tf_op jit(solution)/shard_map/jit(_take)/gather | solution.py:371
  1169.1 20.5 reduce-scatter.22.cloned.1.call-done
  1197.6 66.7 %gather_fusion.1 = bf16[2880,128,128]{2,1,0:T(8,128)(2,1)} fusion(bf16[180,128,128]{2,1,0:T(8,128)(2,1)} %bitcast_dynamic-update-slice_fusion.2, s32[3072]{0:T(1024)S(1)} %copy-done.51), kind=kCustom, calls=%fused_computation.12 | custom fusion | bytes 188755200 | tf_op jit(solution)/shard_map/jit(_take)/gather | solution.py:372
  1264.3 106.6 %multiply_convert_fusion = bf16[2880,128,128]{2,1,0:T(8,128)(2,1)} fusion(f32[2880]{0:T(1024)S(1)} %copy-done.53, bf16[2880,128,128]{2,1,0:T(8,128)(2,1)} %gather_fusion.1, pred[2880]{0:T(1024)(128)(4,1)S(1)} %get-tuple-element.1094, bf16[2880,128,128]{2,1,0:T(8,128)(2,1)} %gather_fusion, pred[2880]{0:T(1024)(128)(4,1)S(1)} %copy-done.60), kind=kOutput, calls=%fused_computation.70 | convolution fusion | flops 12268339200 | bytes 283132800 | tf_op jit(solution)/shard_map/snb,snc->sbc/dot_general | solution.py:376
  1372.0 18.5 fusion.93
  1398.9 40.3 %all-reduce.2 = f32[5120]{0:T(1024)S(1)} all-reduce(f32[5120]{0:T(1024)S(1)} %constant_dynamic-update-slice_fusion.2), channel_id=7, replica_groups=mesh['dp'=2,'blk'=4,'uly'=4] {'dp','blk','uly'}, use_global_device_ids=true, to_apply=%region_24.30.clone | all-reduce | flops 5120 | bytes 40960
  1441.0 707.3 %reduce-scatter.28.cloned.1.call-done = bf16[90,128,128]{2,1,0:T(8,128)(2,1)} async-done(((bf16[2880,128,128]{2,1,0:T(8,128)(2,1)}), bf16[90,128,128]{2,1,0:T(8,128)(2,1)}) %reduce-scatter.28.cloned.1.call-update) | async-done | bytes 2949136
  2148.3 16.0 fusion.60
  2164.3 16.8 multiply_subtract_fusion
  (425 shorter events, 391.1 us)
Async XLA Ops:
  7.2 56.5 %copy-start.45 = (s32[2856]{0:T(1024)S(1)}, s32[2856]{0:T(1024)}, u32[]{:S(2)}) copy-start(s32[2856]{0:T(1024)} %param.31) | copy-start | bytes 34276
  7.2 56.9 %copy-start.50 = (s32[2]{0:T(128)S(1)}, s32[2]{0:T(128)}, u32[]{:S(2)}) copy-start(s32[2]{0:T(128)} %param.30) | copy-start | bytes 28
  7.2 60.0 %copy-start.43 = (bf16[2,64,1536]{2,1,0:T(8,128)(2,1)S(1)}, bf16[2,64,1536]{2,1,0:T(8,128)(2,1)}, u32[]{:S(2)}) copy-start(bf16[2,64,1536]{2,1,0:T(8,128)(2,1)} %param.29) | copy-start | bytes 1179652
  7.2 494.6 %all-gather.4.cloned.1.call-start = ((), (), s32[]{:S(2)}) async-start(), calls=%async_computation.9 | async-start | bytes 97320960 | tf_op jit(solution)/shard_map/all_gather | solution.py:144
  15.1 728.3 %all-gather.6.cloned.1.call-start = ((), (), s32[]{:S(2)}) async-start(), calls=%async_computation.10 | async-start | bytes 1310720 | tf_op jit(solution)/shard_map/all_gather | solution.py:217
  64.1 443.1 %copy-start.57 = (f32[2,64]{1,0:T(2,128)}, f32[2,64]{1,0:T(2,128)S(1)}, u32[]{:S(2)}) copy-start(f32[2,64]{1,0:T(2,128)S(1)} %add_rsqrt_fusion) | copy-start | bytes 1540
  65.5 441.7 %copy-start.47 = (f32[1536]{0:T(1024)}, f32[1536]{0:T(1024)S(1)}, u32[]{:S(2)}) copy-start(f32[1536]{0:T(1024)S(1)} %get-tuple-element.1073) | copy-start | bytes 18436
  66.3 473.6 %copy-start.33 = (f32[64,64]{1,0:T(8,128)}, f32[64,64]{1,0:T(8,128)S(1)}, u32[]{:S(2)}) copy-start(f32[64,64]{1,0:T(8,128)S(1)} %get-tuple-element.1079) | copy-start | bytes 49156
  68.2 647.9 %copy-start.26 = (bf16[2,64,1536]{2,1,0:T(8,128)(2,1)}, bf16[2,64,1536]{2,1,0:T(8,128)(2,1)S(1)}, u32[]{:S(2)}) copy-start(bf16[2,64,1536]{2,1,0:T(8,128)(2,1)S(1)} %get-tuple-element.1054) | copy-start | bytes 1179652
  541.5 201.9 %all-to-all-start = ((bf16[2,64,12,128]{3,1,0,2:T(8,128)(2,1)}), bf16[2,64,12,128]{3,1,0,2:T(8,128)(2,1)S(1)}, u32[]{:S(2)}, u32[]{:S(2)}) async-start(bf16[2,64,12,128]{3,1,0,2:T(8,128)(2,1)} %copy.210), calls=%async_computation | async-start | bytes 786432 | tf_op jit(solution)/shard_map/all_to_all | solution.py:166
  546.3 198.5 %all-gather.8.cloned.1.call-start = ((), (), s32[]{:S(2)}) async-start(), calls=%async_computation.11 | async-start | bytes 1310720 | tf_op jit(solution)/shard_map/all_gather | solution.py:218
  757.9 52.2 %all-to-all-start.1 = ((bf16[2,256,3,128]{3,0,2,1:T(2,128)(2,1)}), bf16[2,256,3,128]{3,0,2,1:T(2,128)(2,1)S(1)}, u32[]{:S(2)}, u32[]{:S(2)}) async-start(bf16[2,256,3,128]{3,0,2,1:T(2,128)(2,1)} %copy.216), calls=%async_computation.1 | async-start | bytes 786432 | tf_op jit(solution)/shard_map/all_to_all | solution.py:225
  901.6 9.5 all-to-all-start.2
  905.8 148.8 %reduce-scatter.24.cloned.1.call-start = ((), (), s32[]{:S(2)}) async-start(), calls=%async_computation.14 | async-start | bytes 1310720
  941.3 219.5 %reduce-scatter.20.cloned.1.call-start = ((), (), s32[]{:S(2)}) async-start(), calls=%async_computation.12 | async-start | bytes 1310720
  960.2 206.6 %reduce-scatter.26.cloned.1.call-start = ((), (), s32[]{:S(2)}) async-start(), calls=%async_computation.15 | async-start | bytes 655360
  960.4 93.2 %copy-start.55 = (f32[128]{0:T(128)}, f32[128]{0:T(128)S(1)}, u32[]{:S(2)}) copy-start(f32[128]{0:T(128)S(1)} %rsqrt.22) | copy-start | bytes 1540
  1089.3 70.4 %all-to-all-start.3 = ((bf16[2,256,3,128]{3,0,2,1:T(2,128)(2,1)}), bf16[2,256,3,128]{3,0,2,1:T(2,128)(2,1)}, u32[]{:S(2)}, u32[]{:S(2)}) async-start(bf16[2,256,3,128]{3,0,2,1:T(2,128)(2,1)} %copy.227), calls=%async_computation.3 | async-start | bytes 786432 | tf_op jit(solution)/shard_map/all_to_all | solution.py:297
  1094.0 95.6 %reduce-scatter.22.cloned.1.call-start = ((), (), s32[]{:S(2)}) async-start(), calls=%async_computation.13 | async-start | bytes 655360
  1163.2 985.1 %reduce-scatter.28.cloned.1.call-start = ((), (), s32[]{:S(2)}) async-start(), calls=%async_computation.16 | async-start | bytes 97320960
  1197.6 66.7 %copy-start.53 = (f32[2880]{0:T(1024)S(1)}, f32[2880]{0:T(1024)}, u32[]{:S(2)}) copy-start(f32[2880]{0:T(1024)} %broadcast_select_fusion.9) | copy-start | bytes 34564
  1197.6 66.7 %copy-start.60 = (pred[2880]{0:T(1024)(128)(4,1)S(1)}, pred[2880]{0:T(1024)(128)(4,1)}, u32[]{:S(2)}) copy-start(pred[2880]{0:T(1024)(128)(4,1)} %get-tuple-element.1095) | copy-start | bytes 8644
  1391.0 48.1 %copy-start.63 = (f32[160]{0:T(256)S(1)}, f32[160]{0:T(256)}, u32[]{:S(2)}) copy-start(f32[160]{0:T(256)} %param.37) | copy-start | bytes 1924
  1391.1 48.8 %copy-start.21 = (f32[128,1536]{1,0:T(8,128)S(1)}, f32[128,1536]{1,0:T(8,128)}, u32[]{:S(2)}) copy-start(f32[128,1536]{1,0:T(8,128)} %get-tuple-element.1027) | copy-start | bytes 2359300
  (61 other events, 679.2 us)
Sparse Core Ops, SparseCore 0:
  15.3 486.5 all-gather.3
  518.4 28.8 all-gather.5
  633.2 28.3 all-gather.7
  941.5 25.4 reduce-scatter.23
  969.1 25.7 reduce-scatter.19
  1057.2 25.3 reduce-scatter.25
  1163.4 26.1 reduce-scatter.21
  1371.0 777.2 reduce-scatter.27

commit v2 on v0

v2 whole, which is shorter than its diff:
```python
import math

import jax
import jax.numpy as jnp
import numpy as np
from jax import lax
from jax.sharding import PartitionSpec as P

D = 1536
QH = 12
KVH = 2
HD = 128
FF = 8960
BLOCK = 128
QW = 1536
KVW = 256


NORM_EPS = 1e-06
ROPE_BASE = 1000000.0
BETA_FIRST = 0.5
BETA_SECOND = 0.5
ADAM_EPS = 1e-08
SCALE_EPS = 1e-06
RELATIVE_RATE = 0.5
SMALL_RATE = 0.25
WEIGHT_DECAY = 0.01
MASK_FILL = -1e30
TOP_PRECISION = lax.Precision.DEFAULT


def matrix_shapes():
    return [(D, QW), (D, KVW), (D, KVW), (QW, D), (D, FF), (D, FF), (FF, D)]


def split_small(vector):
    edges = [0, D, 2 * D, 2 * D + QW, 2 * D + QW + KVW, 2 * D + QW + 2 * KVW]
    return [vector[edges[number] : edges[number + 1]] for number in range(5)]


GRID_D = D // BLOCK
GRID_FF = FF // BLOCK
ATTN_TILES = GRID_D * (QW + 2 * KVW) // BLOCK + QW // BLOCK * GRID_D
ALL_AXES = ("dp", "blk", "uly")
COLUMN_AXES = ("dp", "uly")


def capacity(mean, factor, limit):
    return int(min(limit, math.ceil(mean + factor * math.sqrt(mean))))


def pick(table, index):
    return jnp.take(table, index, axis=0, mode="clip")


def earlier_equal(keys):
    number = jnp.arange(keys.shape[0], dtype=jnp.int32)
    same = keys[None, :] == keys[:, None]
    return jnp.sum((same & (number[None, :] < number[:, None])).astype(jnp.int32), axis=1)


def locate(wanted, keys, values):
    return jnp.sum(jnp.where(wanted[:, None] == keys[None, :], values[None, :], 0), axis=1)


def tiles_to_matrix(tiles, row_tiles, col_tiles):
    blocked = tiles.reshape(row_tiles, col_tiles, BLOCK, BLOCK)
    return blocked.transpose(0, 2, 1, 3).reshape(row_tiles * BLOCK, col_tiles * BLOCK)


def matrix_to_tiles(matrix):
    row_tiles = matrix.shape[0] // BLOCK
    col_tiles = matrix.shape[1] // BLOCK
    blocked = matrix.reshape(row_tiles, BLOCK, col_tiles, BLOCK)
    return blocked.transpose(0, 2, 1, 3).reshape(row_tiles * col_tiles, BLOCK, BLOCK)


def exchange(values, axes):
    return lax.all_to_all(values, axes, split_axis=0, concat_axis=0, tiled=True)


def spread(values, axes):
    count = lax.axis_size(axes)
    return exchange(jnp.broadcast_to(values[None], (count,) + values.shape), axes)


def exchange_sum(values, axes):
    return jnp.sum(exchange(values, axes).astype(jnp.float32), axis=0)


def shard_owners(owner_slot, shard_count, shard_groups):
    padded = shard_count * shard_groups
    first = ATTN_TILES
    members = []
    for _ in range(2):
        grid = owner_slot[first : first + GRID_D * GRID_FF].reshape(GRID_D, GRID_FF)
        grid = jnp.pad(grid, ((0, 0), (0, padded - GRID_FF)), constant_values=-1)
        members.append(
            grid.reshape(GRID_D, shard_count, shard_groups).transpose(1, 0, 2).reshape(shard_count, -1)
        )
        first = first + GRID_D * GRID_FF
    grid = owner_slot[first : first + GRID_D * GRID_FF].reshape(GRID_FF, GRID_D)
    grid = jnp.pad(grid, ((0, padded - GRID_FF), (0, 0)), constant_values=-1)
    members.append(grid.reshape(shard_count, -1))
    return jnp.concatenate(members, axis=1)


def rotate(values, positions, direction):
    half_size = HD // 2
    frequency = ROPE_BASE ** (-2.0 * jnp.arange(half_size, dtype=jnp.float32) / HD)
    angles = positions.astype(jnp.float32)[:, None] * frequency[None, :]
    cosine = jnp.cos(angles)[:, None, :]
    sine = direction * jnp.sin(angles)[:, None, :]
    first_half = values[..., :half_size]
    second_half = values[..., half_size:]
    return jnp.concatenate(
        [first_half * cosine - second_half * sine, second_half * cosine + first_half * sine],
        axis=-1,
    )


def forward_product(left_side, weight):
    return jnp.dot(left_side, weight, preferred_element_type=jnp.float32)


def back_product(grads, weight):
    return jnp.einsum("nf,df->nd", grads, weight, preferred_element_type=jnp.float32)


def outer_product(left_side, right_side):
    return jnp.einsum(
        "nb,nc->bc", left_side, right_side, preferred_element_type=jnp.float32
    ).astype(jnp.bfloat16)


def norm_backward(values, inverse, gain, grad_normed):
    scaled = values * inverse
    gained = grad_normed * gain
    grad_values = inverse * (gained - scaled * jnp.mean(gained * scaled, axis=-1, keepdims=True))
    return (grad_values, jnp.sum(grad_normed * scaled, axis=0))


def local(
    tokens,
    cotangent,
    lengths,
    owner_slot,
    master,
    moment_first,
    moment_second,
    basis_left,
    basis_right,
    small_master,
    small_first,
    small_second,
):
    uly_count = lax.axis_size("uly")
    blk_count = lax.axis_size("blk")
    all_count = lax.axis_size("dp") * blk_count * uly_count
    uly_index = lax.axis_index("uly")
    blk_index = lax.axis_index("blk")
    seq_count = tokens.shape[0]
    rows_local = tokens.shape[1]
    token_count = seq_count * rows_local
    span_rows = rows_local * uly_count
    heads_local = QH // uly_count
    slot_local = master.shape[0]
    slot_total = slot_local * all_count
    score_root = math.sqrt(HD)
    positions = (blk_index * uly_count + uly_index) * rows_local + jnp.arange(
        rows_local, dtype=jnp.int32
    )
    query_pos = blk_index * span_rows + jnp.arange(span_rows, dtype=jnp.int32)
    head_of = [member * heads_local // (QH // KVH) for member in range(uly_count)]
    dp_index = lax.axis_index("dp")
    my_device = (dp_index * blk_count + blk_index) * uly_count + uly_index
    my_column = dp_index * uly_count + uly_index
    column_count = lax.axis_size("dp") * uly_count
    shard_groups = -(-GRID_FF // blk_count)
    shard_tiles = 3 * GRID_D * shard_groups
    pair_cap = capacity(shard_tiles / all_count, 3.5, slot_local)
    column_cap = capacity(shard_tiles / column_count, 3.45, shard_tiles)
    attn_cap = capacity(ATTN_TILES / all_count, 3.8, slot_local)

    owners = shard_owners(owner_slot, blk_count, shard_groups)
    owner_flat = owners.reshape(-1)
    real_flat = owner_flat >= 0
    shard_flat = jnp.repeat(jnp.arange(blk_count, dtype=jnp.int32), shard_tiles)
    device_flat = jnp.maximum(owner_flat, 0) // slot_local
    column_flat = device_flat // (blk_count * uly_count) * uly_count + device_flat % uly_count
    source_flat = device_flat // uly_count % blk_count
    pair_flat = jnp.where(real_flat, device_flat * blk_count + shard_flat, -1)
    line_flat = jnp.where(real_flat, column_flat * blk_count + shard_flat, -1)
    pair_rank = earlier_equal(pair_flat)
    line_rank = earlier_equal(line_flat)
    attn_owner = owner_slot[:ATTN_TILES]
    attn_device = attn_owner // slot_local
    attn_rank = earlier_equal(attn_device)
    fits_shards = (jnp.max(jnp.where(real_flat, pair_rank, 0)) < pair_cap) & (
        jnp.max(jnp.where(real_flat, line_rank, 0)) < column_cap
    )
    fits_attn = jnp.max(attn_rank) < attn_cap
    my_first = my_device * slot_local

    def mine(flat):
        return lax.dynamic_slice_in_dim(flat, blk_index * shard_tiles, shard_tiles, 0)

    my_real = mine(real_flat)
    my_owner = mine(owner_flat)
    my_source = mine(source_flat)
    my_pair_rank = mine(pair_rank)
    my_line_rank = mine(line_rank)
    my_columns = mine(column_flat)
    in_column = my_real & (my_columns == my_column)
    place = jnp.where(my_real, my_columns * column_cap + my_line_rank, -1)
    send_key = jnp.where(
        real_flat & (device_flat == my_device) & (pair_rank < pair_cap),
        shard_flat * pair_cap + pair_rank,
        -1,
    )
    pair_slots = jnp.arange(blk_count * pair_cap, dtype=jnp.int32)
    send_index = locate(pair_slots, send_key, owner_flat - my_first)
    arrival = my_source * pair_cap + my_pair_rank
    fits_pair = my_pair_rank < pair_cap
    compact_index = locate(
        jnp.arange(column_cap, dtype=jnp.int32),
        jnp.where(in_column & fits_pair, my_line_rank, -1),
        arrival,
    )
    attn_send = locate(
        jnp.arange(attn_cap, dtype=jnp.int32),
        jnp.where(attn_device == my_device, attn_rank, -1),
        attn_owner - my_first,
    )
    attn_place = attn_device * attn_cap + attn_rank

    master_low = master.astype(jnp.bfloat16)
    small_copies = spread(small_master.astype(jnp.bfloat16), ALL_AXES).reshape(-1)
    attn_buffer = lax.all_gather(pick(master_low, attn_send), ALL_AXES, axis=0, tiled=True)

    def whole_tiles(index):
        return pick(lax.all_gather(master_low, ALL_AXES, axis=0, tiled=True), index)

    attn_tiles = lax.cond(
        fits_attn, lambda: pick(attn_buffer, attn_place), lambda: whole_tiles(attn_owner)
    )
    arrived_tiles = exchange(pick(master_low, send_index), "blk")
    shard_buffer = lax.all_gather(pick(arrived_tiles, compact_index), COLUMN_AXES, axis=0, tiled=True)
    shard_stack = lax.cond(
        fits_shards, lambda: pick(shard_buffer, place), lambda: whole_tiles(my_owner)
    )
    third = GRID_D * shard_groups
    real_groups = (
        blk_index * shard_groups + jnp.arange(shard_groups, dtype=jnp.int32)
    ) < GRID_FF
    real_hidden = jnp.repeat(real_groups, BLOCK)
    w_gate = jnp.where(
        real_hidden[None, :], tiles_to_matrix(shard_stack[:third], GRID_D, shard_groups), 0
    )
    w_up = jnp.where(
        real_hidden[None, :], tiles_to_matrix(shard_stack[third : 2 * third], GRID_D, shard_groups), 0
    )
    w_down = jnp.where(
        real_hidden[:, None], tiles_to_matrix(shard_stack[2 * third :], shard_groups, GRID_D), 0
    )
    attn_matrices = []
    first = 0
    for row_count, col_count in matrix_shapes()[:4]:
        tile_count = row_count // BLOCK * (col_count // BLOCK)
        attn_matrices.append(
            tiles_to_matrix(
                attn_tiles[first : first + tile_count], row_count // BLOCK, col_count // BLOCK
            )
        )
        first = first + tile_count
    w_query, w_key, w_value, w_out = attn_matrices
    smalls = [member.astype(jnp.float32) for member in split_small(small_copies)]
    gain_first, gain_second, bias_query, bias_key, bias_value = smalls
    valid_rows = (positions[None, :] < lengths[:, None]).astype(jnp.float32)
    seed_grad = (cotangent.astype(jnp.float32) * valid_rows[:, :, None]).reshape(token_count, D)
    seed_low = seed_grad.astype(jnp.bfloat16)
    seed_line = spread(seed_low, "blk").reshape(blk_count * token_count, D)
    token_rows = tokens.reshape(token_count, D).astype(jnp.float32)
    inverse_first = lax.rsqrt(jnp.mean(token_rows * token_rows, axis=-1, keepdims=True) + NORM_EPS)
    normed = (token_rows * inverse_first * gain_first).astype(jnp.bfloat16)
    query_lin = forward_product(normed, w_query) + bias_query
    key_lin = forward_product(normed, w_key) + bias_key
    value_rows = (
        (forward_product(normed, w_value) + bias_value)
        .astype(jnp.bfloat16)
        .reshape(seq_count, rows_local, KVH, HD)
    )
    query_rot = rotate(query_lin.reshape(seq_count, rows_local, QH, HD), positions, 1.0).astype(
        jnp.bfloat16
    )
    key_rot = rotate(key_lin.reshape(seq_count, rows_local, KVH, HD), positions, 1.0).astype(
        jnp.bfloat16
    )
    query_heads = lax.all_to_all(query_rot, "uly", split_axis=2, concat_axis=1, tiled=True)
    key_value = jnp.concatenate([key_rot, value_rows], axis=-1)
    key_value = jnp.stack([key_value[:, :, head] for head in head_of], axis=0)
    key_value = exchange(key_value, "uly").transpose(1, 0, 2, 3)
    key_value = spread(key_value, "blk").transpose(1, 0, 2, 3, 4)
    key_value = key_value.reshape(seq_count, blk_count * span_rows, 2 * HD)
    keys = key_value[..., :HD]
    values = key_value[..., HD:]
    key_pos = jnp.arange(blk_count * span_rows, dtype=jnp.int32)
    allowed = (key_pos[None, None, :] <= query_pos[None, :, None]) & (
        key_pos[None, None, :] < lengths[:, None, None]
    )
    allowed = allowed[:, :, None, :]
    scores = (
        jnp.einsum("sqhd,skd->sqhk", query_heads, keys, preferred_element_type=jnp.float32)
        / score_root
    )
    scores = jnp.where(allowed, scores, MASK_FILL)
    top = jnp.max(scores, axis=-1, keepdims=True)
    weights = jnp.where(allowed, jnp.exp(scores - top), 0.0)
    probs = weights / jnp.sum(weights, axis=-1, keepdims=True)
    probs_low = probs.astype(jnp.bfloat16)
    attended = jnp.einsum(
        "sqhk,skd->sqhd", probs_low, values, preferred_element_type=jnp.float32
    )
    out_rows = lax.all_to_all(
        attended.astype(jnp.bfloat16), "uly", split_axis=1, concat_axis=2, tiled=True
    ).reshape(token_count, QW)
    middle = token_rows + forward_product(out_rows, w_out)
    inverse_second = lax.rsqrt(jnp.mean(middle * middle, axis=-1, keepdims=True) + NORM_EPS)
    normed_two = (middle * inverse_second * gain_second).astype(jnp.bfloat16)
    normed_line = spread(normed_two, "blk").reshape(blk_count * token_count, D)
    gate_lin = forward_product(normed_line, w_gate)
    upward = forward_product(normed_line, w_up)
    hidden = (jax.nn.silu(gate_lin) * upward).astype(jnp.bfloat16)
    grad_hidden = back_product(seed_line, w_down)
    gate_sigmoid = jax.nn.sigmoid(gate_lin)
    grad_gate = (
        grad_hidden * upward * gate_sigmoid * (1.0 + gate_lin * (1.0 - gate_sigmoid))
    ).astype(jnp.bfloat16)
    grad_up = (grad_hidden * gate_lin * gate_sigmoid).astype(jnp.bfloat16)
    grad_line = back_product(grad_gate, w_gate) + back_product(grad_up, w_up)
    grad_normed_two = exchange_sum(
        grad_line.astype(jnp.bfloat16).reshape(blk_count, token_count, D), "blk"
    )
    mixed_line = forward_product(hidden, w_down).astype(jnp.bfloat16)
    mixed_out = (
        (middle + exchange_sum(mixed_line.reshape(blk_count, token_count, D), "blk"))
        .astype(jnp.bfloat16)
        .reshape(seq_count, rows_local, D)
    )
    shard_grads = jnp.concatenate(
        [
            matrix_to_tiles(outer_product(normed_line, grad_gate)),
            matrix_to_tiles(outer_product(normed_line, grad_up)),
            matrix_to_tiles(outer_product(hidden, seed_line)),
        ],
        axis=0,
    )
    scatter_index = locate(
        jnp.arange(column_count * column_cap, dtype=jnp.int32),
        place,
        jnp.arange(shard_tiles, dtype=jnp.int32),
    )
    column_grads = lax.psum_scatter(
        pick(shard_grads, scatter_index), COLUMN_AXES, scatter_dimension=0, tiled=True
    )
    return_key = jnp.where(in_column & fits_pair, arrival, -1)
    returned_grads = exchange(pick(column_grads, locate(pair_slots, return_key, my_line_rank)), "blk")
    norm_part_two, gain_second_grad = norm_backward(
        middle, inverse_second, gain_second, grad_normed_two
    )
    grad_middle = seed_grad + norm_part_two
    grad_middle_low = grad_middle.astype(jnp.bfloat16)
    grad_out_rows = (
        back_product(grad_middle_low, w_out)
        .astype(jnp.bfloat16)
        .reshape(seq_count, rows_local, QH, HD)
    )
    grad_heads = lax.all_to_all(grad_out_rows, "uly", split_axis=2, concat_axis=1, tiled=True)
    grad_heads_wide = grad_heads.astype(jnp.float32)
    row_delta = jnp.sum(grad_heads_wide * attended, axis=-1)

    grad_prob = jnp.einsum(
        "sqhd,skd->sqhk", grad_heads, values, preferred_element_type=jnp.float32
    )
    grad_score = (probs * (grad_prob - row_delta[..., None])).astype(jnp.bfloat16)
    grad_query = jnp.einsum(
        "sqhk,skd->sqhd", grad_score, keys, preferred_element_type=jnp.float32
    )
    grad_keys = jnp.einsum(
        "sqhk,sqhd->skd", grad_score, query_heads, preferred_element_type=jnp.float32
    )
    grad_values = jnp.einsum(
        "sqhk,sqhd->skd", probs_low, grad_heads, preferred_element_type=jnp.float32
    )
    grad_query_low = (grad_query / score_root).astype(jnp.bfloat16)
    grad_query_rows = lax.all_to_all(grad_query_low, "uly", split_axis=1, concat_axis=2, tiled=True)
    grad_pair = jnp.concatenate([grad_keys / score_root, grad_values], axis=-1).astype(jnp.bfloat16)
    grad_pair = grad_pair.reshape(seq_count, blk_count, span_rows, 2 * HD).transpose(1, 0, 2, 3)
    grad_pair = exchange_sum(grad_pair, "blk").astype(jnp.bfloat16)
    grad_pair = grad_pair.reshape(seq_count, uly_count, rows_local, 2 * HD).transpose(1, 0, 2, 3)
    grad_pair = exchange(grad_pair, "uly").astype(jnp.float32)
    grad_pair = jnp.stack(
        [
            sum(grad_pair[member] for member in range(uly_count) if head_of[member] == head)
            for head in range(KVH)
        ],
        axis=2,
    )
    grad_keys_rows = grad_pair[..., :HD]
    grad_values_rows = grad_pair[..., HD:]
    grad_query_lin = (
        rotate(grad_query_rows.astype(jnp.float32), positions, -1.0)
        .astype(jnp.bfloat16)
        .reshape(token_count, QW)
    )
    key_rounded = grad_keys_rows
    grad_key_lin = (
        rotate(key_rounded, positions, -1.0).astype(jnp.bfloat16).reshape(token_count, KVW)
    )
    grad_value_lin = grad_values_rows.astype(jnp.bfloat16).reshape(token_count, KVW)
    grad_normed = (
        back_product(grad_query_lin, w_query)
        + back_product(grad_key_lin, w_key)
        + back_product(grad_value_lin, w_value)
    )
    norm_part_first, gain_first_grad = norm_backward(
        token_rows, inverse_first, gain_first, grad_normed
    )
    grad_tokens = (grad_middle + norm_part_first).reshape(seq_count, rows_local, D)
    small_partial = jnp.concatenate(
        [
            gain_first_grad,
            gain_second_grad,
            jnp.sum(grad_query_lin, axis=0, dtype=jnp.float32),
            jnp.sum(grad_key_lin, axis=0, dtype=jnp.float32),
            jnp.sum(grad_value_lin, axis=0, dtype=jnp.float32),
        ]
    )
    grad_small = exchange_sum(small_partial.reshape(all_count, -1), ALL_AXES)
    attn_grads = jnp.concatenate(
        [
            matrix_to_tiles(outer_product(normed, grad_query_lin)),
            matrix_to_tiles(outer_product(normed, grad_key_lin)),
            matrix_to_tiles(outer_product(normed, grad_value_lin)),
            matrix_to_tiles(outer_product(out_rows, grad_middle_low)),
        ],
        axis=0,
    )
    attn_index = locate(
        jnp.arange(all_count * attn_cap, dtype=jnp.int32),
        attn_place,
        jnp.arange(ATTN_TILES, dtype=jnp.int32),
    )
    attn_returned = lax.psum_scatter(
        pick(attn_grads, attn_index), ALL_AXES, scatter_dimension=0, tiled=True
    )
    my_slots = my_first + jnp.arange(slot_local, dtype=jnp.int32)
    slot_index = locate(my_slots, owner_flat, shard_flat * pair_cap + pair_rank) + locate(
        my_slots, attn_owner, blk_count * pair_cap + attn_rank
    )
    slot_used = jnp.any(my_slots[:, None] == owner_slot[None, :], axis=1)

    def routed_grads():
        return pick(jnp.concatenate([returned_grads, attn_returned], axis=0), slot_index)

    def summed_grads():
        every_slot = jnp.arange(slot_total, dtype=jnp.int32)
        tile_owner = jnp.concatenate([my_owner, attn_owner])
        index = locate(every_slot, tile_owner, jnp.arange(tile_owner.shape[0], dtype=jnp.int32))
        held = jnp.any(every_slot[:, None] == tile_owner[None, :], axis=1)
        parts = pick(jnp.concatenate([shard_grads, attn_grads], axis=0), index)
        parts = jnp.where(held[:, None, None], parts, 0)
        return lax.psum_scatter(parts, ALL_AXES, scatter_dimension=0, tiled=True)

    grad_slots = lax.cond(fits_shards & fits_attn, routed_grads, summed_grads)
    grad_slots = jnp.where(slot_used[:, None, None], grad_slots, 0).astype(jnp.float32)
    rotated = jnp.einsum("sji,sjk->sik", basis_left, grad_slots, precision=TOP_PRECISION)
    rotated = jnp.einsum("sik,skl->sil", rotated, basis_right, precision=TOP_PRECISION)
    first_new = BETA_FIRST * moment_first + (1.0 - BETA_FIRST) * rotated
    second_new = BETA_SECOND * moment_second + (1.0 - BETA_SECOND) * rotated * rotated
    normalized = first_new / (jnp.sqrt(second_new) + ADAM_EPS)
    update = jnp.einsum("sik,skl->sil", basis_left, normalized, precision=TOP_PRECISION)
    update = jnp.einsum("sik,slk->sil", update, basis_right, precision=TOP_PRECISION)
    tile_scale = jnp.sqrt(jnp.mean(master * master, axis=(1, 2), keepdims=True) + SCALE_EPS)
    master_new = master - RELATIVE_RATE * tile_scale * (update + WEIGHT_DECAY * master)
    small_first_new = BETA_FIRST * small_first + (1.0 - BETA_FIRST) * grad_small
    small_second_new = BETA_SECOND * small_second + (1.0 - BETA_SECOND) * grad_small * grad_small
    small_new = small_master - SMALL_RATE * (
        small_first_new / (jnp.sqrt(small_second_new) + ADAM_EPS) + WEIGHT_DECAY * small_master
    )
    return (
        mixed_out,
        grad_tokens,
        first_new,
        second_new,
        master_new,
        small_first_new,
        small_second_new,
        small_new,
    )


def solution(mesh):
    in_specs = (
        P("dp", ("blk", "uly"), None),
        P("dp", ("blk", "uly"), None),
        P("dp"),
        P(),
        P(("dp", "blk", "uly"), None, None),
        P(("dp", "blk", "uly"), None, None),
        P(("dp", "blk", "uly"), None, None),
        P(("dp", "blk", "uly"), None, None),
        P(("dp", "blk", "uly"), None, None),
        P(("dp", "blk", "uly")),
        P(("dp", "blk", "uly")),
        P(("dp", "blk", "uly")),
    )
    out_specs = (
        P("dp", ("blk", "uly"), None),
        P("dp", ("blk", "uly"), None),
        P(("dp", "blk", "uly"), None, None),
        P(("dp", "blk", "uly"), None, None),
        P(("dp", "blk", "uly"), None, None),
        P(("dp", "blk", "uly")),
        P(("dp", "blk", "uly")),
        P(("dp", "blk", "uly")),
    )
    return jax.shard_map(local, mesh=mesh, in_specs=in_specs, out_specs=out_specs, check_vma=False)
```

time: 3000 us -> 1570 us (0.52)
  waiting for transfers between devices: 1910 us -> 846 us
  matrix products: 344 us -> 152 us
  local copies, waits for them, and re-layouts: 492 us -> 343 us
  blocking collectives: 106 us -> 13.8 us
  starting transfers between devices: 18.3 us -> 84.6 us
    unnamed x13 -> x5, waiting for transfers between devices: 1470 us -> 0.63 us
    reduce_scatter x0 -> x1, waiting for transfers between devices: none -> 425 us  [local(): lax.psum_scatter(pick(attn_grads, attn_index), ALL_AXES, scatter_dimensio...]
    all_gather x3 -> x2, waiting for transfers between devices: 434 us -> 82.4 us  [the longest x1 60.7 us: local(): lax.all_gather(pick(master_low, attn_send), ALL_AXES, axis=0, tiled=True)]
    all_to_all x1 -> x12, waiting for transfers between devices: 3.8 us -> 325 us  [exchange(): return lax.all_to_all(values, axes, split_axis=0, concat_axis=0, tiled=True)]
    gather x14 -> x9, local copies, waits for them, and re-layouts: 303 us -> 129 us  [pick(): return jnp.take(table, index, axis=0, mode='clip')]
    dot_general x31 -> x12, matrix products: 192 us -> 42.5 us  [the longest x7 31.2 us: outer_product(): jnp.einsum('nb,nc->bc', left_side, right_side, preferred_element_type=jnp...]
    unnamed x2 -> x0, blocking collectives: 87.5 us -> none
    all_to_all x1 -> x12, starting transfers between devices: 4.2 us -> 71.9 us  [exchange(): return lax.all_to_all(values, axes, split_axis=0, concat_axis=0, tiled=True)]
  transfers between devices with their start and end apart: 12 -> 19, of which waited for: 4 -> 15; matrix products, arithmetic and copies ran while one was open for 17% -> 22% of each run, Pallas kernels for 0% -> 0%
where the time goes in v2:
time: 1570 us; the launch traced here: 1560 us
  waiting for transfers between devices  846 us (54%)
  local copies, waits for them, and re-layouts  343 us (22%)
  matrix products  152 us (10%)
  other arithmetic  94.8 us (6%)
  starting transfers between devices  84.6 us (5%)
  between operations  19.6 us (1%)
    reduce_scatter x1, waiting for transfers between devices, local(): lax.psum_scatter(pick(attn_grads, attn_index), ALL_AXES, scatter_dimensio...  425 us
    all_to_all x12, waiting for transfers between devices, exchange(): return lax.all_to_all(values, axes, split_axis=0, concat_axis=0, tiled=True)  325 us
    gather x9, local copies, waits for them, and re-layouts, pick(): return jnp.take(table, index, axis=0, mode='clip')  129 us
    all_to_all x12, starting transfers between devices, exchange(): return lax.all_to_all(values, axes, split_axis=0, concat_axis=0, tiled=True)  71.9 us
    all_gather x1, waiting for transfers between devices, local(): lax.all_gather(pick(master_low, attn_send), ALL_AXES, axis=0, tiled=True)  60.7 us
    reshape x7, local copies, waits for them, and re-layouts, matrix_to_tiles(): blocked = matrix.reshape(row_tiles, BLOCK, col_tiles, BLOCK)  59.5 us
    reshape x7, local copies, waits for them, and re-layouts, tiles_to_matrix(): blocked = tiles.reshape(row_tiles, col_tiles, BLOCK, BLOCK)  57.1 us
    transpose x7, local copies, waits for them, and re-layouts, matrix_to_tiles(): blocked.transpose(0, 2, 1, 3).reshape(row_tiles * col_tiles, BLOCK, BLOCK)  39.4 us
  transfers between devices with their start and end apart: 19, of which 15 were waited for; matrix products, arithmetic and copies ran while one was open for 22% of the time, Pallas kernels for 0%

profile of v2, /device:TPU:10, one launch (start us, length us, event | category | flops | bytes accessed | tf_op | source)
XLA Modules:
  0.0 1556.9 jit_solution(5346334344662711570)
XLA Ops:
  42.7 142.6 %all-to-all-done.6 = bf16[144,128,128]{2,1,0:T(8,128)(2,1)} async-done(((bf16[144,128,128]{2,1,0:T(8,128)(2,1)}), bf16[144,128,128]{2,1,0:T(8,128)(2,1)}, u32[]{:S(2)}, u32[]{:S(2)}) %all-to-all-start.6) | async-done | bytes 4718624 | tf_op jit(solution)/shard_map/all_to_all | solution.py:79
  190.7 60.7 %all-gather.11.cloned.1.call-done = bf16[736,128,128]{2,1,0:T(8,128)(2,1)} async-done(((bf16[23,128,128]{2,1,0:T(8,128)(2,1)}), bf16[736,128,128]{2,1,0:T(8,128)(2,1)}) %all-gather.11.cloned.1.call-update) | async-done | bytes 24117264 | tf_op jit(solution)/shard_map/all_gather | solution.py:239
  251.4 21.5 %conditional.3 = (bf16[336,128,128]{2,1,0:T(8,128)(2,1)}) conditional(s32[]{:T(128)} %convert_element_type.248, (bf16[90,128,128]{2,1,0:T(8,128)(2,1)}, s32[336]{0:T(512)S(1)}) %tuple.27, (s32[336]{0:T(512)S(1)}, bf16[736,128,128]{2,1,0:T(8,128)(2,1)}) %tuple.28), branch_computations={%region_4.5_spmd, %region_5.6_spmd} | conditional | flops 1024 | bytes 313989824 | solution.py:244
  254.3 18.7 %gather_fusion = bf16[336,128,128]{2,1,0:T(8,128)(2,1)} fusion(bf16[736,128,128]{2,1,0:T(8,128)(2,1)} %get-tuple-element.83, s32[1024]{0:T(1024)S(1)} %pad_clamp_fusion.1), kind=kCustom, calls=%fused_computation.1 | custom fusion | bytes 22021440 | tf_op jit(solution)/shard_map/cond/branch_1_fun/jit(_take)/gather | solution.py:53
  346.1 18.2 %all-to-all-done.3 = bf16[4,2,4,64,256]{4,3,2,1,0:T(8,128)(2,1)S(1)} async-done(((bf16[4,2,4,64,256]{4,3,2,1,0:T(8,128)(2,1)}), bf16[4,2,4,64,256]{4,3,2,1,0:T(8,128)(2,1)S(1)}, u32[]{:S(2)}, u32[]{:S(2)}) %all-to-all-start.3) | async-done | bytes 1048608 | tf_op jit(solution)/shard_map/all_to_all | solution.py:79
  409.2 21.6 %all-gather.13.cloned.1.call-done = bf16[904,128,128]{2,1,0:T(8,128)(2,1)} async-done(((bf16[113,128,128]{2,1,0:T(8,128)(2,1)}), bf16[904,128,128]{2,1,0:T(8,128)(2,1)}) %all-gather.13.cloned.1.call-update) | async-done | bytes 29622288 | tf_op jit(solution)/shard_map/all_gather | solution.py:248
  430.9 28.0 %conditional.4 = (bf16[648,128,128]{2,1,0:T(8,128)(2,1)}) conditional(s32[]{:T(128)} %convert_element_type.261, (bf16[90,128,128]{2,1,0:T(8,128)(2,1)}, s32[648]{0:T(1024)S(1)}) %tuple.29, (s32[648]{0:T(1024)S(1)}, bf16[904,128,128]{2,1,0:T(8,128)(2,1)}) %tuple.30), branch_computations={%region_15.16_spmd, %region_16.17_spmd} | conditional | flops 1024 | bytes 334439552 | solution.py:249
  431.3 27.5 %gather_fusion.1 = bf16[648,128,128]{2,1,0:T(8,128)(2,1)} fusion(bf16[904,128,128]{2,1,0:T(8,128)(2,1)} %get-tuple-element.87, s32[1024]{0:T(1024)S(1)} %pad_clamp_fusion.3), kind=kCustom, calls=%fused_computation.3 | custom fusion | bytes 42469920 | tf_op jit(solution)/shard_map/cond/branch_1_fun/jit(_take)/gather | solution.py:53
  458.8 14.2 fusion.135
  502.1 14.1 bitcast_select_fusion.2
  554.5 13.8 reshape.836
  584.9 13.1 reshape.834
  614.5 13.2 reshape.832
  636.6 14.4 pad_maximum_fusion.2
  651.0 27.2 %gather_fusion.9 = bf16[904,128,128]{2,1,0:T(8,128)(2,1)} fusion(bf16[648,128,128]{2,1,0:T(8,128)(2,1)} %pad_maximum_fusion.2, s32[1024]{0:T(1024)S(1)} %pad_clamp_fusion.8), kind=kCustom, calls=%fused_computation.9 | custom fusion | bytes 59248160 | tf_op jit(solution)/shard_map/jit(_take)/gather | solution.py:53
  678.3 14.1 copy.313
  692.4 16.0 %copy.312 = bf16[12,18,128,128]{3,1,2,0:T(8,128)(2,1)} copy(bf16[12,18,128,128]{3,2,1,0:T(8,128)(2,1)} %bitcast.268) | data formatting | bytes 14155776 | tf_op jit(solution)/shard_map/reshape | solution.py:67
  775.3 31.5 %all-to-all-done.7 = bf16[4,128,1536]{2,1,0:T(8,128)(2,1)} async-done(((bf16[4,128,1536]{2,1,0:T(8,128)(2,1)}), bf16[4,128,1536]{2,1,0:T(8,128)(2,1)}, u32[]{:S(2)}, u32[]{:S(2)}) %all-to-all-start.7) | async-done | bytes 1572896 | tf_op jit(solution)/shard_map/all_to_all | solution.py:79
  816.0 13.8 all_to_all.125
  924.2 22.8 %gather_fusion.11 = bf16[736,128,128]{2,1,0:T(8,128)(2,1)} fusion(bf16[336,128,128]{2,1,0:T(8,128)(2,1)} %pad_maximum_fusion.3, s32[1024]{0:T(1024)S(1)} %copy-done.59), kind=kCustom, calls=%fused_computation.11 | custom fusion | bytes 48237440 | tf_op jit(solution)/shard_map/jit(_take)/gather | solution.py:53
  982.1 97.4 %all-to-all-done.14 = bf16[144,128,128]{2,1,0:T(8,128)(2,1)} async-done(((bf16[144,128,128]{2,1,0:T(8,128)(2,1)}), bf16[144,128,128]{2,1,0:T(8,128)(2,1)}, u32[]{:S(2)}, u32[]{:S(2)}) %all-to-all-start.14) | async-done | bytes 4718624 | tf_op jit(solution)/shard_map/all_to_all | solution.py:79
  1079.5 424.7 %reduce-scatter.10.cloned.1.call-done = bf16[23,128,128]{2,1,0:T(8,128)(2,1)} async-done(((bf16[736,128,128]{2,1,0:T(8,128)(2,1)}), bf16[23,128,128]{2,1,0:T(8,128)(2,1)}) %reduce-scatter.10.cloned.1.call-update) | async-done | bytes 753680 | tf_op jit(solution)/shard_map/reduce_scatter | solution.py:454
  1516.0 16.1 %fusion.22 = (f32[90,128,128]{2,1,0:T(8,128)}, f32[90,128,128]{2,1,0:T(8,128)}) fusion(f32[90,128,128]{2,1,0:T(8,128)} %param.24, f32[90,128,128]{2,1,0:T(8,128)} %param.23, f32[90,128,128]{2,1,0:T(8,128)} %param.26, f32[90,128,128]{2,1,0:T(8,128)} %param.25, bf16[90,128,128]{2,1,0:T(8,128)(2,1)} %get-tuple-element.198, pred[90]{0:T(512)(128)(4,1)S(1)} %copy-done.69), kind=kOutput, calls=%fused_computation.71 | convolution fusion | flops 765296640 | bytes 38338648 | tf_op jit(solution)/shard_map/sik,skl->sil/dot_general | solution.py:478
  1532.1 16.8 %multiply_subtract_fusion = f32[90,128,128]{2,1,0:T(8,128)} fusion(f32[90,128,128]{2,1,0:T(8,128)} %param.22, f32[90]{0:T(128)S(1)} %copy-done.76, f32[90,128,128]{2,1,0:T(8,128)} %param.26, f32[90,128,128]{2,1,0:T(8,128)} %param.25, f32[90,128,128]{2,1,0:T(8,128)} %get-tuple-element.146, f32[90,128,128]{2,1,0:T(8,128)} %get-tuple-element.145), kind=kOutput, calls=%fused_computation.72 | convolution fusion | flops 763822080 | bytes 35389800 | tf_op jit(solution)/shard_map/sik,slk->sil/dot_general | solution.py:483
  (408 shorter events, 492.7 us)
Async XLA Ops:
  8.0 243.4 %all-gather.11.cloned.1.call-start = ((), (), s32[]{:S(2)}) async-start(), calls=%async_computation.23 | async-start | bytes 24870912 | tf_op jit(solution)/shard_map/all_gather | solution.py:239
  33.4 151.9 %all-to-all-start.6 = ((bf16[144,128,128]{2,1,0:T(8,128)(2,1)}), bf16[144,128,128]{2,1,0:T(8,128)(2,1)}, u32[]{:S(2)}, u32[]{:S(2)}) async-start(bf16[144,128,128]{2,1,0:T(8,128)(2,1)} %gather_fusion.7), calls=%async_computation.7 | async-start | bytes 9437184 | tf_op jit(solution)/shard_map/all_to_all | solution.py:79
  273.0 157.9 %all-gather.13.cloned.1.call-start = ((), (), s32[]{:S(2)}) async-start(), calls=%async_computation.24 | async-start | bytes 33325056 | tf_op jit(solution)/shard_map/all_gather | solution.py:248
  274.2 10.3 all-to-all-start
  309.8 13.6 all-to-all-start.2
  323.4 12.8 all-to-all-start.1
  337.2 27.1 %all-to-all-start.3 = ((bf16[4,2,4,64,256]{4,3,2,1,0:T(8,128)(2,1)}), bf16[4,2,4,64,256]{4,3,2,1,0:T(8,128)(2,1)S(1)}, u32[]{:S(2)}, u32[]{:S(2)}) async-start(bf16[4,2,4,64,256]{4,3,2,1,0:T(8,128)(2,1)} %broadcast_in_dim.376), calls=%async_computation.4 | async-start | bytes 2097152 | tf_op jit(solution)/shard_map/all_to_all | solution.py:79
  380.2 14.8 all-to-all-start.4
  396.3 87.7 %all-to-all-start.8 = ((bf16[4,128,1536]{2,1,0:T(8,128)(2,1)}), bf16[4,128,1536]{2,1,0:T(8,128)(2,1)S(1)}, u32[]{:S(2)}, u32[]{:S(2)}) async-start(bf16[4,128,1536]{2,1,0:T(8,128)(2,1)} %broadcast_in_dim.394), calls=%async_computation.9 | async-start | bytes 3145728 | tf_op jit(solution)/shard_map/all_to_all | solution.py:79
  486.4 39.5 %all-to-all-start.5 = ((bf16[4,128,1536]{2,1,0:T(8,128)(2,1)}), bf16[4,128,1536]{2,1,0:T(8,128)(2,1)}, u32[]{:S(2)}, u32[]{:S(2)}) async-start(bf16[4,128,1536]{2,1,0:T(8,128)(2,1)} %broadcast_in_dim.379), calls=%async_computation.6 | async-start | bytes 3145728 | tf_op jit(solution)/shard_map/all_to_all | solution.py:79
  491.8 468.9 %reduce-scatter.12.cloned.1.call-start = ((), (), s32[]{:S(2)}) async-start(), calls=%async_computation.25 | async-start | bytes 33325056
  724.6 40.0 %all-to-all-start.9 = ((bf16[4,128,1536]{2,1,0:T(8,128)(2,1)}), bf16[4,128,1536]{2,1,0:T(8,128)(2,1)S(1)}, u32[]{:S(2)}, u32[]{:S(2)}) async-start(bf16[4,128,1536]{2,1,0:T(8,128)(2,1)} %bitcast.38), calls=%async_computation.10 | async-start | bytes 3145728 | tf_op jit(solution)/shard_map/all_to_all | solution.py:79
  765.7 41.0 %all-to-all-start.7 = ((bf16[4,128,1536]{2,1,0:T(8,128)(2,1)}), bf16[4,128,1536]{2,1,0:T(8,128)(2,1)}, u32[]{:S(2)}, u32[]{:S(2)}) async-start(bf16[4,128,1536]{2,1,0:T(8,128)(2,1)} %bitcast.330), calls=%async_computation.8 | async-start | bytes 3145728 | tf_op jit(solution)/shard_map/all_to_all | solution.py:79
  837.6 15.0 all-to-all-start.11
  852.6 31.3 %all-to-all-start.12 = ((bf16[4,2,256,256]{3,2,1,0:T(8,128)(2,1)}), bf16[4,2,256,256]{3,2,1,0:T(8,128)(2,1)S(1)}, u32[]{:S(2)}, u32[]{:S(2)}) async-start(bf16[4,2,256,256]{3,2,1,0:T(8,128)(2,1)} %copy_bitcast_fusion), calls=%async_computation.13 | async-start | bytes 2097152 | tf_op jit(solution)/shard_map/all_to_all | solution.py:79
  884.9 23.5 %all-to-all-start.13 = ((bf16[4,2,64,256]{3,2,1,0:T(8,128)(2,1)}), bf16[4,2,64,256]{3,2,1,0:T(8,128)(2,1)S(1)}, u32[]{:S(2)}, u32[]{:S(2)}) async-start(bf16[4,2,64,256]{3,2,1,0:T(8,128)(2,1)} %bitcast.265), calls=%async_computation.14 | async-start | bytes 524288 | tf_op jit(solution)/shard_map/all_to_all | solution.py:79
  888.8 615.5 %reduce-scatter.10.cloned.1.call-start = ((), (), s32[]{:S(2)}) async-start(), calls=%async_computation.22 | async-start | bytes 24870912 | tf_op jit(solution)/shard_map/reduce_scatter | solution.py:454
  954.6 18.1 %all-to-all-start.15 = ((f32[32,1,160]{2,1,0:T(1,128)}), f32[32,1,160]{2,1,0:T(1,128)S(1)}, u32[]{:S(2)}, u32[]{:S(2)}) async-start(f32[32,1,160]{2,1,0:T(1,128)} %all_to_all.107), calls=%async_computation.17 | async-start | bytes 65536 | tf_op jit(solution)/shard_map/all_to_all | solution.py:79
  970.3 534.0 %copy-start.39 = (s32[2592]{0:T(1024)S(1)}, s32[2592]{0:T(1024)}, u32[]{:S(2)}) copy-start(s32[2592]{0:T(1024)} %copy-done.38) | copy-start | bytes 31108
  970.3 533.9 %copy-start.42 = (s32[2592]{0:T(1024)S(1)}, s32[2592]{0:T(1024)}, u32[]{:S(2)}) copy-start(s32[2592]{0:T(1024)} %copy-done.41) | copy-start | bytes 31108
  970.3 533.9 %copy-start.52 = (s32[648]{0:T(1024)S(1)}, s32[648]{0:T(1024)}, u32[]{:S(2)}) copy-start(s32[648]{0:T(1024)} %copy-done.51) | copy-start | bytes 7780
  970.4 533.9 %copy-start.54 = (s32[336]{0:T(512)S(1)}, s32[336]{0:T(512)}, u32[]{:S(2)}) copy-start(s32[336]{0:T(512)} %copy-done.53) | copy-start | bytes 4036
  970.4 533.9 %copy-start.58 = (s32[336]{0:T(512)S(1)}, s32[336]{0:T(512)}, u32[]{:S(2)}) copy-start(s32[336]{0:T(512)} %copy-done.57) | copy-start | bytes 4036
  972.7 106.9 %all-to-all-start.14 = ((bf16[144,128,128]{2,1,0:T(8,128)(2,1)}), bf16[144,128,128]{2,1,0:T(8,128)(2,1)}, u32[]{:S(2)}, u32[]{:S(2)}) async-start(bf16[144,128,128]{2,1,0:T(8,128)(2,1)} %gather_fusion.10), calls=%async_computation.15 | async-start | bytes 9437184 | tf_op jit(solution)/shard_map/all_to_all | solution.py:79
  (82 other events, 2573.3 us)
Sparse Core Ops, SparseCore 0:
  20.5 230.8 all-gather.10
Sparse Core Ops, SparseCore 1:
  275.9 154.9 all-gather.12
  678.3 191.1 reduce-scatter.11
  947.2 557.1 reduce-scatter.9

commit v3 on v2

--- a/solution.py
+++ b/solution.py
@@ -103,6 +103,93 @@
     grid = jnp.pad(grid, ((0, padded - GRID_FF), (0, 0)), constant_values=-1)
     members.append(grid.reshape(shard_count, -1))
     return jnp.concatenate(members, axis=1)
+
+
+def attention_owners(owner_slot, shard_count, shard_rows):
+    grids = []
+    first = 0
+    for row_count, col_count in matrix_shapes()[:4]:
+        tile_count = row_count // BLOCK * (col_count // BLOCK)
+        grids.append(owner_slot[first : first + tile_count].reshape(row_count // BLOCK, -1))
+        first = first + tile_count
+    members = []
+    for grid in (jnp.concatenate(grids[:3], axis=1), grids[3]):
+        missing = shard_count * shard_rows - grid.shape[0]
+        grid = jnp.pad(grid, ((0, missing), (0, 0)), constant_values=-1)
+        members.append(grid.reshape(shard_count, -1))
+    return jnp.concatenate(members, axis=1)
+
+
+def split_columns(values, shard_count, shard_rows):
+    width = shard_rows * BLOCK
+    padded = jnp.pad(values, ((0, 0), (0, shard_count * width - values.shape[1])))
+    parts = padded.reshape(values.shape[0], shard_count, width).transpose(1, 0, 2)
+    return exchange(parts, "blk").reshape(-1, width)
+
+
+class Route:
+    def __init__(self, owners, slot_local, factors):
+        uly_count = lax.axis_size("uly")
+        blk_count = lax.axis_size("blk")
+        blk_index = lax.axis_index("blk")
+        self.column_count = lax.axis_size("dp") * uly_count
+        self.column = lax.axis_index("dp") * uly_count + lax.axis_index("uly")
+        self.device = (lax.axis_index("dp") * blk_count + blk_index) * uly_count + lax.axis_index(
+            "uly"
+        )
+        self.tiles = owners.shape[1]
+        self.pair_cap = capacity(self.tiles / (self.column_count * blk_count), factors[0], slot_local)
+        self.column_cap = capacity(self.tiles / self.column_count, factors[1], self.tiles)
+        flat = owners.reshape(-1)
+        self.owner = flat
+        self.first = self.device * slot_local
+        self.real = flat >= 0
+        self.shard = jnp.repeat(jnp.arange(blk_count, dtype=jnp.int32), self.tiles)
+        self.holder = jnp.maximum(flat, 0) // slot_local
+        columns = self.holder // (blk_count * uly_count) * uly_count + self.holder % uly_count
+        source = self.holder // uly_count % blk_count
+        self.pair_rank = earlier_equal(jnp.where(self.real, self.holder * blk_count + self.shard, -1))
+        line_rank = earlier_equal(jnp.where(self.real, columns * blk_count + self.shard, -1))
+        self.fits = (jnp.max(jnp.where(self.real, self.pair_rank, 0)) < self.pair_cap) & (
+            jnp.max(jnp.where(self.real, line_rank, 0)) < self.column_cap
+        )
+
+        def mine(values):
+            return lax.dynamic_slice_in_dim(values, blk_index * self.tiles, self.tiles, 0)
+
+        self.my_owner = mine(flat)
+        self.my_rank = mine(line_rank)
+        my_real = mine(self.real)
+        my_columns = mine(columns)
+        my_pair_rank = mine(self.pair_rank)
+        self.place = jnp.where(my_real, my_columns * self.column_cap + self.my_rank, -1)
+        self.held = my_real & (my_columns == self.column) & (my_pair_rank < self.pair_cap)
+        self.arrival = mine(source) * self.pair_cap + my_pair_rank
+        self.pair_slots = jnp.arange(blk_count * self.pair_cap, dtype=jnp.int32)
+
+    def slot_position(self):
+        return self.shard * self.pair_cap + self.pair_rank
+
+    def send_index(self):
+        key = jnp.where(
+            self.real & (self.holder == self.device) & (self.pair_rank < self.pair_cap),
+            self.slot_position(),
+            -1,
+        )
+        return locate(self.pair_slots, key, self.owner - self.first)
+
+    def compact_index(self):
+        wanted = jnp.arange(self.column_cap, dtype=jnp.int32)
+        return locate(wanted, jnp.where(self.held, self.my_rank, -1), self.arrival)
+
+    def send_home(self, tiles):
+        wanted = jnp.arange(self.column_count * self.column_cap, dtype=jnp.int32)
+        index = locate(wanted, self.place, jnp.arange(self.tiles, dtype=jnp.int32))
+        summed = lax.psum_scatter(
+            pick(tiles, index), COLUMN_AXES, scatter_dimension=0, tiled=True
+        )
+        back = locate(self.pair_slots, jnp.where(self.held, self.arrival, -1), self.my_rank)
+        return exchange(pick(summed, back), "blk")
 
 
 def rotate(values, positions, direction):
@@ -172,64 +259,19 @@
     )
     query_pos = blk_index * span_rows + jnp.arange(span_rows, dtype=jnp.int32)
     head_of = [member * heads_local // (QH // KVH) for member in range(uly_count)]
-    dp_index = lax.axis_index("dp")
-    my_device = (dp_index * blk_count + blk_index) * uly_count + uly_index
-    my_column = dp_index * uly_count + uly_index
-    column_count = lax.axis_size("dp") * uly_count
     shard_groups = -(-GRID_FF // blk_count)
-    shard_tiles = 3 * GRID_D * shard_groups
-    pair_cap = capacity(shard_tiles / all_count, 3.5, slot_local)
-    column_cap = capacity(shard_tiles / column_count, 3.45, shard_tiles)
+    shard_rows = -(-GRID_D // blk_count)
     attn_cap = capacity(ATTN_TILES / all_count, 3.8, slot_local)
-
-    owners = shard_owners(owner_slot, blk_count, shard_groups)
-    owner_flat = owners.reshape(-1)
-    real_flat = owner_flat >= 0
-    shard_flat = jnp.repeat(jnp.arange(blk_count, dtype=jnp.int32), shard_tiles)
-    device_flat = jnp.maximum(owner_flat, 0) // slot_local
-    column_flat = device_flat // (blk_count * uly_count) * uly_count + device_flat % uly_count
-    source_flat = device_flat // uly_count % blk_count
-    pair_flat = jnp.where(real_flat, device_flat * blk_count + shard_flat, -1)
-    line_flat = jnp.where(real_flat, column_flat * blk_count + shard_flat, -1)
-    pair_rank = earlier_equal(pair_flat)
-    line_rank = earlier_equal(line_flat)
+    route = Route(shard_owners(owner_slot, blk_count, shard_groups), slot_local, (3.5, 3.45))
+    attn_route = Route(attention_owners(owner_slot, blk_count, shard_rows), slot_local, (5.0, 3.8))
+    my_first = route.first
     attn_owner = owner_slot[:ATTN_TILES]
     attn_device = attn_owner // slot_local
     attn_rank = earlier_equal(attn_device)
-    fits_shards = (jnp.max(jnp.where(real_flat, pair_rank, 0)) < pair_cap) & (
-        jnp.max(jnp.where(real_flat, line_rank, 0)) < column_cap
-    )
     fits_attn = jnp.max(attn_rank) < attn_cap
-    my_first = my_device * slot_local
-
-    def mine(flat):
-        return lax.dynamic_slice_in_dim(flat, blk_index * shard_tiles, shard_tiles, 0)
-
-    my_real = mine(real_flat)
-    my_owner = mine(owner_flat)
-    my_source = mine(source_flat)
-    my_pair_rank = mine(pair_rank)
-    my_line_rank = mine(line_rank)
-    my_columns = mine(column_flat)
-    in_column = my_real & (my_columns == my_column)
-    place = jnp.where(my_real, my_columns * column_cap + my_line_rank, -1)
-    send_key = jnp.where(
-        real_flat & (device_flat == my_device) & (pair_rank < pair_cap),
-        shard_flat * pair_cap + pair_rank,
-        -1,
-    )
-    pair_slots = jnp.arange(blk_count * pair_cap, dtype=jnp.int32)
-    send_index = locate(pair_slots, send_key, owner_flat - my_first)
-    arrival = my_source * pair_cap + my_pair_rank
-    fits_pair = my_pair_rank < pair_cap
-    compact_index = locate(
-        jnp.arange(column_cap, dtype=jnp.int32),
-        jnp.where(in_column & fits_pair, my_line_rank, -1),
-        arrival,
-    )
     attn_send = locate(
         jnp.arange(attn_cap, dtype=jnp.int32),
-        jnp.where(attn_device == my_device, attn_rank, -1),
+        jnp.where(attn_device == route.device, attn_rank, -1),
         attn_owner - my_first,
     )
     attn_place = attn_device * attn_cap + attn_rank
@@ -244,10 +286,12 @@
     attn_tiles = lax.cond(
         fits_attn, lambda: pick(attn_buffer, attn_place), lambda: whole_tiles(attn_owner)
     )
-    arrived_tiles = exchange(pick(master_low, send_index), "blk")
-    shard_buffer = lax.all_gather(pick(arrived_tiles, compact_index), COLUMN_AXES, axis=0, tiled=True)
+    arrived_tiles = exchange(pick(master_low, route.send_index()), "blk")
+    shard_buffer = lax.all_gather(
+        pick(arrived_tiles, route.compact_index()), COLUMN_AXES, axis=0, tiled=True
+    )
     shard_stack = lax.cond(
-        fits_shards, lambda: pick(shard_buffer, place), lambda: whole_tiles(my_owner)
+        route.fits, lambda: pick(shard_buffer, route.place), lambda: whole_tiles(route.my_owner)
     )
     third = GRID_D * shard_groups
     real_groups = (
@@ -355,16 +399,7 @@
         ],
         axis=0,
     )
-    scatter_index = locate(
-        jnp.arange(column_count * column_cap, dtype=jnp.int32),
-        place,
-        jnp.arange(shard_tiles, dtype=jnp.int32),
-    )
-    column_grads = lax.psum_scatter(
-        pick(shard_grads, scatter_index), COLUMN_AXES, scatter_dimension=0, tiled=True
-    )
-    return_key = jnp.where(in_column & fits_pair, arrival, -1)
-    returned_grads = exchange(pick(column_grads, locate(pair_slots, return_key, my_line_rank)), "blk")
+    returned_grads = route.send_home(shard_grads)
     norm_part_two, gain_second_grad = norm_backward(
         middle, inverse_second, gain_second, grad_normed_two
     )
@@ -437,26 +472,25 @@
         ]
     )
     grad_small = exchange_sum(small_partial.reshape(all_count, -1), ALL_AXES)
+    grad_lines = spread(
+        jnp.concatenate([grad_query_lin, grad_key_lin, grad_value_lin], axis=1), "blk"
+    ).reshape(blk_count * token_count, QW + 2 * KVW)
+    middle_lines = spread(grad_middle_low, "blk").reshape(blk_count * token_count, D)
     attn_grads = jnp.concatenate(
         [
-            matrix_to_tiles(outer_product(normed, grad_query_lin)),
-            matrix_to_tiles(outer_product(normed, grad_key_lin)),
-            matrix_to_tiles(outer_product(normed, grad_value_lin)),
-            matrix_to_tiles(outer_product(out_rows, grad_middle_low)),
+            matrix_to_tiles(
+                outer_product(split_columns(normed, blk_count, shard_rows), grad_lines)
+            ),
+            matrix_to_tiles(
+                outer_product(split_columns(out_rows, blk_count, shard_rows), middle_lines)
+            ),
         ],
         axis=0,
     )
-    attn_index = locate(
-        jnp.arange(all_count * attn_cap, dtype=jnp.int32),
-        attn_place,
-        jnp.arange(ATTN_TILES, dtype=jnp.int32),
-    )
-    attn_returned = lax.psum_scatter(
-        pick(attn_grads, attn_index), ALL_AXES, scatter_dimension=0, tiled=True
-    )
+    attn_returned = attn_route.send_home(attn_grads)
     my_slots = my_first + jnp.arange(slot_local, dtype=jnp.int32)
-    slot_index = locate(my_slots, owner_flat, shard_flat * pair_cap + pair_rank) + locate(
-        my_slots, attn_owner, blk_count * pair_cap + attn_rank
+    slot_index = locate(my_slots, route.owner, route.slot_position()) + locate(
+        my_slots, attn_route.owner, blk_count * route.pair_cap + attn_route.slot_position()
     )
     slot_used = jnp.any(my_slots[:, None] == owner_slot[None, :], axis=1)
 
@@ -465,14 +499,14 @@
 
     def summed_grads():
         every_slot = jnp.arange(slot_total, dtype=jnp.int32)
-        tile_owner = jnp.concatenate([my_owner, attn_owner])
+        tile_owner = jnp.concatenate([route.my_owner, attn_route.my_owner])
         index = locate(every_slot, tile_owner, jnp.arange(tile_owner.shape[0], dtype=jnp.int32))
         held = jnp.any(every_slot[:, None] == tile_owner[None, :], axis=1)
         parts = pick(jnp.concatenate([shard_grads, attn_grads], axis=0), index)
         parts = jnp.where(held[:, None, None], parts, 0)
         return lax.psum_scatter(parts, ALL_AXES, scatter_dimension=0, tiled=True)
 
-    grad_slots = lax.cond(fits_shards & fits_attn, routed_grads, summed_grads)
+    grad_slots = lax.cond(route.fits & attn_route.fits, routed_grads, summed_grads)
     grad_slots = jnp.where(slot_used[:, None, None], grad_slots, 0).astype(jnp.float32)
     rotated = jnp.einsum("sji,sjk->sik", basis_left, grad_slots, precision=TOP_PRECISION)
     rotated = jnp.einsum("sik,skl->sil", rotated, basis_right, precision=TOP_PRECISION)

time: 1570 us -> 1380 us (0.88)
  waiting for transfers between devices: 846 us -> 605 us
  starting transfers between devices: 84.6 us -> 117 us
  other arithmetic: 94.8 us -> 112 us
    reduce_scatter x1, waiting for transfers between devices: 425 us -> 0.01 us  [send_home(): lax.psum_scatter(pick(tiles, index), COLUMN_AXES, scatter_dimension=0, ti...]
    unnamed x5, waiting for transfers between devices: 0.63 us -> 149 us
    all_to_all x12 -> x16, waiting for transfers between devices: 325 us -> 378 us  [exchange(): return lax.all_to_all(values, axes, split_axis=0, concat_axis=0, tiled=True)]
    all_to_all x12 -> x16, starting transfers between devices: 71.9 us -> 98.9 us  [exchange(): return lax.all_to_all(values, axes, split_axis=0, concat_axis=0, tiled=True)]
    reshape x7 -> x4, local copies, waits for them, and re-layouts: 59.5 us -> 43.1 us  [matrix_to_tiles(): blocked = matrix.reshape(row_tiles, BLOCK, col_tiles, BLOCK)]
    gather x9 -> x10, local copies, waits for them, and re-layouts: 129 us -> 118 us  [pick(): return jnp.take(table, index, axis=0, mode='clip')]
    transpose x7 -> x6, local copies, waits for them, and re-layouts: 39.4 us -> 29.3 us  [matrix_to_tiles(): blocked.transpose(0, 2, 1, 3).reshape(row_tiles * col_tiles, BLOCK, BLOCK)]
  transfers between devices with their start and end apart: 19 -> 24, of which waited for: 15 -> 17; matrix products, arithmetic and copies ran while one was open for 22% -> 33% of each run, Pallas kernels for 0% -> 0%
where the time goes in v3:
time: 1380 us; the launch traced here: 1360 us
  waiting for transfers between devices  605 us (44%)
  local copies, waits for them, and re-layouts  330 us (24%)
  matrix products  166 us (12%)
  starting transfers between devices  117 us (8%)
  other arithmetic  112 us (8%)
  between operations  20.4 us (1%)
    all_to_all x16, waiting for transfers between devices, exchange(): return lax.all_to_all(values, axes, split_axis=0, concat_axis=0, tiled=True)  378 us
    unnamed x5, waiting for transfers between devices  149 us
    gather x10, local copies, waits for them, and re-layouts, pick(): return jnp.take(table, index, axis=0, mode='clip')  118 us
    all_to_all x16, starting transfers between devices, exchange(): return lax.all_to_all(values, axes, split_axis=0, concat_axis=0, tiled=True)  98.9 us
    all_gather x1, waiting for transfers between devices, local(): lax.all_gather(pick(master_low, attn_send), ALL_AXES, axis=0, tiled=True)  60.7 us
    reshape x7, local copies, waits for them, and re-layouts, tiles_to_matrix(): blocked = tiles.reshape(row_tiles, col_tiles, BLOCK, BLOCK)  52.8 us
    reshape x4, local copies, waits for them, and re-layouts, matrix_to_tiles(): blocked = matrix.reshape(row_tiles, BLOCK, col_tiles, BLOCK)  43.1 us
    dot_general x7, matrix products, forward_product(): return jnp.dot(left_side, weight, preferred_element_type=jnp.float32)  42.8 us
  transfers between devices with their start and end apart: 24, of which 17 were waited for; matrix products, arithmetic and copies ran while one was open for 33% of the time, Pallas kernels for 0%

profile of v3, /device:TPU:10, one launch (start us, length us, event | category | flops | bytes accessed | tf_op | source)
XLA Modules:
  0.0 1360.9 jit_solution(4168939471320827143)
XLA Ops:
  43.4 141.9 %all-to-all-done.6 = bf16[144,128,128]{2,1,0:T(8,128)(2,1)} async-done(((bf16[144,128,128]{2,1,0:T(8,128)(2,1)}), bf16[144,128,128]{2,1,0:T(8,128)(2,1)}, u32[]{:S(2)}, u32[]{:S(2)}) %all-to-all-start.6) | async-done | bytes 4718624 | tf_op jit(solution)/shard_map/all_to_all | solution.py:79
  190.6 60.7 %all-gather.11.cloned.1.call-done = bf16[736,128,128]{2,1,0:T(8,128)(2,1)} async-done(((bf16[23,128,128]{2,1,0:T(8,128)(2,1)}), bf16[736,128,128]{2,1,0:T(8,128)(2,1)}) %all-gather.11.cloned.1.call-update) | async-done | bytes 24117264 | tf_op jit(solution)/shard_map/all_gather | solution.py:281
  251.4 21.5 %conditional.3 = (bf16[336,128,128]{2,1,0:T(8,128)(2,1)}) conditional(s32[]{:T(128)} %convert_element_type.255, (bf16[90,128,128]{2,1,0:T(8,128)(2,1)}, s32[336]{0:T(512)S(1)}) %tuple.28, (s32[336]{0:T(512)S(1)}, s32[336]{0:T(512)S(1)}, bf16[736,128,128]{2,1,0:T(8,128)(2,1)}) %tuple.29), branch_computations={%region_4.5_spmd, %region_5.6_spmd} | conditional | flops 1696 | bytes 313989824 | solution.py:286
  254.2 18.7 %gather_fusion = bf16[336,128,128]{2,1,0:T(8,128)(2,1)} fusion(bf16[736,128,128]{2,1,0:T(8,128)(2,1)} %get-tuple-element.99, s32[1024]{0:T(1024)S(1)} %pad_clamp_fusion.1), kind=kCustom, calls=%fused_computation.1 | custom fusion | bytes 22021440 | tf_op jit(solution)/shard_map/cond/branch_1_fun/jit(_take)/gather | solution.py:53
  350.8 14.4 %all-to-all-done.3 = bf16[4,2,4,64,256]{4,3,2,1,0:T(8,128)(2,1)S(1)} async-done(((bf16[4,2,4,64,256]{4,3,2,1,0:T(8,128)(2,1)}), bf16[4,2,4,64,256]{4,3,2,1,0:T(8,128)(2,1)S(1)}, u32[]{:S(2)}, u32[]{:S(2)}) %all-to-all-start.3) | async-done | bytes 1048608 | tf_op jit(solution)/shard_map/all_to_all | solution.py:79
  426.6 27.8 %conditional.4 = (bf16[648,128,128]{2,1,0:T(8,128)(2,1)}) conditional(s32[]{:T(128)} %convert_element_type.268, (bf16[90,128,128]{2,1,0:T(8,128)(2,1)}, s32[648]{0:T(1024)S(1)}) %tuple.115, (s32[648]{0:T(1024)S(1)}, bf16[904,128,128]{2,1,0:T(8,128)(2,1)}) %tuple.31), branch_computations={%region_15.16_spmd, %region_16.17_spmd} | conditional | flops 1024 | bytes 334439552 | solution.py:293
  426.8 27.5 %gather_fusion.1 = bf16[648,128,128]{2,1,0:T(8,128)(2,1)} fusion(bf16[904,128,128]{2,1,0:T(8,128)(2,1)} %get-tuple-element.104, s32[1024]{0:T(1024)S(1)} %pad_clamp_fusion.3), kind=kCustom, calls=%fused_computation.3 | custom fusion | bytes 42469920 | tf_op jit(solution)/shard_map/cond/branch_1_fun/jit(_take)/gather | solution.py:53
  454.4 14.1 %fusion.132 = (bf16[216,128,128]{2,1,0:T(8,128)(2,1)}, bf16[216,128,128]{2,1,0:T(8,128)(2,1)}, bf16[216,128,128]{2,1,0:T(8,128)(2,1)}) fusion(bf16[648,128,128]{2,1,0:T(8,128)(2,1)} %get-tuple-element.231), kind=kLoop, calls=%fused_computation.350 | loop fusion | bytes 42467328 | tf_op jit(solution)/shard_map/slice | solution.py:308
  522.4 17.4 %bitcast_select_fusion.2 = (bf16[12,128,18,128]{3,2,1,0:T(8,128)(2,1)}, bf16[12,128,18,128]{3,2,1,0:T(8,128)(2,1)}) fusion(pred[18]{0:T(512)(128)(4,1)S(1)} %copy-done.50, bf16[12,18,128,128]{3,2,1,0:T(8,128)(2,1)} %bitcast.285, bf16[12,18,128,128]{3,2,1,0:T(8,128)(2,1)} %bitcast.283), kind=kLoop, calls=%fused_computation.44 | loop fusion | flops 7077888 | bytes 28311570 | tf_op jit(solution)/shard_map/jit(_where)/select_n | solution.py:301
  550.1 14.8 %multiply_convert_fusion.2 = (bf16[512,2304]{1,0:T(8,128)(2,1)S(1)}, bf16[512,2304]{1,0:T(8,128)(2,1)}, bf16[512,2304]{1,0:T(8,128)(2,1)}) fusion(f32[512,2304]{1,0:T(8,128)} %fusion.8, f32[512,2304]{1,0:T(8,128)} %fusion.13, bf16[512,1536]{1,0:T(8,128)(2,1)} %bitcast.24, bf16[192,8,18,128]{3,2,1,0:T(8,128)(2,1)} %bitcast.300), kind=kOutput, calls=%fused_computation.88 | convolution fusion | flops 3642753024 | bytes 25165824 | tf_op jit(solution)/shard_map/dot_general | solution.py:210
  585.6 12.8 copy.321
  632.1 28.1 %all-to-all-done.7 = bf16[4,128,1536]{2,1,0:T(8,128)(2,1)} async-done(((bf16[4,128,1536]{2,1,0:T(8,128)(2,1)}), bf16[4,128,1536]{2,1,0:T(8,128)(2,1)}, u32[]{:S(2)}, u32[]{:S(2)}) %all-to-all-start.7) | async-done | bytes 1572896 | tf_op jit(solution)/shard_map/all_to_all | solution.py:79
  733.6 16.6 %all-to-all-done.12 = bf16[4,2,256,256]{3,2,1,0:T(8,128)(2,1)S(1)} async-done(((bf16[4,2,256,256]{3,2,1,0:T(8,128)(2,1)}), bf16[4,2,256,256]{3,2,1,0:T(8,128)(2,1)S(1)}, u32[]{:S(2)}, u32[]{:S(2)}) %all-to-all-start.12) | async-done | bytes 1048608 | tf_op jit(solution)/shard_map/all_to_all | solution.py:79
  780.2 26.3 %all-to-all-done.17 = bf16[4,128,1536]{2,1,0:T(8,128)(2,1)S(1)} async-done(((bf16[4,128,1536]{2,1,0:T(8,128)(2,1)}), bf16[4,128,1536]{2,1,0:T(8,128)(2,1)S(1)}, u32[]{:S(2)}, u32[]{:S(2)}) %all-to-all-start.17) | async-done | bytes 1572896 | tf_op jit(solution)/shard_map/all_to_all | solution.py:79
  826.8 33.5 %all-to-all-done.15 = bf16[4,128,2048]{2,1,0:T(8,128)(2,1)} async-done(((bf16[4,128,2048]{2,1,0:T(8,128)(2,1)}), bf16[4,128,2048]{2,1,0:T(8,128)(2,1)}, u32[]{:S(2)}, u32[]{:S(2)}) %all-to-all-start.15) | async-done | bytes 2097184 | tf_op jit(solution)/shard_map/all_to_all | solution.py:79
  882.2 14.4 %reshape.1012 = bf16[18,128,12,128]{3,2,1,0:T(8,128)(2,1)} reshape(bf16[2304,1536]{1,0:T(8,128)(2,1)} %convolution_convert_fusion) | data formatting | bytes 14155776 | tf_op jit(solution)/shard_map/reshape | solution.py:74
  914.1 13.1 reshape.1010
  943.9 13.1 reshape.1008
  965.6 15.7 %pad_maximum_fusion.2 = bf16[648,128,128]{2,1,0:T(8,128)(2,1)} fusion(bf16[216,128,128]{2,1,0:T(8,128)(2,1)} %bitcast.289, bf16[216,128,128]{2,1,0:T(8,128)(2,1)} %bitcast.290, bf16[216,128,128]{2,1,0:T(8,128)(2,1)} %bitcast.291), kind=kLoop, calls=%fused_computation.38 | loop fusion | flops 21233664 | bytes 42467328 | tf_op jit(solution)/shard_map/concatenate | solution.py:394
  981.3 26.9 %gather_fusion.9 = bf16[904,128,128]{2,1,0:T(8,128)(2,1)} fusion(bf16[648,128,128]{2,1,0:T(8,128)(2,1)} %pad_maximum_fusion.2, s32[1024]{0:T(1024)S(1)} %pad_clamp_fusion.9), kind=kCustom, calls=%fused_computation.9 | custom fusion | bytes 59248160 | tf_op jit(solution)/shard_map/jit(_take)/gather | solution.py:53
  1042.5 148.7 %reduce-scatter.12.cloned.1.call-done = bf16[113,128,128]{2,1,0:T(8,128)(2,1)} async-done(((bf16[904,128,128]{2,1,0:T(8,128)(2,1)}), bf16[113,128,128]{2,1,0:T(8,128)(2,1)}) %reduce-scatter.12.cloned.1.call-update) | async-done | bytes 3702800
  1213.2 94.5 %all-to-all-done.18 = bf16[144,128,128]{2,1,0:T(8,128)(2,1)} async-done(((bf16[144,128,128]{2,1,0:T(8,128)(2,1)}), bf16[144,128,128]{2,1,0:T(8,128)(2,1)}, u32[]{:S(2)}, u32[]{:S(2)}) %all-to-all-start.18) | async-done | bytes 4718624 | tf_op jit(solution)/shard_map/all_to_all | solution.py:79
  1320.2 16.1 %fusion.22 = (f32[90,128,128]{2,1,0:T(8,128)}, f32[90,128,128]{2,1,0:T(8,128)}) fusion(f32[90,128,128]{2,1,0:T(8,128)} %param.24, f32[90,128,128]{2,1,0:T(8,128)} %param.23, f32[90,128,128]{2,1,0:T(8,128)} %param.26, f32[90,128,128]{2,1,0:T(8,128)} %param.25, bf16[90,128,128]{2,1,0:T(8,128)(2,1)} %get-tuple-element.232, pred[90]{0:T(512)(128)(4,1)S(1)} %copy-done.61), kind=kOutput, calls=%fused_computation.71 | convolution fusion | flops 765296640 | bytes 38338648 | tf_op jit(solution)/shard_map/sik,skl->sil/dot_general | solution.py:512
  1336.3 16.8 %multiply_subtract_fusion = f32[90,128,128]{2,1,0:T(8,128)} fusion(f32[90,128,128]{2,1,0:T(8,128)} %param.22, f32[90]{0:T(128)S(1)} %copy-done.67, f32[90,128,128]{2,1,0:T(8,128)} %param.26, f32[90,128,128]{2,1,0:T(8,128)} %param.25, f32[90,128,128]{2,1,0:T(8,128)} %get-tuple-element.177, f32[90,128,128]{2,1,0:T(8,128)} %get-tuple-element.176), kind=kOutput, calls=%fused_computation.72 | convolution fusion | flops 763822080 | bytes 35389800 | tf_op jit(solution)/shard_map/sik,slk->sil/dot_general | solution.py:517
  (427 shorter events, 563.3 us)
Async XLA Ops:
  8.0 243.3 %all-gather.11.cloned.1.call-start = ((), (), s32[]{:S(2)}) async-start(), calls=%async_computation.28 | async-start | bytes 24870912 | tf_op jit(solution)/shard_map/all_gather | solution.py:281
  33.4 151.9 %all-to-all-start.6 = ((bf16[144,128,128]{2,1,0:T(8,128)(2,1)}), bf16[144,128,128]{2,1,0:T(8,128)(2,1)}, u32[]{:S(2)}, u32[]{:S(2)}) async-start(bf16[144,128,128]{2,1,0:T(8,128)(2,1)} %gather_fusion.7), calls=%async_computation.7 | async-start | bytes 9437184 | tf_op jit(solution)/shard_map/all_to_all | solution.py:79
  272.9 153.7 %all-gather.13.cloned.1.call-start = ((), (), s32[]{:S(2)}) async-start(), calls=%async_computation.29 | async-start | bytes 33325056 | tf_op jit(solution)/shard_map/all_gather | solution.py:290
  274.1 10.3 all-to-all-start
  314.5 14.2 %all-to-all-start.2 = ((bf16[4,2,64,256]{3,2,1,0:T(8,128)(2,1)}), bf16[4,2,64,256]{3,2,1,0:T(8,128)(2,1)}, u32[]{:S(2)}, u32[]{:S(2)}) async-start(bf16[4,2,64,256]{3,2,1,0:T(8,128)(2,1)} %pad_maximum_fusion.7), calls=%async_computation.3 | async-start | bytes 524288 | tf_op jit(solution)/shard_map/all_to_all | solution.py:79
  328.7 9.5 all-to-all-start.1
  339.4 25.8 %all-to-all-start.3 = ((bf16[4,2,4,64,256]{4,3,2,1,0:T(8,128)(2,1)}), bf16[4,2,4,64,256]{4,3,2,1,0:T(8,128)(2,1)S(1)}, u32[]{:S(2)}, u32[]{:S(2)}) async-start(bf16[4,2,4,64,256]{4,3,2,1,0:T(8,128)(2,1)} %broadcast_in_dim.430), calls=%async_computation.4 | async-start | bytes 2097152 | tf_op jit(solution)/shard_map/all_to_all | solution.py:79
  379.8 17.1 %all-to-all-start.4 = ((bf16[2,256,3,128]{3,0,2,1:T(2,128)(2,1)}), bf16[2,256,3,128]{3,0,2,1:T(2,128)(2,1)}, u32[]{:S(2)}, u32[]{:S(2)}) async-start(bf16[2,256,3,128]{3,0,2,1:T(2,128)(2,1)} %copy.313), calls=%async_computation.5 | async-start | bytes 786432 | tf_op jit(solution)/shard_map/all_to_all | solution.py:368
  399.2 80.2 %all-to-all-start.8 = ((bf16[4,128,1536]{2,1,0:T(8,128)(2,1)}), bf16[4,128,1536]{2,1,0:T(8,128)(2,1)}, u32[]{:S(2)}, u32[]{:S(2)}) async-start(bf16[4,128,1536]{2,1,0:T(8,128)(2,1)} %broadcast_in_dim.448), calls=%async_computation.9 | async-start | bytes 3145728 | tf_op jit(solution)/shard_map/all_to_all | solution.py:79
  481.7 58.1 %all-to-all-start.5 = ((bf16[4,128,1536]{2,1,0:T(8,128)(2,1)}), bf16[4,128,1536]{2,1,0:T(8,128)(2,1)}, u32[]{:S(2)}, u32[]{:S(2)}) async-start(bf16[4,128,1536]{2,1,0:T(8,128)(2,1)} %broadcast_in_dim.433), calls=%async_computation.6 | async-start | bytes 3145728 | tf_op jit(solution)/shard_map/all_to_all | solution.py:79
  580.5 38.6 %all-to-all-start.9 = ((bf16[4,128,1536]{2,1,0:T(8,128)(2,1)}), bf16[4,128,1536]{2,1,0:T(8,128)(2,1)}, u32[]{:S(2)}, u32[]{:S(2)}) async-start(bf16[4,128,1536]{2,1,0:T(8,128)(2,1)} %bitcast.331), calls=%async_computation.10 | async-start | bytes 3145728 | tf_op jit(solution)/shard_map/all_to_all | solution.py:79
  619.1 41.1 %all-to-all-start.7 = ((bf16[4,128,1536]{2,1,0:T(8,128)(2,1)}), bf16[4,128,1536]{2,1,0:T(8,128)(2,1)}, u32[]{:S(2)}, u32[]{:S(2)}) async-start(bf16[4,128,1536]{2,1,0:T(8,128)(2,1)} %bitcast.330), calls=%async_computation.8 | async-start | bytes 3145728 | tf_op jit(solution)/shard_map/all_to_all | solution.py:79
  674.9 17.3 %all-to-all-start.10 = ((bf16[2,64,12,128]{3,1,0,2:T(8,128)(2,1)}), bf16[2,64,12,128]{3,1,0,2:T(8,128)(2,1)}, u32[]{:S(2)}, u32[]{:S(2)}) async-start(bf16[2,64,12,128]{3,1,0,2:T(8,128)(2,1)} %copy.322), calls=%async_computation.11 | async-start | bytes 786432 | tf_op jit(solution)/shard_map/all_to_all | solution.py:413
  692.2 18.3 %all-to-all-start.14 = ((bf16[4,128,384]{1,2,0:T(8,128)(2,1)}), bf16[4,128,384]{1,2,0:T(8,128)(2,1)}, u32[]{:S(2)}, u32[]{:S(2)}) async-start(bf16[4,128,384]{1,2,0:T(8,128)(2,1)} %fusion.93), calls=%async_computation.15 | async-start | bytes 786432 | tf_op jit(solution)/shard_map/all_to_all | solution.py:79
  710.5 13.1 all-to-all-start.16
  723.7 26.6 %all-to-all-start.12 = ((bf16[4,2,256,256]{3,2,1,0:T(8,128)(2,1)}), bf16[4,2,256,256]{3,2,1,0:T(8,128)(2,1)S(1)}, u32[]{:S(2)}, u32[]{:S(2)}) async-start(bf16[4,2,256,256]{3,2,1,0:T(8,128)(2,1)} %copy_bitcast_fusion), calls=%async_computation.13 | async-start | bytes 2097152 | tf_op jit(solution)/shard_map/all_to_all | solution.py:79
  750.3 9.5 all-to-all-start.11
  768.8 37.7 %all-to-all-start.17 = ((bf16[4,128,1536]{2,1,0:T(8,128)(2,1)}), bf16[4,128,1536]{2,1,0:T(8,128)(2,1)S(1)}, u32[]{:S(2)}, u32[]{:S(2)}) async-start(bf16[4,128,1536]{2,1,0:T(8,128)(2,1)} %broadcast_in_dim.456), calls=%async_computation.18 | async-start | bytes 3145728 | tf_op jit(solution)/shard_map/all_to_all | solution.py:79
  808.1 52.2 %all-to-all-start.15 = ((bf16[4,128,2048]{2,1,0:T(8,128)(2,1)}), bf16[4,128,2048]{2,1,0:T(8,128)(2,1)}, u32[]{:S(2)}, u32[]{:S(2)}) async-start(bf16[4,128,2048]{2,1,0:T(8,128)(2,1)} %broadcast_in_dim.455), calls=%async_computation.16 | async-start | bytes 4194304 | tf_op jit(solution)/shard_map/all_to_all | solution.py:79
  815.8 216.1 %reduce-scatter.10.cloned.1.call-start = ((), (), s32[]{:S(2)}) async-start(), calls=%async_computation.27 | async-start | bytes 6782976 | tf_op jit(solution)/shard_map/reduce_scatter | solution.py:188
  872.7 318.5 %reduce-scatter.12.cloned.1.call-start = ((), (), s32[]{:S(2)}) async-start(), calls=%async_computation.30 | async-start | bytes 33325056
  1024.6 11.9 all-to-all-start.20
  1036.5 164.4 %all-to-all-start.19 = ((bf16[44,128,128]{2,1,0:T(8,128)(2,1)}), bf16[44,128,128]{2,1,0:T(8,128)(2,1)}, u32[]{:S(2)}, u32[]{:S(2)}) async-start(bf16[44,128,128]{2,1,0:T(8,128)(2,1)} %gather_fusion.12), calls=%async_computation.21 | async-start | bytes 2883584 | tf_op jit(solution)/shard_map/all_to_all | solution.py:79
  1201.0 106.8 %all-to-all-start.18 = ((bf16[144,128,128]{2,1,0:T(8,128)(2,1)}), bf16[144,128,128]{2,1,0:T(8,128)(2,1)}, u32[]{:S(2)}, u32[]{:S(2)}) async-start(bf16[144,128,128]{2,1,0:T(8,128)(2,1)} %gather_fusion.10), calls=%async_computation.19 | async-start | bytes 9437184 | tf_op jit(solution)/shard_map/all_to_all | solution.py:79
  (75 other events, 1913.7 us)
Sparse Core Ops, SparseCore 0:
  20.4 230.8 all-gather.10
Sparse Core Ops, SparseCore 1:
  275.8 150.7 all-gather.12
  872.8 61.0 reduce-scatter.9
  1008.4 182.8 reduce-scatter.11

commit v4 on v3

--- a/solution.py
+++ b/solution.py
@@ -4,6 +4,8 @@
 import jax.numpy as jnp
 import numpy as np
 from jax import lax
+from jax.experimental import pallas as pl
+from jax.experimental.pallas import tpu as pltpu
 from jax.sharding import PartitionSpec as P
 
 D = 1536
@@ -88,21 +90,143 @@
     return jnp.sum(exchange(values, axes).astype(jnp.float32), axis=0)
 
 
+STEP_GROUPS = 2
+STEP_TILES = 3 * STEP_GROUPS * GRID_D
+STEP_COLUMNS = STEP_GROUPS * BLOCK
+ROW_CHUNK = 512
+
+
 def shard_owners(owner_slot, shard_count, shard_groups):
-    padded = shard_count * shard_groups
+    missing = shard_count * shard_groups - GRID_FF
     first = ATTN_TILES
     members = []
-    for _ in range(2):
-        grid = owner_slot[first : first + GRID_D * GRID_FF].reshape(GRID_D, GRID_FF)
-        grid = jnp.pad(grid, ((0, 0), (0, padded - GRID_FF)), constant_values=-1)
+    for number in range(3):
+        grid = owner_slot[first : first + GRID_D * GRID_FF]
+        if number < 2:
+            grid = grid.reshape(GRID_D, GRID_FF).transpose(1, 0)
+        else:
+            grid = grid.reshape(GRID_FF, GRID_D)
+        grid = jnp.pad(grid, ((0, missing), (0, 0)), constant_values=-1)
         members.append(
-            grid.reshape(GRID_D, shard_count, shard_groups).transpose(1, 0, 2).reshape(shard_count, -1)
+            grid.reshape(shard_count, shard_groups // STEP_GROUPS, STEP_GROUPS * GRID_D)
         )
         first = first + GRID_D * GRID_FF
-    grid = owner_slot[first : first + GRID_D * GRID_FF].reshape(GRID_FF, GRID_D)
-    grid = jnp.pad(grid, ((0, padded - GRID_FF), (0, 0)), constant_values=-1)
-    members.append(grid.reshape(shard_count, -1))
-    return jnp.concatenate(members, axis=1)
+    return jnp.stack(members, axis=2).reshape(shard_count, -1)
+
+
+def mix_kernel(first_ref, x_ref, xt_ref, seed_ref, w_ref, tiles_ref, grad_ref, mixed_ref, acc_grad, acc_mixed):
+    step = pl.program_id(0)
+    kind = STEP_GROUPS * GRID_D
+
+    @pl.when(step == 0)
+    def _():
+        acc_grad[...] = jnp.zeros_like(acc_grad)
+        acc_mixed[...] = jnp.zeros_like(acc_mixed)
+
+    def tall(first):
+        return jnp.concatenate(
+            [
+                w_ref[first + group * GRID_D : first + (group + 1) * GRID_D].reshape(D, BLOCK)
+                for group in range(STEP_GROUPS)
+            ],
+            axis=1,
+        )
+
+    def product(left, right, dims):
+        return lax.dot_general(left, right, (dims, ((), ())), preferred_element_type=jnp.float32)
+
+    w_gate = tall(0)
+    w_up = tall(kind)
+    w_down = jnp.concatenate(
+        [
+            jnp.concatenate(
+                [w_ref[2 * kind + group * GRID_D + col] for col in range(GRID_D)], axis=1
+            )
+            for group in range(STEP_GROUPS)
+        ],
+        axis=0,
+    )
+    rows = x_ref.shape[0]
+    real_columns = (GRID_FF - first_ref[0] - step * STEP_GROUPS) * BLOCK
+    real = lax.broadcasted_iota(jnp.int32, (rows, STEP_COLUMNS), 1) < real_columns
+    x = x_ref[...]
+    seed = seed_ref[...]
+    gate = product(x, w_gate, ((1,), (0,)))
+    upward = product(x, w_up, ((1,), (0,)))
+    grad_hidden = product(seed, w_down, ((1,), (1,)))
+    sig = 1.0 / (1.0 + jnp.exp(-gate))
+    silu = gate * sig
+    hidden = jnp.where(real, silu * upward, 0.0).astype(jnp.bfloat16)
+    grad_gate = jnp.where(
+        real, grad_hidden * upward * sig * (1.0 + gate * (1.0 - sig)), 0.0
+    ).astype(jnp.bfloat16)
+    grad_up = jnp.where(real, grad_hidden * silu, 0.0).astype(jnp.bfloat16)
+    acc_grad[...] += product(grad_gate, w_gate, ((1,), (1,))) + product(
+        grad_up, w_up, ((1,), (1,))
+    )
+    acc_mixed[...] += product(hidden, w_down, ((1,), (0,)))
+    xt = xt_ref[...]
+    for number, right in ((0, grad_gate), (1, grad_up)):
+        part = product(xt, right, ((1,), (0,))).astype(jnp.bfloat16)
+        for group in range(STEP_GROUPS):
+            first = number * kind + group * GRID_D
+            tiles_ref[first : first + GRID_D] = part[
+                :, group * BLOCK : (group + 1) * BLOCK
+            ].reshape(GRID_D, BLOCK, BLOCK)
+    part = product(hidden, seed, ((0,), (0,))).astype(jnp.bfloat16)
+    for group in range(STEP_GROUPS):
+        for col in range(GRID_D):
+            tiles_ref[2 * kind + group * GRID_D + col] = part[
+                group * BLOCK : (group + 1) * BLOCK, col * BLOCK : (col + 1) * BLOCK
+            ]
+
+    @pl.when(step == pl.num_programs(0) - 1)
+    def _():
+        grad_ref[...] = acc_grad[...].astype(grad_ref.dtype)
+        mixed_ref[...] = acc_mixed[...].astype(mixed_ref.dtype)
+
+
+def mix_chunk(first_group, x, seed, stack):
+    rows = x.shape[0]
+    steps = stack.shape[0] // STEP_TILES
+
+    def fixed(shape):
+        return pl.BlockSpec(shape, lambda step, first: (0,) * len(shape))
+
+    tiles = pl.BlockSpec((STEP_TILES, BLOCK, BLOCK), lambda step, first: (step, 0, 0))
+    return pl.pallas_call(
+        mix_kernel,
+        out_shape=(
+            jax.ShapeDtypeStruct(stack.shape, jnp.bfloat16),
+            jax.ShapeDtypeStruct((rows, D), jnp.bfloat16),
+            jax.ShapeDtypeStruct((rows, D), jnp.bfloat16),
+        ),
+        grid_spec=pltpu.PrefetchScalarGridSpec(
+            num_scalar_prefetch=1,
+            grid=(steps,),
+            in_specs=[fixed((rows, D)), fixed((D, rows)), fixed((rows, D)), tiles],
+            out_specs=(tiles, fixed((rows, D)), fixed((rows, D))),
+            scratch_shapes=[pltpu.VMEM((rows, D), jnp.float32), pltpu.VMEM((rows, D), jnp.float32)],
+        ),
+        compiler_params=pltpu.CompilerParams(
+            dimension_semantics=("arbitrary",), vmem_limit_bytes=56 * 1024 * 1024
+        ),
+    )(first_group, x, x.T, seed, stack)
+
+
+def mix_lines(first_group, x, seed, stack):
+    parts = []
+    for first in range(0, x.shape[0], ROW_CHUNK):
+        last = min(first + ROW_CHUNK, x.shape[0])
+        parts.append(mix_chunk(first_group, x[first:last], seed[first:last], stack))
+    if len(parts) == 1:
+        return parts[0]
+    tiles = sum(part[0].astype(jnp.float32) for part in parts).astype(jnp.bfloat16)
+    return (
+        tiles,
+        jnp.concatenate([part[1] for part in parts], axis=0),
+        jnp.concatenate([part[2] for part in parts], axis=0),
+    )
 
 
 def attention_owners(owner_slot, shard_count, shard_rows):
@@ -182,12 +306,13 @@
         wanted = jnp.arange(self.column_cap, dtype=jnp.int32)
         return locate(wanted, jnp.where(self.held, self.my_rank, -1), self.arrival)
 
-    def send_home(self, tiles):
+    def home_buffer(self, tiles):
         wanted = jnp.arange(self.column_count * self.column_cap, dtype=jnp.int32)
         index = locate(wanted, self.place, jnp.arange(self.tiles, dtype=jnp.int32))
-        summed = lax.psum_scatter(
-            pick(tiles, index), COLUMN_AXES, scatter_dimension=0, tiled=True
-        )
+        return pick(tiles, index)
+
+    def send_home(self, buffer):
+        summed = lax.psum_scatter(buffer, COLUMN_AXES, scatter_dimension=0, tiled=True)
         back = locate(self.pair_slots, jnp.where(self.held, self.arrival, -1), self.my_rank)
         return exchange(pick(summed, back), "blk")
 
@@ -259,7 +384,7 @@
     )
     query_pos = blk_index * span_rows + jnp.arange(span_rows, dtype=jnp.int32)
     head_of = [member * heads_local // (QH // KVH) for member in range(uly_count)]
-    shard_groups = -(-GRID_FF // blk_count)
+    shard_groups = -(-GRID_FF // (blk_count * STEP_GROUPS)) * STEP_GROUPS
     shard_rows = -(-GRID_D // blk_count)
     attn_cap = capacity(ATTN_TILES / all_count, 3.8, slot_local)
     route = Route(shard_owners(owner_slot, blk_count, shard_groups), slot_local, (3.5, 3.45))
@@ -292,20 +417,6 @@
     )
     shard_stack = lax.cond(
         route.fits, lambda: pick(shard_buffer, route.place), lambda: whole_tiles(route.my_owner)
-    )
-    third = GRID_D * shard_groups
-    real_groups = (
-        blk_index * shard_groups + jnp.arange(shard_groups, dtype=jnp.int32)
-    ) < GRID_FF
-    real_hidden = jnp.repeat(real_groups, BLOCK)
-    w_gate = jnp.where(
-        real_hidden[None, :], tiles_to_matrix(shard_stack[:third], GRID_D, shard_groups), 0
-    )
-    w_up = jnp.where(
-        real_hidden[None, :], tiles_to_matrix(shard_stack[third : 2 * third], GRID_D, shard_groups), 0
-    )
-    w_down = jnp.where(
-        real_hidden[:, None], tiles_to_matrix(shard_stack[2 * third :], shard_groups, GRID_D), 0
     )
     attn_matrices = []
     first = 0
@@ -372,34 +483,14 @@
     inverse_second = lax.rsqrt(jnp.mean(middle * middle, axis=-1, keepdims=True) + NORM_EPS)
     normed_two = (middle * inverse_second * gain_second).astype(jnp.bfloat16)
     normed_line = spread(normed_two, "blk").reshape(blk_count * token_count, D)
-    gate_lin = forward_product(normed_line, w_gate)
-    upward = forward_product(normed_line, w_up)
-    hidden = (jax.nn.silu(gate_lin) * upward).astype(jnp.bfloat16)
-    grad_hidden = back_product(seed_line, w_down)
-    gate_sigmoid = jax.nn.sigmoid(gate_lin)
-    grad_gate = (
-        grad_hidden * upward * gate_sigmoid * (1.0 + gate_lin * (1.0 - gate_sigmoid))
-    ).astype(jnp.bfloat16)
-    grad_up = (grad_hidden * gate_lin * gate_sigmoid).astype(jnp.bfloat16)
-    grad_line = back_product(grad_gate, w_gate) + back_product(grad_up, w_up)
-    grad_normed_two = exchange_sum(
-        grad_line.astype(jnp.bfloat16).reshape(blk_count, token_count, D), "blk"
-    )
-    mixed_line = forward_product(hidden, w_down).astype(jnp.bfloat16)
-    mixed_out = (
-        (middle + exchange_sum(mixed_line.reshape(blk_count, token_count, D), "blk"))
-        .astype(jnp.bfloat16)
-        .reshape(seq_count, rows_local, D)
-    )
-    shard_grads = jnp.concatenate(
-        [
-            matrix_to_tiles(outer_product(normed_line, grad_gate)),
-            matrix_to_tiles(outer_product(normed_line, grad_up)),
-            matrix_to_tiles(outer_product(hidden, seed_line)),
-        ],
-        axis=0,
-    )
-    returned_grads = route.send_home(shard_grads)
+    first_group = jnp.full((1,), blk_index * shard_groups, jnp.int32)
+    shard_grads, grad_line, mixed_line = mix_lines(
+        first_group, normed_line, seed_line, shard_stack
+    )
+    grad_normed_two = exchange_sum(grad_line.reshape(blk_count, token_count, D), "blk")
+    home_buffer = route.home_buffer(shard_grads)
+    grad_normed_two, home_buffer = lax.optimization_barrier((grad_normed_two, home_buffer))
+    returned_grads = route.send_home(home_buffer)
     norm_part_two, gain_second_grad = norm_backward(
         middle, inverse_second, gain_second, grad_normed_two
     )
@@ -411,6 +502,12 @@
         .reshape(seq_count, rows_local, QH, HD)
     )
     grad_heads = lax.all_to_all(grad_out_rows, "uly", split_axis=2, concat_axis=1, tiled=True)
+    mixed_line, grad_heads = lax.optimization_barrier((mixed_line, grad_heads))
+    mixed_out = (
+        (middle + exchange_sum(mixed_line.reshape(blk_count, token_count, D), "blk"))
+        .astype(jnp.bfloat16)
+        .reshape(seq_count, rows_local, D)
+    )
     grad_heads_wide = grad_heads.astype(jnp.float32)
     row_delta = jnp.sum(grad_heads_wide * attended, axis=-1)
 
@@ -487,7 +584,7 @@
         ],
         axis=0,
     )
-    attn_returned = attn_route.send_home(attn_grads)
+    attn_returned = attn_route.send_home(attn_route.home_buffer(attn_grads))
     my_slots = my_first + jnp.arange(slot_local, dtype=jnp.int32)
     slot_index = locate(my_slots, route.owner, route.slot_position()) + locate(
         my_slots, attn_route.owner, blk_count * route.pair_cap + attn_route.slot_position()

time: 1380 us -> 1230 us (0.89)
  local copies, waits for them, and re-layouts: 330 us -> 212 us
  matrix products: 166 us -> 77.3 us
  Pallas kernels: 0 us -> 48.4 us
  waiting for transfers between devices: 605 us -> 652 us
  other arithmetic: 112 us -> 65.1 us
    pallas_call x0 -> x1, Pallas kernels: none -> 48.4 us  [mix_chunk(): pl.pallas_call(mix_kernel, out_shape=(jax.ShapeDtypeStruct(stack.shape, j...]
    reshape x4 -> x1, local copies, waits for them, and re-layouts: 43.1 us -> 2.51 us  [matrix_to_tiles(): blocked = matrix.reshape(row_tiles, BLOCK, col_tiles, BLOCK)]
    reshape x7 -> x4, local copies, waits for them, and re-layouts: 52.8 us -> 13.9 us  [tiles_to_matrix(): blocked = tiles.reshape(row_tiles, col_tiles, BLOCK, BLOCK)]
    dot_general x7 -> x4, matrix products: 42.8 us -> 5.56 us  [forward_product(): return jnp.dot(left_side, weight, preferred_element_type=jnp.float32)]
    reduce_scatter x1, waiting for transfers between devices: 0.01 us -> 29.8 us  [send_home(): lax.psum_scatter(buffer, COLUMN_AXES, scatter_dimension=0, tiled=True)]
    select_n x2 -> x0, other arithmetic: 28.3 us -> none  [the longest x1 17.4 us: local(): jnp.where(real_hidden[None, :], tiles_to_matrix(shard_stack[:third], GRID...]
    transpose x6 -> x3, local copies, waits for them, and re-layouts: 29.3 us -> 2 us  [matrix_to_tiles(): blocked.transpose(0, 2, 1, 3).reshape(row_tiles * col_tiles, BLOCK, BLOCK)]
    dot_general x7 -> x4, matrix products: 37.2 us -> 11.5 us  [back_product(): jnp.einsum('nf,df->nd', grads, weight, preferred_element_type=jnp.float32)]
  transfers between devices with their start and end apart: 24 -> 23, of which waited for: 17 -> 17; matrix products, arithmetic and copies ran while one was open for 33% -> 20% of each run, Pallas kernels for 0% -> 0%
where the time goes in v4:
time: 1230 us; the launch traced here: 1210 us
  waiting for transfers between devices  652 us (53%)
  local copies, waits for them, and re-layouts  212 us (17%)
  starting transfers between devices  112 us (9%)
  matrix products  77.3 us (6%)
  other arithmetic  65.1 us (5%)
  Pallas kernels  48.4 us (4%)
  between operations  20.4 us (2%)
  blocking collectives  18.7 us (2%)
    all_to_all x15, waiting for transfers between devices, exchange(): return lax.all_to_all(values, axes, split_axis=0, concat_axis=0, tiled=True)  370 us
    unnamed x5, waiting for transfers between devices  174 us
    gather x10, local copies, waits for them, and re-layouts, pick(): return jnp.take(table, index, axis=0, mode='clip')  117 us
    all_to_all x15, starting transfers between devices, exchange(): return lax.all_to_all(values, axes, split_axis=0, concat_axis=0, tiled=True)  93.4 us
    all_gather x1, waiting for transfers between devices, local(): lax.all_gather(pick(master_low, attn_send), ALL_AXES, axis=0, tiled=True)  60.7 us
    pallas_call x1, Pallas kernels, mix_chunk(): pl.pallas_call(mix_kernel, out_shape=(jax.ShapeDtypeStruct(stack.shape, j...  48.4 us
    reduce_scatter x1, waiting for transfers between devices, send_home(): lax.psum_scatter(buffer, COLUMN_AXES, scatter_dimension=0, tiled=True)  29.8 us
  transfers between devices with their start and end apart: 23, of which 17 were waited for; matrix products, arithmetic and copies ran while one was open for 20% of the time, Pallas kernels for 0%

profile of v4, /device:TPU:10, one launch (start us, length us, event | category | flops | bytes accessed | tf_op | source)
XLA Modules:
  0.0 1211.1 jit_solution(1287179956866937841)
XLA Ops:
  24.8 9.4 gather_fusion.7
  44.1 142.0 %all-to-all-done.7 = bf16[144,128,128]{2,1,0:T(8,128)(2,1)} async-done(((bf16[144,128,128]{2,1,0:T(8,128)(2,1)}), bf16[144,128,128]{2,1,0:T(8,128)(2,1)}, u32[]{:S(2)}, u32[]{:S(2)}) %all-to-all-start.7) | async-done | bytes 4718624 | tf_op jit(solution)/shard_map/all_to_all | solution.py:81
  191.4 60.7 %all-gather.11.cloned.1.call-done = bf16[736,128,128]{2,1,0:T(8,128)(2,1)} async-done(((bf16[23,128,128]{2,1,0:T(8,128)(2,1)}), bf16[736,128,128]{2,1,0:T(8,128)(2,1)}) %all-gather.11.cloned.1.call-update) | async-done | bytes 24117264 | tf_op jit(solution)/shard_map/all_gather | solution.py:406
  252.2 23.9 %conditional.3 = (bf16[336,128,128]{2,1,0:T(8,128)(2,1)}) conditional(s32[]{:T(128)} %convert_element_type.226, (bf16[90,128,128]{2,1,0:T(8,128)(2,1)}, s32[336]{0:T(512)S(1)}) %tuple.30, (s32[336]{0:T(512)S(1)}, s32[336]{0:T(512)S(1)}, bf16[736,128,128]{2,1,0:T(8,128)(2,1)}) %tuple.31), branch_computations={%region_4.5_spmd, %region_5.6_spmd} | conditional | flops 1696 | bytes 313989824 | solution.py:411
  257.4 18.7 %gather_fusion = bf16[336,128,128]{2,1,0:T(8,128)(2,1)} fusion(bf16[736,128,128]{2,1,0:T(8,128)(2,1)} %get-tuple-element.99, s32[1024]{0:T(1024)S(1)} %pad_clamp_fusion.1), kind=kCustom, calls=%fused_computation.1 | custom fusion | bytes 22021440 | tf_op jit(solution)/shard_map/cond/branch_1_fun/jit(_take)/gather | solution.py:55
  299.5 9.1 fusion.106
  321.8 11.1 all-to-all-done.1
  339.6 20.7 %all-to-all-done.3 = bf16[4,2,4,64,256]{4,3,2,1,0:T(8,128)(2,1)S(1)} async-done(((bf16[4,2,4,64,256]{4,3,2,1,0:T(8,128)(2,1)}), bf16[4,2,4,64,256]{4,3,2,1,0:T(8,128)(2,1)S(1)}, u32[]{:S(2)}, u32[]{:S(2)}) %all-to-all-start.3) | async-done | bytes 1048608 | tf_op jit(solution)/shard_map/all_to_all | solution.py:81
  415.8 29.0 %all-to-all-done.5 = bf16[4,128,1536]{1,2,0:T(8,128)(2,1)} async-done(((bf16[4,128,1536]{1,2,0:T(8,128)(2,1)}), bf16[4,128,1536]{1,2,0:T(8,128)(2,1)}, u32[]{:S(2)}, u32[]{:S(2)}) %all-to-all-start.5) | async-done | bytes 1572896 | tf_op jit(solution)/shard_map/all_to_all | solution.py:81
  465.4 28.7 %conditional.4 = (bf16[648,128,128]{2,1,0:T(8,128)(2,1)}) conditional(s32[]{:T(128)} %convert_element_type.242, (bf16[90,128,128]{2,1,0:T(8,128)(2,1)}, s32[648]{0:T(1024)}) %tuple.32, (s32[648]{0:T(1024)S(1)}, bf16[904,128,128]{2,1,0:T(8,128)(2,1)}) %tuple.113), branch_computations={%region_15.16_spmd, %region_16.17_spmd} | conditional | flops 1024 | bytes 334439552 | solution.py:418
  466.5 27.7 %gather_fusion.1 = bf16[648,128,128]{2,1,0:T(8,128)(2,1)} fusion(bf16[904,128,128]{2,1,0:T(8,128)(2,1)} %get-tuple-element.104, s32[1024]{0:T(1024)} %pad_clamp_fusion.3), kind=kCustom, calls=%fused_computation.3 | custom fusion | bytes 42469920 | tf_op jit(solution)/shard_map/cond/branch_1_fun/jit(_take)/gather | solution.py:55
  494.2 48.4 %shard_map.179 = (bf16[648,128,128]{2,1,0:T(8,128)(2,1)}, bf16[512,1536]{1,0:T(8,128)(2,1)}, bf16[512,1536]{1,0:T(8,128)(2,1)}) custom-call(s32[1]{0:T(128)} %bitcast.24.first_ref, bf16[512,1536]{1,0:T(8,128)(2,1)} %copy.310.x_ref, bf16[1536,512]{1,0:T(8,128)(2,1)} %get-tuple-element.188.xt_ref, bf16[512,1536]{1,0:T(8,128)(2,1)} %bitcast.27.seed_ref, ...), custom_call_target="tpu_custom_call" | custom-call | tf_op jit(solution)/shard_map/pallas_call | solution.py:197
  548.0 26.7 %gather_fusion.9 = bf16[904,128,128]{2,1,0:T(8,128)(2,1)} fusion(bf16[648,128,128]{2,1,0:T(8,128)(2,1)} %get-tuple-element.137, s32[1024]{0:T(1024)S(1)} %pad_clamp_fusion.9), kind=kCustom, calls=%fused_computation.9 | custom fusion | bytes 59248160 | tf_op jit(solution)/shard_map/jit(_take)/gather | solution.py:55
  656.1 16.6 %all-to-all-done.12 = bf16[4,2,256,256]{3,2,1,0:T(8,128)(2,1)S(1)} async-done(((bf16[4,2,256,256]{3,2,1,0:T(8,128)(2,1)}), bf16[4,2,256,256]{3,2,1,0:T(8,128)(2,1)S(1)}, u32[]{:S(2)}, u32[]{:S(2)}) %all-to-all-start.12) | async-done | bytes 1048608 | tf_op jit(solution)/shard_map/all_to_all | solution.py:81
  703.1 25.7 %all-to-all-done.17 = bf16[4,128,1536]{2,1,0:T(8,128)(2,1)S(1)} async-done(((bf16[4,128,1536]{2,1,0:T(8,128)(2,1)}), bf16[4,128,1536]{2,1,0:T(8,128)(2,1)S(1)}, u32[]{:S(2)}, u32[]{:S(2)}) %all-to-all-start.17) | async-done | bytes 1572896 | tf_op jit(solution)/shard_map/all_to_all | solution.py:81
  749.3 33.3 %all-to-all-done.15 = bf16[4,128,2048]{2,1,0:T(8,128)(2,1)} async-done(((bf16[4,128,2048]{2,1,0:T(8,128)(2,1)}), bf16[4,128,2048]{2,1,0:T(8,128)(2,1)}, u32[]{:S(2)}, u32[]{:S(2)}) %all-to-all-start.15) | async-done | bytes 2097184 | tf_op jit(solution)/shard_map/all_to_all | solution.py:81
  809.4 11.0 all_to_all.151
  826.4 29.8 %reduce-scatter.10.cloned.1.call-done = bf16[23,128,128]{2,1,0:T(8,128)(2,1)} async-done(((bf16[184,128,128]{2,1,0:T(8,128)(2,1)}), bf16[23,128,128]{2,1,0:T(8,128)(2,1)}) %reduce-scatter.10.cloned.1.call-update) | async-done | bytes 753680 | tf_op jit(solution)/shard_map/reduce_scatter | solution.py:315
  868.6 172.9 %reduce-scatter.12.cloned.1.call-done = bf16[113,128,128]{2,1,0:T(8,128)(2,1)} async-done(((bf16[904,128,128]{2,1,0:T(8,128)(2,1)}), bf16[113,128,128]{2,1,0:T(8,128)(2,1)}) %reduce-scatter.12.cloned.1.call-update) | async-done | bytes 3702800
  1041.5 9.6 gather_fusion.10
  1067.2 90.8 %all-to-all-done.18 = bf16[144,128,128]{2,1,0:T(8,128)(2,1)} async-done(((bf16[144,128,128]{2,1,0:T(8,128)(2,1)}), bf16[144,128,128]{2,1,0:T(8,128)(2,1)}, u32[]{:S(2)}, u32[]{:S(2)}) %all-to-all-start.18) | async-done | bytes 4718624 | tf_op jit(solution)/shard_map/all_to_all | solution.py:81
  1158.1 12.3 %conditional.5 = (bf16[90,128,128]{2,1,0:T(8,128)(2,1)}) conditional(s32[]{:T(128)} %convert_element_type.262, (s32[336]{0:T(512)S(1)}, s32[]{:T(128)}, s32[648]{0:T(1024)S(1)}, bf16[648,128,128]{2,1,0:T(8,128)(2,1)}, bf16[84,128,128]{2,1,0:T(8,128)(2,1)S(1)}) %tuple.114, (bf16[144,128,128]{2,1,0:T(8,128)(2,1)}, bf16[44,128,128]{2,1,0:T(8,128)(2,1)}, ...), branch_computations={%region_34.38_spmd, %region_38.41_spmd} | conditional | flops 69717856 | bytes 717487616 | solution.py:606
  1170.4 16.1 %fusion.4 = (f32[90,128,128]{2,1,0:T(8,128)}, f32[90,128,128]{2,1,0:T(8,128)}) fusion(f32[90,128,128]{2,1,0:T(8,128)} %param.24, f32[90,128,128]{2,1,0:T(8,128)} %param.23, f32[90,128,128]{2,1,0:T(8,128)} %param.26, f32[90,128,128]{2,1,0:T(8,128)} %param.25, bf16[90,128,128]{2,1,0:T(8,128)(2,1)} %get-tuple-element.239, pred[90]{0:T(512)(128)(4,1)S(1)} %copy-done.54), kind=kOutput, calls=%fused_computation.43 | convolution fusion | flops 765296640 | bytes 38338648 | tf_op jit(solution)/shard_map/sik,skl->sil/dot_general | solution.py:609
  1186.5 16.8 %multiply_subtract_fusion = f32[90,128,128]{2,1,0:T(8,128)} fusion(f32[90,128,128]{2,1,0:T(8,128)} %param.22, f32[90]{0:T(128)S(1)} %copy-done.61, f32[90,128,128]{2,1,0:T(8,128)} %param.26, f32[90,128,128]{2,1,0:T(8,128)} %param.25, f32[90,128,128]{2,1,0:T(8,128)} %get-tuple-element.185, f32[90,128,128]{2,1,0:T(8,128)} %get-tuple-element.184), kind=kOutput, calls=%fused_computation.44 | convolution fusion | flops 763822080 | bytes 35389800 | tf_op jit(solution)/shard_map/sik,slk->sil/dot_general | solution.py:614
  (383 shorter events, 358.7 us)
Async XLA Ops:
  8.0 244.2 %all-gather.11.cloned.1.call-start = ((), (), s32[]{:S(2)}) async-start(), calls=%async_computation.28 | async-start | bytes 24870912 | tf_op jit(solution)/shard_map/all_gather | solution.py:406
  34.2 151.9 %all-to-all-start.7 = ((bf16[144,128,128]{2,1,0:T(8,128)(2,1)}), bf16[144,128,128]{2,1,0:T(8,128)(2,1)}, u32[]{:S(2)}, u32[]{:S(2)}) async-start(bf16[144,128,128]{2,1,0:T(8,128)(2,1)} %gather_fusion.7), calls=%async_computation.8 | async-start | bytes 9437184 | tf_op jit(solution)/shard_map/all_to_all | solution.py:81
  43.2 209.0 %copy-start.39 = (s32[2592]{0:T(1024)}, s32[2592]{0:T(1024)S(1)}, u32[]{:S(2)}) copy-start(s32[2592]{0:T(1024)S(1)} %convert_reduce_fusion) | copy-start | bytes 31108
  276.1 189.3 %all-gather.13.cloned.1.call-start = ((), (), s32[]{:S(2)}) async-start(), calls=%async_computation.29 | async-start | bytes 33325056 | tf_op jit(solution)/shard_map/all_gather | solution.py:415
  277.3 9.9 all-to-all-start
  294.5 23.1 %all-to-all-start.2 = ((bf16[4,2,64,256]{3,2,1,0:T(8,128)(2,1)}), bf16[4,2,64,256]{3,2,1,0:T(8,128)(2,1)S(1)}, u32[]{:S(2)}, u32[]{:S(2)}) async-start(bf16[4,2,64,256]{3,2,1,0:T(8,128)(2,1)} %pad_maximum_fusion.6), calls=%async_computation.3 | async-start | bytes 524288 | tf_op jit(solution)/shard_map/all_to_all | solution.py:81
  317.6 15.3 %all-to-all-start.1 = ((bf16[2,64,12,128]{3,1,0,2:T(8,128)(2,1)}), bf16[2,64,12,128]{3,1,0,2:T(8,128)(2,1)S(1)}, u32[]{:S(2)}, u32[]{:S(2)}) async-start(bf16[2,64,12,128]{3,1,0,2:T(8,128)(2,1)} %copy.290), calls=%async_computation.2 | async-start | bytes 786432 | tf_op jit(solution)/shard_map/all_to_all | solution.py:454
  334.0 26.4 %all-to-all-start.3 = ((bf16[4,2,4,64,256]{4,3,2,1,0:T(8,128)(2,1)}), bf16[4,2,4,64,256]{4,3,2,1,0:T(8,128)(2,1)S(1)}, u32[]{:S(2)}, u32[]{:S(2)}) async-start(bf16[4,2,4,64,256]{4,3,2,1,0:T(8,128)(2,1)} %broadcast_in_dim.392), calls=%async_computation.4 | async-start | bytes 2097152 | tf_op jit(solution)/shard_map/all_to_all | solution.py:81
  373.6 15.5 %all-to-all-start.4 = ((bf16[2,256,3,128]{3,0,2,1:T(2,128)(2,1)}), bf16[2,256,3,128]{3,0,2,1:T(2,128)(2,1)}, u32[]{:S(2)}, u32[]{:S(2)}) async-start(bf16[2,256,3,128]{3,0,2,1:T(2,128)(2,1)} %copy.301), calls=%async_computation.5 | async-start | bytes 786432 | tf_op jit(solution)/shard_map/all_to_all | solution.py:479
  404.4 40.4 %all-to-all-start.5 = ((bf16[4,128,1536]{1,2,0:T(8,128)(2,1)}), bf16[4,128,1536]{1,2,0:T(8,128)(2,1)}, u32[]{:S(2)}, u32[]{:S(2)}) async-start(bf16[4,128,1536]{1,2,0:T(8,128)(2,1)} %broadcast_in_dim.396), calls=%async_computation.6 | async-start | bytes 3145728 | tf_op jit(solution)/shard_map/all_to_all | solution.py:81
  447.1 47.1 %all-to-all-start.6 = ((bf16[4,128,1536]{2,1,0:T(8,128)(2,1)}), bf16[4,128,1536]{2,1,0:T(8,128)(2,1)}, u32[]{:S(2)}, u32[]{:S(2)}) async-start(bf16[4,128,1536]{2,1,0:T(8,128)(2,1)} %broadcast_in_dim.397), calls=%async_computation.7 | async-start | bytes 3145728 | tf_op jit(solution)/shard_map/all_to_all | solution.py:81
  542.6 37.8 %all-to-all-start.8 = ((bf16[4,128,1536]{2,1,0:T(8,128)(2,1)}), bf16[4,128,1536]{2,1,0:T(8,128)(2,1)}, u32[]{:S(2)}, u32[]{:S(2)}) async-start(bf16[4,128,1536]{2,1,0:T(8,128)(2,1)} %bitcast.253), calls=%async_computation.9 | async-start | bytes 3145728 | tf_op jit(solution)/shard_map/all_to_all | solution.py:81
  596.7 18.1 %all-to-all-start.9 = ((bf16[2,64,12,128]{3,1,0,2:T(8,128)(2,1)}), bf16[2,64,12,128]{3,1,0,2:T(8,128)(2,1)}, u32[]{:S(2)}, u32[]{:S(2)}) async-start(bf16[2,64,12,128]{3,1,0,2:T(8,128)(2,1)} %copy.311), calls=%async_computation.10 | async-start | bytes 786432 | tf_op jit(solution)/shard_map/all_to_all | solution.py:504
  614.8 18.3 %all-to-all-start.14 = ((bf16[4,128,384]{1,2,0:T(8,128)(2,1)}), bf16[4,128,384]{1,2,0:T(8,128)(2,1)}, u32[]{:S(2)}, u32[]{:S(2)}) async-start(bf16[4,128,384]{1,2,0:T(8,128)(2,1)} %fusion.69), calls=%async_computation.15 | async-start | bytes 786432 | tf_op jit(solution)/shard_map/all_to_all | solution.py:81
  633.0 13.1 %all-to-all-start.16 = ((bf16[4,128,384]{1,2,0:T(8,128)(2,1)}), bf16[4,128,384]{1,2,0:T(8,128)(2,1)}, u32[]{:S(2)}, u32[]{:S(2)}) async-start(bf16[4,128,384]{1,2,0:T(8,128)(2,1)} %bitcast.257), calls=%async_computation.17 | async-start | bytes 786432 | tf_op jit(solution)/shard_map/all_to_all | solution.py:81
  646.2 26.6 %all-to-all-start.12 = ((bf16[4,2,256,256]{3,2,1,0:T(8,128)(2,1)}), bf16[4,2,256,256]{3,2,1,0:T(8,128)(2,1)S(1)}, u32[]{:S(2)}, u32[]{:S(2)}) async-start(bf16[4,2,256,256]{3,2,1,0:T(8,128)(2,1)} %copy_bitcast_fusion.1), calls=%async_computation.13 | async-start | bytes 2097152 | tf_op jit(solution)/shard_map/all_to_all | solution.py:81
  672.7 9.5 all-to-all-start.11
  691.3 37.5 %all-to-all-start.17 = ((bf16[4,128,1536]{2,1,0:T(8,128)(2,1)}), bf16[4,128,1536]{2,1,0:T(8,128)(2,1)S(1)}, u32[]{:S(2)}, u32[]{:S(2)}) async-start(bf16[4,128,1536]{2,1,0:T(8,128)(2,1)} %broadcast_in_dim.412), calls=%async_computation.18 | async-start | bytes 3145728 | tf_op jit(solution)/shard_map/all_to_all | solution.py:81
  730.4 52.2 %all-to-all-start.15 = ((bf16[4,128,2048]{2,1,0:T(8,128)(2,1)}), bf16[4,128,2048]{2,1,0:T(8,128)(2,1)}, u32[]{:S(2)}, u32[]{:S(2)}) async-start(bf16[4,128,2048]{2,1,0:T(8,128)(2,1)} %broadcast_in_dim.411), calls=%async_computation.16 | async-start | bytes 4194304 | tf_op jit(solution)/shard_map/all_to_all | solution.py:81
  738.1 118.0 %reduce-scatter.10.cloned.1.call-start = ((), (), s32[]{:S(2)}) async-start(), calls=%async_computation.27 | async-start | bytes 6782976 | tf_op jit(solution)/shard_map/reduce_scatter | solution.py:315
  794.9 246.6 %reduce-scatter.12.cloned.1.call-start = ((), (), s32[]{:S(2)}) async-start(), calls=%async_computation.30 | async-start | bytes 33325056
  820.4 39.9 %all-to-all-start.10 = ((bf16[4,128,1536]{2,1,0:T(8,128)(2,1)}), bf16[4,128,1536]{2,1,0:T(8,128)(2,1)}, u32[]{:S(2)}, u32[]{:S(2)}) async-start(bf16[4,128,1536]{2,1,0:T(8,128)(2,1)} %bitcast.252), calls=%async_computation.11 | async-start | bytes 3145728 | tf_op jit(solution)/shard_map/all_to_all | solution.py:81
  860.3 190.9 %all-to-all-start.19 = ((bf16[44,128,128]{2,1,0:T(8,128)(2,1)}), bf16[44,128,128]{2,1,0:T(8,128)(2,1)}, u32[]{:S(2)}, u32[]{:S(2)}) async-start(bf16[44,128,128]{2,1,0:T(8,128)(2,1)} %gather_fusion.12), calls=%async_computation.21 | async-start | bytes 2883584 | tf_op jit(solution)/shard_map/all_to_all | solution.py:81
  1051.2 106.8 %all-to-all-start.18 = ((bf16[144,128,128]{2,1,0:T(8,128)(2,1)}), bf16[144,128,128]{2,1,0:T(8,128)(2,1)}, u32[]{:S(2)}, u32[]{:S(2)}) async-start(bf16[144,128,128]{2,1,0:T(8,128)(2,1)} %gather_fusion.10), calls=%async_computation.19 | async-start | bytes 9437184 | tf_op jit(solution)/shard_map/all_to_all | solution.py:81
  (63 other events, 981.4 us)
Sparse Core Ops, SparseCore 0:
  21.3 230.8 all-gather.10
Sparse Core Ops, SparseCore 1:
  279.0 154.9 all-gather.12
  795.0 61.0 reduce-scatter.9
  859.6 181.8 reduce-scatter.11

commit v5 on v4

--- a/solution.py
+++ b/solution.py
@@ -28,7 +28,6 @@
 SMALL_RATE = 0.25
 WEIGHT_DECAY = 0.01
 MASK_FILL = -1e30
-TOP_PRECISION = lax.Precision.DEFAULT
 
 
 def matrix_shapes():
@@ -311,10 +310,63 @@
         index = locate(wanted, self.place, jnp.arange(self.tiles, dtype=jnp.int32))
         return pick(tiles, index)
 
-    def send_home(self, buffer):
-        summed = lax.psum_scatter(buffer, COLUMN_AXES, scatter_dimension=0, tiled=True)
+    def sum_columns(self, buffer):
+        return lax.psum_scatter(buffer, COLUMN_AXES, scatter_dimension=0, tiled=True)
+
+    def send_home(self, summed):
         back = locate(self.pair_slots, jnp.where(self.held, self.arrival, -1), self.my_rank)
         return exchange(pick(summed, back), "blk")
+
+
+def soap_kernel(
+    used_ref, grad_ref, master_ref, first_ref, second_ref, left_ref, right_ref,
+    master_out, first_out, second_out,
+):
+    count = grad_ref.shape[0]
+    base = pl.program_id(0) * count
+
+    def product(one, other, dims):
+        return lax.dot_general(
+            one.astype(jnp.bfloat16),
+            other.astype(jnp.bfloat16),
+            (dims, ((), ())),
+            preferred_element_type=jnp.float32,
+        )
+
+    for number in range(count):
+        grad = jnp.where(used_ref[base + number] > 0, grad_ref[number], jnp.bfloat16(0))
+        left = left_ref[number].astype(jnp.bfloat16)
+        right = right_ref[number].astype(jnp.bfloat16)
+        rotated = product(product(left, grad, ((0,), (0,))), right, ((1,), (0,)))
+        first_new = BETA_FIRST * first_ref[number] + (1.0 - BETA_FIRST) * rotated
+        second_new = BETA_SECOND * second_ref[number] + (1.0 - BETA_SECOND) * rotated * rotated
+        normalized = first_new / (jnp.sqrt(second_new) + ADAM_EPS)
+        update = product(product(left, normalized, ((1,), (0,))), right, ((1,), (1,)))
+        master = master_ref[number]
+        scale = jnp.sqrt(jnp.mean(master * master, keepdims=True) + SCALE_EPS)
+        first_out[number] = first_new
+        second_out[number] = second_new
+        master_out[number] = master - RELATIVE_RATE * scale * (update + WEIGHT_DECAY * master)
+
+
+def soap_step(used, grads, *state):
+    slots = grads.shape[0]
+    count = max(number for number in range(1, 11) if slots % number == 0)
+    tiles = pl.BlockSpec((count, BLOCK, BLOCK), lambda step, flags: (step, 0, 0))
+    whole = jax.ShapeDtypeStruct((slots, BLOCK, BLOCK), jnp.float32)
+    return pl.pallas_call(
+        soap_kernel,
+        out_shape=(whole, whole, whole),
+        grid_spec=pltpu.PrefetchScalarGridSpec(
+            num_scalar_prefetch=1,
+            grid=(slots // count,),
+            in_specs=[tiles] * 6,
+            out_specs=(tiles, tiles, tiles),
+        ),
+        compiler_params=pltpu.CompilerParams(
+            dimension_semantics=("arbitrary",), vmem_limit_bytes=40 * 1024 * 1024
+        ),
+    )(used, grads, *state)
 
 
 def rotate(values, positions, direction):
@@ -403,13 +455,13 @@
 
     master_low = master.astype(jnp.bfloat16)
     small_copies = spread(small_master.astype(jnp.bfloat16), ALL_AXES).reshape(-1)
-    attn_buffer = lax.all_gather(pick(master_low, attn_send), ALL_AXES, axis=0, tiled=True)
+    attn_gathered = lax.all_gather(pick(master_low, attn_send), ALL_AXES, axis=0, tiled=True)
 
     def whole_tiles(index):
         return pick(lax.all_gather(master_low, ALL_AXES, axis=0, tiled=True), index)
 
     attn_tiles = lax.cond(
-        fits_attn, lambda: pick(attn_buffer, attn_place), lambda: whole_tiles(attn_owner)
+        fits_attn, lambda: pick(attn_gathered, attn_place), lambda: whole_tiles(attn_owner)
     )
     arrived_tiles = exchange(pick(master_low, route.send_index()), "blk")
     shard_buffer = lax.all_gather(
@@ -490,7 +542,7 @@
     grad_normed_two = exchange_sum(grad_line.reshape(blk_count, token_count, D), "blk")
     home_buffer = route.home_buffer(shard_grads)
     grad_normed_two, home_buffer = lax.optimization_barrier((grad_normed_two, home_buffer))
-    returned_grads = route.send_home(home_buffer)
+    summed_tiles = route.sum_columns(home_buffer)
     norm_part_two, gain_second_grad = norm_backward(
         middle, inverse_second, gain_second, grad_normed_two
     )
@@ -502,12 +554,6 @@
         .reshape(seq_count, rows_local, QH, HD)
     )
     grad_heads = lax.all_to_all(grad_out_rows, "uly", split_axis=2, concat_axis=1, tiled=True)
-    mixed_line, grad_heads = lax.optimization_barrier((mixed_line, grad_heads))
-    mixed_out = (
-        (middle + exchange_sum(mixed_line.reshape(blk_count, token_count, D), "blk"))
-        .astype(jnp.bfloat16)
-        .reshape(seq_count, rows_local, D)
-    )
     grad_heads_wide = grad_heads.astype(jnp.float32)
     row_delta = jnp.sum(grad_heads_wide * attended, axis=-1)
 
@@ -572,6 +618,13 @@
     grad_lines = spread(
         jnp.concatenate([grad_query_lin, grad_key_lin, grad_value_lin], axis=1), "blk"
     ).reshape(blk_count * token_count, QW + 2 * KVW)
+    returned_grads = route.send_home(summed_tiles)
+    grad_lines, mixed_line = lax.optimization_barrier((grad_lines, mixed_line))
+    mixed_out = (
+        (middle + exchange_sum(mixed_line.reshape(blk_count, token_count, D), "blk"))
+        .astype(jnp.bfloat16)
+        .reshape(seq_count, rows_local, D)
+    )
     middle_lines = spread(grad_middle_low, "blk").reshape(blk_count * token_count, D)
     attn_grads = jnp.concatenate(
         [
@@ -584,7 +637,9 @@
         ],
         axis=0,
     )
-    attn_returned = attn_route.send_home(attn_route.home_buffer(attn_grads))
+    attn_buffer = attn_route.home_buffer(attn_grads)
+    attn_buffer, summed_tiles = lax.optimization_barrier((attn_buffer, summed_tiles))
+    attn_returned = attn_route.send_home(attn_route.sum_columns(attn_buffer))
     my_slots = my_first + jnp.arange(slot_local, dtype=jnp.int32)
     slot_index = locate(my_slots, route.owner, route.slot_position()) + locate(
         my_slots, attn_route.owner, blk_count * route.pair_cap + attn_route.slot_position()
@@ -604,16 +659,15 @@
         return lax.psum_scatter(parts, ALL_AXES, scatter_dimension=0, tiled=True)
 
     grad_slots = lax.cond(route.fits & attn_route.fits, routed_grads, summed_grads)
-    grad_slots = jnp.where(slot_used[:, None, None], grad_slots, 0).astype(jnp.float32)
-    rotated = jnp.einsum("sji,sjk->sik", basis_left, grad_slots, precision=TOP_PRECISION)
-    rotated = jnp.einsum("sik,skl->sil", rotated, basis_right, precision=TOP_PRECISION)
-    first_new = BETA_FIRST * moment_first + (1.0 - BETA_FIRST) * rotated
-    second_new = BETA_SECOND * moment_second + (1.0 - BETA_SECOND) * rotated * rotated
-    normalized = first_new / (jnp.sqrt(second_new) + ADAM_EPS)
-    update = jnp.einsum("sik,skl->sil", basis_left, normalized, precision=TOP_PRECISION)
-    update = jnp.einsum("sik,slk->sil", update, basis_right, precision=TOP_PRECISION)
-    tile_scale = jnp.sqrt(jnp.mean(master * master, axis=(1, 2), keepdims=True) + SCALE_EPS)
-    master_new = master - RELATIVE_RATE * tile_scale * (update + WEIGHT_DECAY * master)
+    master_new, first_new, second_new = soap_step(
+        slot_used.astype(jnp.int32),
+        grad_slots,
+        master,
+        moment_first,
+        moment_second,
+        basis_left,
+        basis_right,
+    )
     small_first_new = BETA_FIRST * small_first + (1.0 - BETA_FIRST) * grad_small
     small_second_new = BETA_SECOND * small_second + (1.0 - BETA_SECOND) * grad_small * grad_small
     small_new = small_master - SMALL_RATE * (

time: 1230 us -> 1060 us (0.86)
  waiting for transfers between devices: 652 us -> 490 us
  matrix products: 77.3 us -> 40.4 us
  Pallas kernels: 48.4 us -> 81.3 us
    unnamed x5, waiting for transfers between devices: 174 us -> 0.6 us
    pallas_call x0 -> x1, Pallas kernels: none -> 32.9 us  [soap_step(): pl.pallas_call(soap_kernel, out_shape=(whole, whole, whole), grid_spec=pl...]
    dot_general x2 -> x0, matrix products: 32.9 us -> none  [the longest x1 16.8 us: local(): jnp.einsum('sik,slk->sil', update, basis_right, precision=TOP_PRECISION)]
    all_to_all x15 -> x16, starting transfers between devices: 93.4 us -> 103 us  [exchange(): return lax.all_to_all(values, axes, split_axis=0, concat_axis=0, tiled=True)]
    all_to_all x15 -> x16, waiting for transfers between devices: 370 us -> 378 us  [exchange(): return lax.all_to_all(values, axes, split_axis=0, concat_axis=0, tiled=True)]
  transfers between devices with their start and end apart: 23 -> 24, of which waited for: 17 -> 17; matrix products, arithmetic and copies ran while one was open for 20% -> 25% of each run, Pallas kernels for 0% -> 0%
where the time goes in v5:
time: 1060 us; the launch traced here: 1040 us
  waiting for transfers between devices  490 us (46%)
  local copies, waits for them, and re-layouts  212 us (20%)
  starting transfers between devices  122 us (12%)
  Pallas kernels  81.3 us (8%)
  other arithmetic  62.4 us (6%)
  matrix products  40.4 us (4%)
  between operations  20.4 us (2%)
  blocking collectives  10.6 us (1%)
    all_to_all x16, waiting for transfers between devices, exchange(): return lax.all_to_all(values, axes, split_axis=0, concat_axis=0, tiled=True)  378 us
    gather x10, local copies, waits for them, and re-layouts, pick(): return jnp.take(table, index, axis=0, mode='clip')  114 us
    all_to_all x16, starting transfers between devices, exchange(): return lax.all_to_all(values, axes, split_axis=0, concat_axis=0, tiled=True)  103 us
    all_gather x1, waiting for transfers between devices, local(): lax.all_gather(pick(master_low, attn_send), ALL_AXES, axis=0, tiled=True)  60.7 us
    pallas_call x1, Pallas kernels, mix_chunk(): pl.pallas_call(mix_kernel, out_shape=(jax.ShapeDtypeStruct(stack.shape, j...  48.4 us
    pallas_call x1, Pallas kernels, soap_step(): pl.pallas_call(soap_kernel, out_shape=(whole, whole, whole), grid_spec=pl...  32.9 us
    reduce_scatter x1, waiting for transfers between devices, sum_columns(): lax.psum_scatter(buffer, COLUMN_AXES, scatter_dimension=0, tiled=True)  27.9 us
  transfers between devices with their start and end apart: 24, of which 17 were waited for; matrix products, arithmetic and copies ran while one was open for 25% of the time, Pallas kernels for 0%

profile of v5, /device:TPU:10, one launch (start us, length us, event | category | flops | bytes accessed | tf_op | source)
XLA Modules:
  0.0 1043.7 jit_solution(12583077042996858615)
XLA Ops:
  36.1 143.8 %all-to-all-done.7 = bf16[144,128,128]{2,1,0:T(8,128)(2,1)} async-done(((bf16[144,128,128]{2,1,0:T(8,128)(2,1)}), bf16[144,128,128]{2,1,0:T(8,128)(2,1)}, u32[]{:S(2)}, u32[]{:S(2)}) %all-to-all-start.7) | async-done | bytes 4718624 | tf_op jit(solution)/shard_map/all_to_all | solution.py:80
  185.2 60.7 %all-gather.11.cloned.1.call-done = bf16[736,128,128]{2,1,0:T(8,128)(2,1)} async-done(((bf16[23,128,128]{2,1,0:T(8,128)(2,1)}), bf16[736,128,128]{2,1,0:T(8,128)(2,1)}) %all-gather.11.cloned.1.call-update) | async-done | bytes 24117264 | tf_op jit(solution)/shard_map/all_gather | solution.py:458
  246.0 23.6 %conditional.3 = (bf16[336,128,128]{2,1,0:T(8,128)(2,1)}) conditional(s32[]{:T(128)} %convert_element_type.226, (bf16[90,128,128]{2,1,0:T(8,128)(2,1)S(1)}, s32[336]{0:T(512)S(1)}) %tuple.31, (s32[336]{0:T(512)S(1)}, s32[336]{0:T(512)S(1)}, bf16[736,128,128]{2,1,0:T(8,128)(2,1)}) %tuple.32), branch_computations={%region_4.5_spmd, %region_5.6_spmd} | conditional | flops 1696 | bytes 325786304 | solution.py:463
  250.9 18.7 %gather_fusion = bf16[336,128,128]{2,1,0:T(8,128)(2,1)} fusion(bf16[736,128,128]{2,1,0:T(8,128)(2,1)} %get-tuple-element.99, s32[1024]{0:T(1024)S(1)} %pad_clamp_fusion.1), kind=kCustom, calls=%fused_computation.1 | custom fusion | bytes 22021440 | tf_op jit(solution)/shard_map/cond/branch_1_fun/jit(_take)/gather | solution.py:54
  293.1 9.1 fusion.86
  315.4 11.1 %all-to-all-done.1 = bf16[2,64,12,128]{3,1,0,2:T(8,128)(2,1)S(1)} async-done(((bf16[2,64,12,128]{3,1,0,2:T(8,128)(2,1)}), bf16[2,64,12,128]{3,1,0,2:T(8,128)(2,1)S(1)}, u32[]{:S(2)}, u32[]{:S(2)}) %all-to-all-start.1) | async-done | bytes 393248 | tf_op jit(solution)/shard_map/all_to_all | solution.py:506
  333.5 20.7 %all-to-all-done.3 = bf16[4,2,4,64,256]{4,3,2,1,0:T(8,128)(2,1)S(1)} async-done(((bf16[4,2,4,64,256]{4,3,2,1,0:T(8,128)(2,1)}), bf16[4,2,4,64,256]{4,3,2,1,0:T(8,128)(2,1)S(1)}, u32[]{:S(2)}, u32[]{:S(2)}) %all-to-all-start.3) | async-done | bytes 1048608 | tf_op jit(solution)/shard_map/all_to_all | solution.py:80
  409.6 29.0 %all-to-all-done.5 = bf16[4,128,1536]{1,2,0:T(8,128)(2,1)} async-done(((bf16[4,128,1536]{1,2,0:T(8,128)(2,1)}), bf16[4,128,1536]{1,2,0:T(8,128)(2,1)}, u32[]{:S(2)}, u32[]{:S(2)}) %all-to-all-start.5) | async-done | bytes 1572896 | tf_op jit(solution)/shard_map/all_to_all | solution.py:80
  459.2 28.4 %conditional.4 = (bf16[648,128,128]{2,1,0:T(8,128)(2,1)}) conditional(s32[]{:T(128)} %convert_element_type.242, (bf16[90,128,128]{2,1,0:T(8,128)(2,1)}, s32[648]{0:T(1024)}) %tuple.112, (s32[648]{0:T(1024)S(1)}, bf16[904,128,128]{2,1,0:T(8,128)(2,1)}) %tuple.114), branch_computations={%region_15.16_spmd, %region_16.17_spmd} | conditional | flops 1024 | bytes 334439552 | solution.py:470
  459.9 27.7 %gather_fusion.1 = bf16[648,128,128]{2,1,0:T(8,128)(2,1)} fusion(bf16[904,128,128]{2,1,0:T(8,128)(2,1)} %get-tuple-element.104, s32[1024]{0:T(1024)} %pad_clamp_fusion.3), kind=kCustom, calls=%fused_computation.3 | custom fusion | bytes 42469920 | tf_op jit(solution)/shard_map/cond/branch_1_fun/jit(_take)/gather | solution.py:54
  487.6 48.4 %shard_map.179 = (bf16[648,128,128]{2,1,0:T(8,128)(2,1)}, bf16[512,1536]{1,0:T(8,128)(2,1)}, bf16[512,1536]{1,0:T(8,128)(2,1)}) custom-call(s32[1]{0:T(128)} %bitcast.25.first_ref, bf16[512,1536]{1,0:T(8,128)(2,1)} %copy.288.x_ref, bf16[1536,512]{1,0:T(8,128)(2,1)} %get-tuple-element.192.xt_ref, bf16[512,1536]{1,0:T(8,128)(2,1)} %bitcast.27.seed_ref, ...), custom_call_target="tpu_custom_call" | custom-call | tf_op jit(solution)/shard_map/pallas_call | solution.py:196
  541.5 26.7 %gather_fusion.9 = bf16[904,128,128]{2,1,0:T(8,128)(2,1)} fusion(bf16[648,128,128]{2,1,0:T(8,128)(2,1)} %get-tuple-element.140, s32[1024]{0:T(1024)S(1)} %pad_clamp_fusion.9), kind=kCustom, calls=%fused_computation.9 | custom fusion | bytes 59248160 | tf_op jit(solution)/shard_map/jit(_take)/gather | solution.py:54
  636.1 16.0 %all-to-all-done.11 = bf16[4,2,256,256]{3,2,1,0:T(8,128)(2,1)S(1)} async-done(((bf16[4,2,256,256]{3,2,1,0:T(8,128)(2,1)}), bf16[4,2,256,256]{3,2,1,0:T(8,128)(2,1)S(1)}, u32[]{:S(2)}, u32[]{:S(2)}) %all-to-all-start.11) | async-done | bytes 1048608 | tf_op jit(solution)/shard_map/all_to_all | solution.py:80
  656.5 10.1 all-to-all-done.10
  666.6 10.6 %all_to_all.150 = bf16[4,2,64,256]{3,2,1,0:T(8,128)(2,1)S(1)} all-to-all(bf16[4,2,64,256]{3,2,1,0:T(8,128)(2,1)S(1)} %bitcast.259), channel_id=1, replica_groups=mesh['dp'=2,'blk'=4,'uly'=4] {'uly'}, dimensions={0} | all-to-all | bytes 524288 | tf_op jit(solution)/shard_map/all_to_all | solution.py:80
  696.5 21.1 %all-to-all-done.17 = bf16[4,128,1536]{2,1,0:T(8,128)(2,1)S(1)} async-done(((bf16[4,128,1536]{2,1,0:T(8,128)(2,1)}), bf16[4,128,1536]{2,1,0:T(8,128)(2,1)S(1)}, u32[]{:S(2)}, u32[]{:S(2)}) %all-to-all-start.17) | async-done | bytes 1572896 | tf_op jit(solution)/shard_map/all_to_all | solution.py:80
  740.3 30.8 %all-to-all-done.13 = bf16[4,128,2048]{2,1,0:T(8,128)(2,1)S(1)} async-done(((bf16[4,128,2048]{2,1,0:T(8,128)(2,1)}), bf16[4,128,2048]{2,1,0:T(8,128)(2,1)S(1)}, u32[]{:S(2)}, u32[]{:S(2)}) %all-to-all-start.13) | async-done | bytes 2097184 | tf_op jit(solution)/shard_map/all_to_all | solution.py:80
  815.1 9.7 gather_fusion.10
  824.8 13.3 %all-to-all-done.14 = bf16[4,128,1536]{2,1,0:T(8,128)(2,1)} async-done(((bf16[4,128,1536]{2,1,0:T(8,128)(2,1)}), bf16[4,128,1536]{2,1,0:T(8,128)(2,1)}, u32[]{:S(2)}, u32[]{:S(2)}) %all-to-all-start.14) | async-done | bytes 1572896 | tf_op jit(solution)/shard_map/all_to_all | solution.py:80
  846.6 27.9 %reduce-scatter.10.cloned.1.call-done = bf16[23,128,128]{2,1,0:T(8,128)(2,1)} async-done(((bf16[184,128,128]{2,1,0:T(8,128)(2,1)}), bf16[23,128,128]{2,1,0:T(8,128)(2,1)}) %reduce-scatter.10.cloned.1.call-update) | async-done | bytes 753680 | tf_op jit(solution)/shard_map/reduce_scatter | solution.py:314
  877.5 69.5 %all-to-all-done.18 = bf16[144,128,128]{2,1,0:T(8,128)(2,1)} async-done(((bf16[144,128,128]{2,1,0:T(8,128)(2,1)}), bf16[144,128,128]{2,1,0:T(8,128)(2,1)}, u32[]{:S(2)}, u32[]{:S(2)}) %all-to-all-start.18) | async-done | bytes 4718624 | tf_op jit(solution)/shard_map/all_to_all | solution.py:80
  964.0 21.2 %all-to-all-done.19 = bf16[44,128,128]{2,1,0:T(8,128)(2,1)} async-done(((bf16[44,128,128]{2,1,0:T(8,128)(2,1)}), bf16[44,128,128]{2,1,0:T(8,128)(2,1)}, u32[]{:S(2)}, u32[]{:S(2)}) %all-to-all-start.19) | async-done | bytes 1441824 | tf_op jit(solution)/shard_map/all_to_all | solution.py:80
  985.2 12.4 %conditional.5 = (bf16[90,128,128]{2,1,0:T(8,128)(2,1)}) conditional(s32[]{:T(128)} %convert_element_type.263, (s32[336]{0:T(512)S(1)}, s32[]{:T(128)}, s32[648]{0:T(1024)S(1)}, bf16[648,128,128]{2,1,0:T(8,128)(2,1)}, bf16[84,128,128]{2,1,0:T(8,128)(2,1)S(1)}) %tuple.115, (bf16[144,128,128]{2,1,0:T(8,128)(2,1)}, bf16[44,128,128]{2,1,0:T(8,128)(2,1)}, ...), branch_computations={%region_34.38_spmd, %region_38.41_spmd} | conditional | flops 69717856 | bytes 717487616 | solution.py:661
  1002.9 32.9 %shard_map.180 = (f32[90,128,128]{2,1,0:T(8,128)}, f32[90,128,128]{2,1,0:T(8,128)}, f32[90,128,128]{2,1,0:T(8,128)}) custom-call(s32[90]{0:T(128)S(1)} %convert_element_type.260.used_ref, bf16[90,128,128]{2,1,0:T(8,128)(2,1)} %get-tuple-element.243.grad_ref, f32[90,128,128]{2,1,0:T(8,128)S(1)} %copy-done, f32[90,128,128]{2,1,0:T(8,128)S(1)} %copy-done.1, ...), custom_call_target="tpu_custom_call" | custom-call | tf_op jit(solution)/shard_map/pallas_call | solution.py:357
  (397 shorter events, 358.9 us)
Async XLA Ops:
  8.0 238.0 %all-gather.11.cloned.1.call-start = ((), (), s32[]{:S(2)}) async-start(), calls=%async_computation.28 | async-start | bytes 24870912 | tf_op jit(solution)/shard_map/all_gather | solution.py:458
  26.2 153.8 %all-to-all-start.7 = ((bf16[144,128,128]{2,1,0:T(8,128)(2,1)}), bf16[144,128,128]{2,1,0:T(8,128)(2,1)}, u32[]{:S(2)}, u32[]{:S(2)}) async-start(bf16[144,128,128]{2,1,0:T(8,128)(2,1)} %gather_fusion.7), calls=%async_computation.8 | async-start | bytes 9437184 | tf_op jit(solution)/shard_map/all_to_all | solution.py:80
  269.6 189.6 %all-gather.13.cloned.1.call-start = ((), (), s32[]{:S(2)}) async-start(), calls=%async_computation.29 | async-start | bytes 33325056 | tf_op jit(solution)/shard_map/all_gather | solution.py:467
  270.8 9.9 all-to-all-start
  288.0 23.2 %all-to-all-start.2 = ((bf16[4,2,64,256]{3,2,1,0:T(8,128)(2,1)}), bf16[4,2,64,256]{3,2,1,0:T(8,128)(2,1)S(1)}, u32[]{:S(2)}, u32[]{:S(2)}) async-start(bf16[4,2,64,256]{3,2,1,0:T(8,128)(2,1)} %pad_maximum_fusion.6), calls=%async_computation.3 | async-start | bytes 524288 | tf_op jit(solution)/shard_map/all_to_all | solution.py:80
  311.2 15.3 %all-to-all-start.1 = ((bf16[2,64,12,128]{3,1,0,2:T(8,128)(2,1)}), bf16[2,64,12,128]{3,1,0,2:T(8,128)(2,1)S(1)}, u32[]{:S(2)}, u32[]{:S(2)}) async-start(bf16[2,64,12,128]{3,1,0,2:T(8,128)(2,1)} %copy.268), calls=%async_computation.2 | async-start | bytes 786432 | tf_op jit(solution)/shard_map/all_to_all | solution.py:506
  327.6 26.6 %all-to-all-start.3 = ((bf16[4,2,4,64,256]{4,3,2,1,0:T(8,128)(2,1)}), bf16[4,2,4,64,256]{4,3,2,1,0:T(8,128)(2,1)S(1)}, u32[]{:S(2)}, u32[]{:S(2)}) async-start(bf16[4,2,4,64,256]{4,3,2,1,0:T(8,128)(2,1)} %broadcast_in_dim.378), calls=%async_computation.4 | async-start | bytes 2097152 | tf_op jit(solution)/shard_map/all_to_all | solution.py:80
  367.9 15.4 %all-to-all-start.4 = ((bf16[2,256,3,128]{3,0,2,1:T(2,128)(2,1)}), bf16[2,256,3,128]{3,0,2,1:T(2,128)(2,1)}, u32[]{:S(2)}, u32[]{:S(2)}) async-start(bf16[2,256,3,128]{3,0,2,1:T(2,128)(2,1)} %copy.279), calls=%async_computation.5 | async-start | bytes 786432 | tf_op jit(solution)/shard_map/all_to_all | solution.py:531
  398.3 40.3 %all-to-all-start.5 = ((bf16[4,128,1536]{1,2,0:T(8,128)(2,1)}), bf16[4,128,1536]{1,2,0:T(8,128)(2,1)}, u32[]{:S(2)}, u32[]{:S(2)}) async-start(bf16[4,128,1536]{1,2,0:T(8,128)(2,1)} %broadcast_in_dim.382), calls=%async_computation.6 | async-start | bytes 3145728 | tf_op jit(solution)/shard_map/all_to_all | solution.py:80
  440.9 46.7 %all-to-all-start.6 = ((bf16[4,128,1536]{2,1,0:T(8,128)(2,1)}), bf16[4,128,1536]{2,1,0:T(8,128)(2,1)}, u32[]{:S(2)}, u32[]{:S(2)}) async-start(bf16[4,128,1536]{2,1,0:T(8,128)(2,1)} %broadcast_in_dim.383), calls=%async_computation.7 | async-start | bytes 3145728 | tf_op jit(solution)/shard_map/all_to_all | solution.py:80
  536.0 37.8 %all-to-all-start.8 = ((bf16[4,128,1536]{2,1,0:T(8,128)(2,1)}), bf16[4,128,1536]{2,1,0:T(8,128)(2,1)}, u32[]{:S(2)}, u32[]{:S(2)}) async-start(bf16[4,128,1536]{2,1,0:T(8,128)(2,1)} %bitcast.248), calls=%async_computation.9 | async-start | bytes 3145728 | tf_op jit(solution)/shard_map/all_to_all | solution.py:80
  541.1 273.2 %reduce-scatter.12.cloned.1.call-start = ((), (), s32[]{:S(2)}) async-start(), calls=%async_computation.30 | async-start | bytes 33325056
  593.0 11.0 %all-to-all-start.9 = ((bf16[2,64,12,128]{3,1,0,2:T(8,128)(2,1)}), bf16[2,64,12,128]{3,1,0,2:T(8,128)(2,1)}, u32[]{:S(2)}, u32[]{:S(2)}) async-start(bf16[2,64,12,128]{3,1,0,2:T(8,128)(2,1)} %copy.289), calls=%async_computation.10 | async-start | bytes 786432 | tf_op jit(solution)/shard_map/all_to_all | solution.py:556
  604.1 22.8 %all-to-all-start.16 = ((bf16[4,128,384]{1,2,0:T(8,128)(2,1)}), bf16[4,128,384]{1,2,0:T(8,128)(2,1)}, u32[]{:S(2)}, u32[]{:S(2)}) async-start(bf16[4,128,384]{1,2,0:T(8,128)(2,1)} %bitcast.252), calls=%async_computation.17 | async-start | bytes 786432 | tf_op jit(solution)/shard_map/all_to_all | solution.py:80
  626.9 25.2 %all-to-all-start.11 = ((bf16[4,2,256,256]{3,2,1,0:T(8,128)(2,1)}), bf16[4,2,256,256]{3,2,1,0:T(8,128)(2,1)S(1)}, u32[]{:S(2)}, u32[]{:S(2)}) async-start(bf16[4,2,256,256]{3,2,1,0:T(8,128)(2,1)} %copy_bitcast_fusion.1), calls=%async_computation.12 | async-start | bytes 2097152 | tf_op jit(solution)/shard_map/all_to_all | solution.py:80
  652.1 14.5 %all-to-all-start.10 = ((bf16[2,256,3,128]{3,0,2,1:T(2,128)(2,1)}), bf16[2,256,3,128]{3,0,2,1:T(2,128)(2,1)S(1)}, u32[]{:S(2)}, u32[]{:S(2)}) async-start(bf16[2,256,3,128]{3,0,2,1:T(2,128)(2,1)} %copy.293), calls=%async_computation.11 | async-start | bytes 786432 | tf_op jit(solution)/shard_map/all_to_all | solution.py:574
  678.5 39.1 %all-to-all-start.17 = ((bf16[4,128,1536]{2,1,0:T(8,128)(2,1)}), bf16[4,128,1536]{2,1,0:T(8,128)(2,1)S(1)}, u32[]{:S(2)}, u32[]{:S(2)}) async-start(bf16[4,128,1536]{2,1,0:T(8,128)(2,1)} %broadcast_in_dim.397), calls=%async_computation.18 | async-start | bytes 3145728 | tf_op jit(solution)/shard_map/all_to_all | solution.py:80
  719.5 51.6 %all-to-all-start.13 = ((bf16[4,128,2048]{2,1,0:T(8,128)(2,1)}), bf16[4,128,2048]{2,1,0:T(8,128)(2,1)S(1)}, u32[]{:S(2)}, u32[]{:S(2)}) async-start(bf16[4,128,2048]{2,1,0:T(8,128)(2,1)} %broadcast_in_dim.395), calls=%async_computation.14 | async-start | bytes 4194304 | tf_op jit(solution)/shard_map/all_to_all | solution.py:80
  771.1 17.0 %all-to-all-start.15 = ((bf16[4,128,384]{2,1,0:T(8,128)(2,1)}), bf16[4,128,384]{2,1,0:T(8,128)(2,1)S(1)}, u32[]{:S(2)}, u32[]{:S(2)}) async-start(bf16[4,128,384]{2,1,0:T(8,128)(2,1)} %copy.305), calls=%async_computation.16 | async-start | bytes 786432 | tf_op jit(solution)/shard_map/all_to_all | solution.py:80
  788.1 10.1 all-to-all-start.20
  798.2 39.9 %all-to-all-start.14 = ((bf16[4,128,1536]{2,1,0:T(8,128)(2,1)}), bf16[4,128,1536]{2,1,0:T(8,128)(2,1)}, u32[]{:S(2)}, u32[]{:S(2)}) async-start(bf16[4,128,1536]{2,1,0:T(8,128)(2,1)} %bitcast.247), calls=%async_computation.15 | async-start | bytes 3145728 | tf_op jit(solution)/shard_map/all_to_all | solution.py:80
  804.0 70.5 %reduce-scatter.10.cloned.1.call-start = ((), (), s32[]{:S(2)}) async-start(), calls=%async_computation.27 | async-start | bytes 6782976 | tf_op jit(solution)/shard_map/reduce_scatter | solution.py:314
  838.1 108.9 %all-to-all-start.18 = ((bf16[144,128,128]{2,1,0:T(8,128)(2,1)}), bf16[144,128,128]{2,1,0:T(8,128)(2,1)}, u32[]{:S(2)}, u32[]{:S(2)}) async-start(bf16[144,128,128]{2,1,0:T(8,128)(2,1)} %gather_fusion.10), calls=%async_computation.19 | async-start | bytes 9437184 | tf_op jit(solution)/shard_map/all_to_all | solution.py:80
  947.0 38.1 %all-to-all-start.19 = ((bf16[44,128,128]{2,1,0:T(8,128)(2,1)}), bf16[44,128,128]{2,1,0:T(8,128)(2,1)}, u32[]{:S(2)}, u32[]{:S(2)}) async-start(bf16[44,128,128]{2,1,0:T(8,128)(2,1)} %gather_fusion.12), calls=%async_computation.21 | async-start | bytes 2883584 | tf_op jit(solution)/shard_map/all_to_all | solution.py:80
  (71 other events, 2419.9 us)
Sparse Core Ops, SparseCore 0:
  15.1 230.8 all-gather.10
Sparse Core Ops, SparseCore 1:
  272.5 154.9 all-gather.12
  576.5 189.8 reduce-scatter.11
  814.4 60.1 reduce-scatter.9

commit v6 on v5

--- a/solution.py
+++ b/solution.py
@@ -313,9 +313,9 @@
     def sum_columns(self, buffer):
         return lax.psum_scatter(buffer, COLUMN_AXES, scatter_dimension=0, tiled=True)
 
-    def send_home(self, summed):
+    def back_buffer(self, summed):
         back = locate(self.pair_slots, jnp.where(self.held, self.arrival, -1), self.my_rank)
-        return exchange(pick(summed, back), "blk")
+        return pick(summed, back)
 
 
 def soap_kernel(
@@ -333,20 +333,29 @@
             preferred_element_type=jnp.float32,
         )
 
-    for number in range(count):
-        grad = jnp.where(used_ref[base + number] > 0, grad_ref[number], jnp.bfloat16(0))
-        left = left_ref[number].astype(jnp.bfloat16)
-        right = right_ref[number].astype(jnp.bfloat16)
-        rotated = product(product(left, grad, ((0,), (0,))), right, ((1,), (0,)))
-        first_new = BETA_FIRST * first_ref[number] + (1.0 - BETA_FIRST) * rotated
-        second_new = BETA_SECOND * second_ref[number] + (1.0 - BETA_SECOND) * rotated * rotated
-        normalized = first_new / (jnp.sqrt(second_new) + ADAM_EPS)
-        update = product(product(left, normalized, ((1,), (0,))), right, ((1,), (1,)))
-        master = master_ref[number]
-        scale = jnp.sqrt(jnp.mean(master * master, keepdims=True) + SCALE_EPS)
-        first_out[number] = first_new
-        second_out[number] = second_new
-        master_out[number] = master - RELATIVE_RATE * scale * (update + WEIGHT_DECAY * master)
+    for start in range(0, count, 5):
+        group = range(start, min(start + 5, count))
+        lefts = [left_ref[number].astype(jnp.bfloat16) for number in group]
+        rights = [right_ref[number].astype(jnp.bfloat16) for number in group]
+        grads = [
+            jnp.where(used_ref[base + number] > 0, grad_ref[number], jnp.bfloat16(0))
+            for number in group
+        ]
+        halves = [product(left, grad, ((0,), (0,))) for left, grad in zip(lefts, grads)]
+        turned = [product(half, right, ((1,), (0,))) for half, right in zip(halves, rights)]
+        normals = []
+        for number, rotated in zip(group, turned):
+            first_new = BETA_FIRST * first_ref[number] + (1.0 - BETA_FIRST) * rotated
+            second_new = BETA_SECOND * second_ref[number] + (1.0 - BETA_SECOND) * rotated * rotated
+            first_out[number] = first_new
+            second_out[number] = second_new
+            normals.append(first_new / (jnp.sqrt(second_new) + ADAM_EPS))
+        halves = [product(left, normal, ((1,), (0,))) for left, normal in zip(lefts, normals)]
+        updates = [product(half, right, ((1,), (1,))) for half, right in zip(halves, rights)]
+        for number, update in zip(group, updates):
+            master = master_ref[number]
+            scale = jnp.sqrt(jnp.mean(master * master, keepdims=True) + SCALE_EPS)
+            master_out[number] = master - RELATIVE_RATE * scale * (update + WEIGHT_DECAY * master)
 
 
 def soap_step(used, grads, *state):
@@ -504,6 +513,10 @@
         jnp.bfloat16
     )
     query_heads = lax.all_to_all(query_rot, "uly", split_axis=2, concat_axis=1, tiled=True)
+    normed_columns = split_columns(normed, blk_count, shard_rows)
+    query_heads, seed_line, normed_columns = lax.optimization_barrier(
+        (query_heads, seed_line, normed_columns)
+    )
     key_value = jnp.concatenate([key_rot, value_rows], axis=-1)
     key_value = jnp.stack([key_value[:, :, head] for head in head_of], axis=0)
     key_value = exchange(key_value, "uly").transpose(1, 0, 2, 3)
@@ -539,6 +552,8 @@
     shard_grads, grad_line, mixed_line = mix_lines(
         first_group, normed_line, seed_line, shard_stack
     )
+    out_columns = split_columns(out_rows, blk_count, shard_rows)
+    grad_line, out_columns = lax.optimization_barrier((grad_line, out_columns))
     grad_normed_two = exchange_sum(grad_line.reshape(blk_count, token_count, D), "blk")
     home_buffer = route.home_buffer(shard_grads)
     grad_normed_two, home_buffer = lax.optimization_barrier((grad_normed_two, home_buffer))
@@ -554,6 +569,8 @@
         .reshape(seq_count, rows_local, QH, HD)
     )
     grad_heads = lax.all_to_all(grad_out_rows, "uly", split_axis=2, concat_axis=1, tiled=True)
+    middle_source, grad_heads = lax.optimization_barrier((grad_middle_low, grad_heads))
+    middle_lines = spread(middle_source, "blk").reshape(blk_count * token_count, D)
     grad_heads_wide = grad_heads.astype(jnp.float32)
     row_delta = jnp.sum(grad_heads_wide * attended, axis=-1)
 
@@ -574,6 +591,7 @@
     grad_query_rows = lax.all_to_all(grad_query_low, "uly", split_axis=1, concat_axis=2, tiled=True)
     grad_pair = jnp.concatenate([grad_keys / score_root, grad_values], axis=-1).astype(jnp.bfloat16)
     grad_pair = grad_pair.reshape(seq_count, blk_count, span_rows, 2 * HD).transpose(1, 0, 2, 3)
+    grad_pair, middle_lines = lax.optimization_barrier((grad_pair, middle_lines))
     grad_pair = exchange_sum(grad_pair, "blk").astype(jnp.bfloat16)
     grad_pair = grad_pair.reshape(seq_count, uly_count, rows_local, 2 * HD).transpose(1, 0, 2, 3)
     grad_pair = exchange(grad_pair, "uly").astype(jnp.float32)
@@ -618,28 +636,23 @@
     grad_lines = spread(
         jnp.concatenate([grad_query_lin, grad_key_lin, grad_value_lin], axis=1), "blk"
     ).reshape(blk_count * token_count, QW + 2 * KVW)
-    returned_grads = route.send_home(summed_tiles)
-    grad_lines, mixed_line = lax.optimization_barrier((grad_lines, mixed_line))
-    mixed_out = (
-        (middle + exchange_sum(mixed_line.reshape(blk_count, token_count, D), "blk"))
-        .astype(jnp.bfloat16)
-        .reshape(seq_count, rows_local, D)
-    )
-    middle_lines = spread(grad_middle_low, "blk").reshape(blk_count * token_count, D)
+    grad_lines, summed_tiles = lax.optimization_barrier((grad_lines, summed_tiles))
+    back_tiles = route.back_buffer(summed_tiles)
     attn_grads = jnp.concatenate(
         [
             matrix_to_tiles(
-                outer_product(split_columns(normed, blk_count, shard_rows), grad_lines)
+                outer_product(normed_columns, grad_lines)
             ),
             matrix_to_tiles(
-                outer_product(split_columns(out_rows, blk_count, shard_rows), middle_lines)
+                outer_product(out_columns, middle_lines)
             ),
         ],
         axis=0,
     )
     attn_buffer = attn_route.home_buffer(attn_grads)
-    attn_buffer, summed_tiles = lax.optimization_barrier((attn_buffer, summed_tiles))
-    attn_returned = attn_route.send_home(attn_route.sum_columns(attn_buffer))
+    attn_buffer, back_tiles = lax.optimization_barrier((attn_buffer, back_tiles))
+    returned_grads = exchange(back_tiles, "blk")
+    attn_returned = exchange(attn_route.back_buffer(attn_route.sum_columns(attn_buffer)), "blk")
     my_slots = my_first + jnp.arange(slot_local, dtype=jnp.int32)
     slot_index = locate(my_slots, route.owner, route.slot_position()) + locate(
         my_slots, attn_route.owner, blk_count * route.pair_cap + attn_route.slot_position()
@@ -659,6 +672,12 @@
         return lax.psum_scatter(parts, ALL_AXES, scatter_dimension=0, tiled=True)
 
     grad_slots = lax.cond(route.fits & attn_route.fits, routed_grads, summed_grads)
+    grad_slots, mixed_line = lax.optimization_barrier((grad_slots, mixed_line))
+    mixed_out = (
+        (middle + exchange_sum(mixed_line.reshape(blk_count, token_count, D), "blk"))
+        .astype(jnp.bfloat16)
+        .reshape(seq_count, rows_local, D)
+    )
     master_new, first_new, second_new = soap_step(
         slot_used.astype(jnp.int32),
         grad_slots,

time: 1060 us -> 1050 us (level)
  Pallas kernels: 81.3 us -> 66.3 us
    all_to_all x16 -> x17, waiting for transfers between devices: 378 us -> 348 us  [exchange(): return lax.all_to_all(values, axes, split_axis=0, concat_axis=0, tiled=True)]
    reduce_scatter x1, waiting for transfers between devices: 27.9 us -> 53.3 us  [sum_columns(): lax.psum_scatter(buffer, COLUMN_AXES, scatter_dimension=0, tiled=True)]
    pallas_call x1, Pallas kernels: 32.9 us -> 17.9 us  [soap_step(): pl.pallas_call(soap_kernel, out_shape=(whole, whole, whole), grid_spec=pl...]
    optimization_barrier x0 -> x1, waiting for transfers between devices: none -> 11 us  [local(): lax.optimization_barrier((grad_lines, summed_tiles))]
    all_to_all x16 -> x17, starting transfers between devices: 103 us -> 105 us  [exchange(): return lax.all_to_all(values, axes, split_axis=0, concat_axis=0, tiled=True)]
  transfers between devices with their start and end apart: 24 -> 24, of which waited for: 17 -> 21; matrix products, arithmetic and copies ran while one was open for 25% -> 25% of each run, Pallas kernels for 0% -> 6%
where the time goes in v6:
time: 1050 us; the launch traced here: 1040 us
  waiting for transfers between devices  489 us (47%)
  local copies, waits for them, and re-layouts  215 us (20%)
  starting transfers between devices  119 us (11%)
  Pallas kernels  66.3 us (6%)
  other arithmetic  63.8 us (6%)
  matrix products  46.6 us (4%)
  between operations  20.6 us (2%)
    all_to_all x17, waiting for transfers between devices, exchange(): return lax.all_to_all(values, axes, split_axis=0, concat_axis=0, tiled=True)  348 us
    gather x10, local copies, waits for them, and re-layouts, pick(): return jnp.take(table, index, axis=0, mode='clip')  114 us
    all_to_all x17, starting transfers between devices, exchange(): return lax.all_to_all(values, axes, split_axis=0, concat_axis=0, tiled=True)  105 us
    all_gather x1, waiting for transfers between devices, local(): lax.all_gather(pick(master_low, attn_send), ALL_AXES, axis=0, tiled=True)  60.7 us
    reduce_scatter x1, waiting for transfers between devices, sum_columns(): lax.psum_scatter(buffer, COLUMN_AXES, scatter_dimension=0, tiled=True)  53.3 us
    pallas_call x1, Pallas kernels, mix_chunk(): pl.pallas_call(mix_kernel, out_shape=(jax.ShapeDtypeStruct(stack.shape, j...  48.4 us
  transfers between devices with their start and end apart: 24, of which 21 were waited for; matrix products, arithmetic and copies ran while one was open for 25% of the time, Pallas kernels for 6%

profile of v6, /device:TPU:10, one launch (start us, length us, event | category | flops | bytes accessed | tf_op | source)
XLA Modules:
  0.0 1035.5 jit_solution(6088961370976713524)
XLA Ops:
  36.1 143.8 %all-to-all-done.8 = bf16[144,128,128]{2,1,0:T(8,128)(2,1)} async-done(((bf16[144,128,128]{2,1,0:T(8,128)(2,1)}), bf16[144,128,128]{2,1,0:T(8,128)(2,1)}, u32[]{:S(2)}, u32[]{:S(2)}) %all-to-all-start.8) | async-done | bytes 4718624 | tf_op jit(solution)/shard_map/all_to_all | solution.py:80
  185.2 60.7 %all-gather.11.cloned.1.call-done = bf16[736,128,128]{2,1,0:T(8,128)(2,1)} async-done(((bf16[23,128,128]{2,1,0:T(8,128)(2,1)}), bf16[736,128,128]{2,1,0:T(8,128)(2,1)}) %all-gather.11.cloned.1.call-update) | async-done | bytes 24117264 | tf_op jit(solution)/shard_map/all_gather | solution.py:467
  246.0 24.1 %conditional.3 = (bf16[336,128,128]{2,1,0:T(8,128)(2,1)}) conditional(s32[]{:T(128)} %convert_element_type.226, (bf16[90,128,128]{2,1,0:T(8,128)(2,1)S(1)}, s32[336]{0:T(512)S(1)}) %tuple.36, (s32[336]{0:T(512)S(1)}, s32[336]{0:T(512)S(1)}, bf16[736,128,128]{2,1,0:T(8,128)(2,1)}) %tuple.37), branch_computations={%region_4.5_spmd, %region_5.6_spmd} | conditional | flops 1696 | bytes 325786304 | solution.py:472
  251.4 18.7 %gather_fusion = bf16[336,128,128]{2,1,0:T(8,128)(2,1)} fusion(bf16[736,128,128]{2,1,0:T(8,128)(2,1)} %get-tuple-element.99, s32[1024]{0:T(1024)S(1)} %pad_clamp_fusion.1), kind=kCustom, calls=%fused_computation.1 | custom fusion | bytes 22021440 | tf_op jit(solution)/shard_map/cond/branch_1_fun/jit(_take)/gather | solution.py:54
  308.6 9.1 fusion.85
  329.1 9.2 all-to-all-done.2
  356.5 9.6 all-to-all-done.1
  376.8 18.5 %all-to-all-done.5 = bf16[4,2,4,64,256]{4,3,2,1,0:T(8,128)(2,1)S(1)} async-done(((bf16[4,2,4,64,256]{4,3,2,1,0:T(8,128)(2,1)}), bf16[4,2,4,64,256]{4,3,2,1,0:T(8,128)(2,1)S(1)}, u32[]{:S(2)}, u32[]{:S(2)}) %all-to-all-start.5) | async-done | bytes 1048608 | tf_op jit(solution)/shard_map/all_to_all | solution.py:80
  455.8 24.1 %all-to-all-done.7 = bf16[4,128,1536]{1,2,0:T(8,128)(2,1)} async-done(((bf16[4,128,1536]{1,2,0:T(8,128)(2,1)}), bf16[4,128,1536]{1,2,0:T(8,128)(2,1)}, u32[]{:S(2)}, u32[]{:S(2)}) %all-to-all-start.7) | async-done | bytes 1572896 | tf_op jit(solution)/shard_map/all_to_all | solution.py:80
  493.2 28.7 %conditional.4 = (bf16[648,128,128]{2,1,0:T(8,128)(2,1)}) conditional(s32[]{:T(128)} %convert_element_type.250, (bf16[90,128,128]{2,1,0:T(8,128)(2,1)}, s32[648]{0:T(1024)}) %tuple.123, (s32[648]{0:T(1024)S(1)}, bf16[904,128,128]{2,1,0:T(8,128)(2,1)}) %tuple.125), branch_computations={%region_19.20_spmd, %region_20.21_spmd} | conditional | flops 1024 | bytes 334439552 | solution.py:479
  494.2 27.7 %gather_fusion.1 = bf16[648,128,128]{2,1,0:T(8,128)(2,1)} fusion(bf16[904,128,128]{2,1,0:T(8,128)(2,1)} %get-tuple-element.104, s32[1024]{0:T(1024)} %pad_clamp_fusion.3), kind=kCustom, calls=%fused_computation.3 | custom fusion | bytes 42469920 | tf_op jit(solution)/shard_map/cond/branch_1_fun/jit(_take)/gather | solution.py:54
  521.9 48.4 %shard_map.179 = (bf16[648,128,128]{2,1,0:T(8,128)(2,1)}, bf16[512,1536]{1,0:T(8,128)(2,1)}, bf16[512,1536]{1,0:T(8,128)(2,1)}) custom-call(s32[1]{0:T(128)} %bitcast.30.first_ref, bf16[512,1536]{1,0:T(8,128)(2,1)} %copy.281.x_ref, bf16[1536,512]{1,0:T(8,128)(2,1)} %get-tuple-element.216.xt_ref, bf16[512,1536]{1,0:T(8,128)(2,1)} %bitcast.218, ...), custom_call_target="tpu_custom_call" | custom-call | tf_op jit(solution)/shard_map/pallas_call | solution.py:196
  575.8 26.7 %gather_fusion.9 = bf16[904,128,128]{2,1,0:T(8,128)(2,1)} fusion(bf16[648,128,128]{2,1,0:T(8,128)(2,1)} %get-tuple-element.153, s32[1024]{0:T(1024)S(1)} %pad_clamp_fusion.9), kind=kCustom, calls=%fused_computation.9 | custom fusion | bytes 59248160 | tf_op jit(solution)/shard_map/jit(_take)/gather | solution.py:54
  626.9 9.3 all_to_all.150
  661.0 17.0 %all-to-all-done.13 = bf16[4,128,1536]{2,1,0:T(8,128)(2,1)} async-done(((bf16[4,128,1536]{2,1,0:T(8,128)(2,1)}), bf16[4,128,1536]{2,1,0:T(8,128)(2,1)}, u32[]{:S(2)}, u32[]{:S(2)}) %all-to-all-start.13) | async-done | bytes 1572896 | tf_op jit(solution)/shard_map/all_to_all | solution.py:80
  701.2 20.8 %all-to-all-done.14 = bf16[4,2,256,256]{3,2,1,0:T(8,128)(2,1)S(1)} async-done(((bf16[4,2,256,256]{3,2,1,0:T(8,128)(2,1)}), bf16[4,2,256,256]{3,2,1,0:T(8,128)(2,1)S(1)}, u32[]{:S(2)}, u32[]{:S(2)}) %all-to-all-start.14) | async-done | bytes 1048608 | tf_op jit(solution)/shard_map/all_to_all | solution.py:80
  761.8 28.8 %all-to-all-done.16 = bf16[4,128,2048]{2,1,0:T(8,128)(2,1)S(1)} async-done(((bf16[4,128,2048]{2,1,0:T(8,128)(2,1)}), bf16[4,128,2048]{2,1,0:T(8,128)(2,1)S(1)}, u32[]{:S(2)}, u32[]{:S(2)}) %all-to-all-start.16) | async-done | bytes 2097184 | tf_op jit(solution)/shard_map/all_to_all | solution.py:80
  790.6 11.0 %reduce-scatter.12.cloned.1.call-done = bf16[113,128,128]{2,1,0:T(8,128)(2,1)} async-done(((bf16[904,128,128]{2,1,0:T(8,128)(2,1)}), bf16[113,128,128]{2,1,0:T(8,128)(2,1)}) %reduce-scatter.12.cloned.1.call-update) | async-done | bytes 3702800 | tf_op jit(solution)/shard_map/optimization_barrier | solution.py:639
  804.1 9.8 gather_fusion.11
  829.0 53.3 %reduce-scatter.10.cloned.1.call-done = bf16[23,128,128]{2,1,0:T(8,128)(2,1)} async-done(((bf16[184,128,128]{2,1,0:T(8,128)(2,1)}), bf16[23,128,128]{2,1,0:T(8,128)(2,1)}) %reduce-scatter.10.cloned.1.call-update) | async-done | bytes 753680 | tf_op jit(solution)/shard_map/reduce_scatter | solution.py:314
  885.4 43.3 %all-to-all-done.17 = bf16[144,128,128]{2,1,0:T(8,128)(2,1)} async-done(((bf16[144,128,128]{2,1,0:T(8,128)(2,1)}), bf16[144,128,128]{2,1,0:T(8,128)(2,1)}, u32[]{:S(2)}, u32[]{:S(2)}) %all-to-all-start.17) | async-done | bytes 4718624 | tf_op jit(solution)/shard_map/all_to_all | solution.py:80
  953.0 14.0 %all-to-all-done.18 = bf16[44,128,128]{2,1,0:T(8,128)(2,1)} async-done(((bf16[44,128,128]{2,1,0:T(8,128)(2,1)}), bf16[44,128,128]{2,1,0:T(8,128)(2,1)}, u32[]{:S(2)}, u32[]{:S(2)}) %all-to-all-start.18) | async-done | bytes 1441824 | tf_op jit(solution)/shard_map/all_to_all | solution.py:80
  974.8 12.2 %conditional.5 = (bf16[90,128,128]{2,1,0:T(8,128)(2,1)}) conditional(s32[]{:T(128)} %convert_element_type.247, (s32[336]{0:T(512)}, s32[]{:T(128)}, s32[648]{0:T(1024)S(1)}, bf16[648,128,128]{2,1,0:T(8,128)(2,1)}, bf16[84,128,128]{2,1,0:T(8,128)(2,1)S(1)}) %tuple.127, (bf16[144,128,128]{2,1,0:T(8,128)(2,1)}, bf16[44,128,128]{2,1,0:T(8,128)(2,1)}, ...), branch_computations={%region_31.35_spmd, %region_35.38_spmd} | conditional | flops 69717856 | bytes 717487616 | solution.py:674
  1002.0 17.9 %shard_map.180 = (f32[90,128,128]{2,1,0:T(8,128)}, f32[90,128,128]{2,1,0:T(8,128)}, f32[90,128,128]{2,1,0:T(8,128)}) custom-call(s32[90]{0:T(128)S(1)} %convert_element_type.270.used_ref, bf16[90,128,128]{2,1,0:T(8,128)(2,1)} %get-tuple-element.269.grad_ref, f32[90,128,128]{2,1,0:T(8,128)S(1)} %copy-done, f32[90,128,128]{2,1,0:T(8,128)S(1)} %copy-done.1, ...), custom_call_target="tpu_custom_call" | custom-call | tf_op jit(solution)/shard_map/pallas_call | solution.py:366
  (390 shorter events, 387.2 us)
Async XLA Ops:
  8.0 238.0 %all-gather.11.cloned.1.call-start = ((), (), s32[]{:S(2)}) async-start(), calls=%async_computation.28 | async-start | bytes 24870912 | tf_op jit(solution)/shard_map/all_gather | solution.py:467
  26.2 153.8 %all-to-all-start.8 = ((bf16[144,128,128]{2,1,0:T(8,128)(2,1)}), bf16[144,128,128]{2,1,0:T(8,128)(2,1)}, u32[]{:S(2)}, u32[]{:S(2)}) async-start(bf16[144,128,128]{2,1,0:T(8,128)(2,1)} %gather_fusion.7), calls=%async_computation.9 | async-start | bytes 9437184 | tf_op jit(solution)/shard_map/all_to_all | solution.py:80
  270.1 223.2 %all-gather.13.cloned.1.call-start = ((), (), s32[]{:S(2)}) async-start(), calls=%async_computation.29 | async-start | bytes 33325056 | tf_op jit(solution)/shard_map/all_gather | solution.py:476
  271.3 9.9 all-to-all-start
  283.0 14.5 %all-to-all-start.3 = ((bf16[4,128,384]{2,1,0:T(8,128)(2,1)}), bf16[4,128,384]{2,1,0:T(8,128)(2,1)S(1)}, u32[]{:S(2)}, u32[]{:S(2)}) async-start(bf16[4,128,384]{2,1,0:T(8,128)(2,1)} %copy.263), calls=%async_computation.4 | async-start | bytes 786432 | tf_op jit(solution)/shard_map/all_to_all | solution.py:80
  298.8 39.5 %all-to-all-start.2 = ((bf16[4,128,1536]{2,1,0:T(8,128)(2,1)}), bf16[4,128,1536]{2,1,0:T(8,128)(2,1)S(1)}, u32[]{:S(2)}, u32[]{:S(2)}) async-start(bf16[4,128,1536]{2,1,0:T(8,128)(2,1)} %broadcast_in_dim.378), calls=%async_computation.3 | async-start | bytes 3145728 | tf_op jit(solution)/shard_map/all_to_all | solution.py:80
  338.3 13.3 %all-to-all-start.4 = ((bf16[4,2,64,256]{3,2,1,0:T(8,128)(2,1)}), bf16[4,2,64,256]{3,2,1,0:T(8,128)(2,1)}, u32[]{:S(2)}, u32[]{:S(2)}) async-start(bf16[4,2,64,256]{3,2,1,0:T(8,128)(2,1)} %pad_maximum_fusion.6), calls=%async_computation.5 | async-start | bytes 524288 | tf_op jit(solution)/shard_map/all_to_all | solution.py:80
  351.5 14.5 %all-to-all-start.1 = ((bf16[2,64,12,128]{3,1,0,2:T(8,128)(2,1)}), bf16[2,64,12,128]{3,1,0,2:T(8,128)(2,1)S(1)}, u32[]{:S(2)}, u32[]{:S(2)}) async-start(bf16[2,64,12,128]{3,1,0,2:T(8,128)(2,1)} %copy.260), calls=%async_computation.2 | async-start | bytes 786432 | tf_op jit(solution)/shard_map/all_to_all | solution.py:515
  367.2 28.1 %all-to-all-start.5 = ((bf16[4,2,4,64,256]{4,3,2,1,0:T(8,128)(2,1)}), bf16[4,2,4,64,256]{4,3,2,1,0:T(8,128)(2,1)S(1)}, u32[]{:S(2)}, u32[]{:S(2)}) async-start(bf16[4,2,4,64,256]{4,3,2,1,0:T(8,128)(2,1)} %broadcast_in_dim.379), calls=%async_computation.6 | async-start | bytes 2097152 | tf_op jit(solution)/shard_map/all_to_all | solution.py:80
  409.9 14.8 %all-to-all-start.6 = ((bf16[2,256,3,128]{3,0,2,1:T(2,128)(2,1)}), bf16[2,256,3,128]{3,0,2,1:T(2,128)(2,1)}, u32[]{:S(2)}, u32[]{:S(2)}) async-start(bf16[2,256,3,128]{3,0,2,1:T(2,128)(2,1)} %copy.272), calls=%async_computation.7 | async-start | bytes 786432 | tf_op jit(solution)/shard_map/all_to_all | solution.py:544
  439.9 40.0 %all-to-all-start.7 = ((bf16[4,128,1536]{1,2,0:T(8,128)(2,1)}), bf16[4,128,1536]{1,2,0:T(8,128)(2,1)}, u32[]{:S(2)}, u32[]{:S(2)}) async-start(bf16[4,128,1536]{1,2,0:T(8,128)(2,1)} %broadcast_in_dim.385), calls=%async_computation.8 | async-start | bytes 3145728 | tf_op jit(solution)/shard_map/all_to_all | solution.py:80
  479.8 90.5 %all-to-all-start.9 = ((bf16[4,128,384]{2,1,0:T(8,128)(2,1)}), bf16[4,128,384]{2,1,0:T(8,128)(2,1)}, u32[]{:S(2)}, u32[]{:S(2)}) async-start(bf16[4,128,384]{2,1,0:T(8,128)(2,1)} %bitcast.250), calls=%async_computation.10 | async-start | bytes 786432 | tf_op jit(solution)/shard_map/all_to_all | solution.py:80
  570.3 37.8 %all-to-all-start.10 = ((bf16[4,128,1536]{2,1,0:T(8,128)(2,1)}), bf16[4,128,1536]{2,1,0:T(8,128)(2,1)}, u32[]{:S(2)}, u32[]{:S(2)}) async-start(bf16[4,128,1536]{2,1,0:T(8,128)(2,1)} %bitcast.247), calls=%async_computation.11 | async-start | bytes 3145728 | tf_op jit(solution)/shard_map/all_to_all | solution.py:80
  575.4 226.2 %reduce-scatter.12.cloned.1.call-start = ((), (), s32[]{:S(2)}) async-start(), calls=%async_computation.30 | async-start | bytes 33325056
  639.4 38.6 %all-to-all-start.13 = ((bf16[4,128,1536]{2,1,0:T(8,128)(2,1)}), bf16[4,128,1536]{2,1,0:T(8,128)(2,1)}, u32[]{:S(2)}, u32[]{:S(2)}) async-start(bf16[4,128,1536]{2,1,0:T(8,128)(2,1)} %broadcast_in_dim.396), calls=%async_computation.14 | async-start | bytes 3145728 | tf_op jit(solution)/shard_map/all_to_all | solution.py:80
  678.0 15.0 %all-to-all-start.12 = ((bf16[2,256,3,128]{3,0,2,1:T(2,128)(2,1)}), bf16[2,256,3,128]{3,0,2,1:T(2,128)(2,1)S(1)}, u32[]{:S(2)}, u32[]{:S(2)}) async-start(bf16[2,256,3,128]{3,0,2,1:T(2,128)(2,1)} %copy.287), calls=%async_computation.13 | async-start | bytes 786432 | tf_op jit(solution)/shard_map/all_to_all | solution.py:591
  693.1 28.9 %all-to-all-start.14 = ((bf16[4,2,256,256]{3,2,1,0:T(8,128)(2,1)}), bf16[4,2,256,256]{3,2,1,0:T(8,128)(2,1)S(1)}, u32[]{:S(2)}, u32[]{:S(2)}) async-start(bf16[4,2,256,256]{3,2,1,0:T(8,128)(2,1)} %copy_bitcast_fusion.1), calls=%async_computation.15 | async-start | bytes 2097152 | tf_op jit(solution)/shard_map/all_to_all | solution.py:80
  723.0 11.8 %all-to-all-start.15 = ((bf16[4,2,64,256]{3,2,1,0:T(8,128)(2,1)}), bf16[4,2,64,256]{3,2,1,0:T(8,128)(2,1)S(1)}, u32[]{:S(2)}, u32[]{:S(2)}) async-start(bf16[4,2,64,256]{3,2,1,0:T(8,128)(2,1)} %bitcast.210), calls=%async_computation.16 | async-start | bytes 524288 | tf_op jit(solution)/shard_map/all_to_all | solution.py:80
  739.5 51.1 %all-to-all-start.16 = ((bf16[4,128,2048]{2,1,0:T(8,128)(2,1)}), bf16[4,128,2048]{2,1,0:T(8,128)(2,1)S(1)}, u32[]{:S(2)}, u32[]{:S(2)}) async-start(bf16[4,128,2048]{2,1,0:T(8,128)(2,1)} %broadcast_in_dim.397), calls=%async_computation.17 | async-start | bytes 4194304 | tf_op jit(solution)/shard_map/all_to_all | solution.py:80
  746.8 135.4 %reduce-scatter.10.cloned.1.call-start = ((), (), s32[]{:S(2)}) async-start(), calls=%async_computation.27 | async-start | bytes 6782976 | tf_op jit(solution)/shard_map/reduce_scatter | solution.py:314
  822.0 106.7 %all-to-all-start.17 = ((bf16[144,128,128]{2,1,0:T(8,128)(2,1)}), bf16[144,128,128]{2,1,0:T(8,128)(2,1)}, u32[]{:S(2)}, u32[]{:S(2)}) async-start(bf16[144,128,128]{2,1,0:T(8,128)(2,1)} %gather_fusion.11), calls=%async_computation.18 | async-start | bytes 9437184 | tf_op jit(solution)/shard_map/all_to_all | solution.py:80
  928.7 38.4 %all-to-all-start.18 = ((bf16[44,128,128]{2,1,0:T(8,128)(2,1)}), bf16[44,128,128]{2,1,0:T(8,128)(2,1)}, u32[]{:S(2)}, u32[]{:S(2)}) async-start(bf16[44,128,128]{2,1,0:T(8,128)(2,1)} %gather_fusion.12), calls=%async_computation.20 | async-start | bytes 2883584 | tf_op jit(solution)/shard_map/all_to_all | solution.py:80
  967.1 19.9 %all-to-all-start.20 = ((f32[32,1,160]{2,1,0:T(1,128)}), f32[32,1,160]{2,1,0:T(1,128)}, u32[]{:S(2)}, u32[]{:S(2)}) async-start(f32[32,1,160]{2,1,0:T(1,128)} %all_to_all.127), calls=%async_computation.22 | async-start | bytes 65536 | tf_op jit(solution)/shard_map/all_to_all | solution.py:80
  987.0 39.3 %all-to-all-start.19 = ((bf16[4,128,1536]{2,1,0:T(8,128)(2,1)}), bf16[4,128,1536]{2,1,0:T(8,128)(2,1)S(1)}, u32[]{:S(2)}, u32[]{:S(2)}) async-start(bf16[4,128,1536]{2,1,0:T(8,128)(2,1)} %bitcast.246), calls=%async_computation.21 | async-start | bytes 3145728 | tf_op jit(solution)/shard_map/all_to_all | solution.py:80
  (68 other events, 1350.7 us)
Sparse Core Ops, SparseCore 0:
  15.1 230.8 all-gather.10
Sparse Core Ops, SparseCore 1:
  273.0 154.8 all-gather.12
  610.8 190.8 reduce-scatter.11
  822.1 60.1 reduce-scatter.9
